TPU v7x, 32 devices: a whole 2x2x4 slice. The times are simulated.
32 devices in a mesh: group: 2 (over y), expert: 4 (over x, core), blk: 4 (over z).
Axes of the slice: x: 2, y: 2, z: 4, core: 2. Of those that a mesh axis runs over, the one named last changes fastest.
Arguments:
- tokens: bfloat16 [128, 2048], P(('group', 'expert', 'blk')), parts along dimension 0, may hold values from -6 to 6
- route_ids: int32 [128, 2], P(('group', 'expert', 'blk')), parts along dimension 0, may hold values from 0 to 3, as said below
- route_slots: int32 [128, 2], P(('group', 'expert', 'blk')), parts along dimension 0, may hold values from 0 to 3, as said below
- gate_fixed: int32 [128, 2], P(('group', 'expert', 'blk')), parts along dimension 0, may hold values from 1 to 255
- w_gate: bfloat16 [4, 2048, 8192], P('expert', None, 'blk'), may hold values from -0.125 to 0.125
- w_up: bfloat16 [4, 2048, 8192], P('expert', None, 'blk'), may hold values from -0.125 to 0.125
- w_down: bfloat16 [4, 8192, 2048], P('expert', 'blk'), may hold values from -0.125 to 0.125
Outputs:
- mixed_out: bfloat16 [128, 2048], P(('group', 'expert', 'blk')), parts along dimension 0
There are 2 independent parts, one for each index of `group`. A program takes and returns all parts, laid end to end along the dimension named above; an argument that names none is the same for every part. Nothing has to cross between parts.
Inputs may be any that keep to these rules, and one draw needn't show every extreme that they name: `route_ids`: each row names two different experts. Among the rows of one device no expert is named more than 4 times, and one expert, the same for every device of a part, is named exactly 4 times by the rows of every device. `route_slots`: among the rows of one device, the choices that name the same expert have distinct slots.
All inputs are finite; a program needn't handle non-finite values.
Results may differ from a plain program's by a relative error of at most 0.0049.
Values may be sent and summed in bfloat16 or wider, within the bound.
No kernel may reach another device: no remote copies, remote signals or barrier semaphores. Data moves between devices by JAX's collectives and lax.ppermute only.
A program may use at most 64 MiB of HBM per device.

v0:
```python
import jax
import jax.numpy as jnp
from jax import lax
from jax.sharding import PartitionSpec as P


def normalized(fixed_weights):
    values = fixed_weights.astype(jnp.float32)
    return values / jnp.sum(values, axis=1, keepdims=True)


def on_device(tokens, route_ids, route_slots, gate_fixed, w_gate, w_up, w_down):
    count_tok, width = tokens.shape
    experts = lax.axis_size("expert")
    capacity = 4 * count_tok // experts
    slots_all = experts * capacity
    destination_expert = route_ids * capacity + route_slots
    slot_lanes = jnp.arange(slots_all, dtype=jnp.int32)
    one_hot = (destination_expert[None, :, 0] == slot_lanes[:, None]) | (
        destination_expert[None, :, 1] == slot_lanes[:, None]
    )
    outgoing = jnp.dot(one_hot.astype(jnp.bfloat16), tokens, preferred_element_type=jnp.float32)
    outgoing = outgoing.astype(jnp.bfloat16).reshape(experts, capacity, width)
    arrived = lax.all_to_all(outgoing, "expert", split_axis=0, concat_axis=0, tiled=True).reshape(
        slots_all, width
    )
    gate_mat = w_gate[0]
    up_mat = w_up[0]
    down_mat = w_down[0]
    gathered = lax.all_gather(arrived, "blk", axis=0, tiled=True)
    gate_part = jnp.dot(gathered, gate_mat, preferred_element_type=jnp.float32)
    up_part = jnp.dot(gathered, up_mat, preferred_element_type=jnp.float32)
    hidden = (jax.nn.silu(gate_part) * up_part).astype(jnp.bfloat16)
    summed = lax.psum_scatter(
        jnp.dot(hidden, down_mat, preferred_element_type=jnp.float32),
        "blk",
        scatter_dimension=0,
        tiled=True,
    )
    returned = lax.all_to_all(
        summed.reshape(experts, capacity, width), "expert", split_axis=0, concat_axis=0, tiled=True
    )
    returned = returned.reshape(slots_all, width)
    shares = normalized(gate_fixed)
    first_pick = jnp.take(returned, destination_expert[:, 0], axis=0)
    second = jnp.take(returned, destination_expert[:, 1], axis=0)
    mixed_out = shares[:, 0:1] * first_pick + shares[:, 1:2] * second
    return mixed_out.astype(jnp.bfloat16)


def solution(mesh):
    return jax.shard_map(
        on_device,
        mesh=mesh,
        in_specs=(
            P(("group", "expert", "blk"), None),
            P(("group", "expert", "blk"), None),
            P(("group", "expert", "blk"), None),
            P(("group", "expert", "blk"), None),
            P("expert", None, "blk"),
            P("expert", None, "blk"),
            P("expert", "blk", None),
        ),
        out_specs=P(("group", "expert", "blk"), None),
        check_vma=False,
    )
```

profile of v0, /device:TPU:0, one launch (start us, length us, event | category | flops | bytes accessed | tf_op | source)
XLA Modules:
  0.0 85.2 jit_solution(3406159153187408253)
XLA Ops:
  6.5 0.0 copy-start
  6.5 0.0 reduce-scatter.2.cloned.1.call-start
  6.5 0.7 multiply_add_fusion
  7.3 0.0 copy-done
  7.3 0.1 convolution_convert_fusion
  7.4 8.2 %all_to_all.10 = bf16[4,4,2048]{2,1,0:T(4,128)(2,1)S(1)} all-to-all(bf16[4,4,2048]{2,1,0:T(4,128)(2,1)S(1)} %reshape.20), channel_id=1, replica_groups=mesh['group'=2,'expert'=4,'blk'=4] {'expert'}, dimensions={0} | all-to-all | bytes 131072 | tf_op jit(solution)/shard_map/all_to_all | solution.py:24
  15.6 14.1 %all_gather.3 = bf16[64,2048]{1,0:T(8,128)(2,1)S(1)} all-gather(bf16[16,2048]{1,0:T(8,128)(2,1)S(1)} %reshape.21), channel_id=1, replica_groups=mesh['group'=2,'expert'=4,'blk'=4] {'blk'}, dimensions={0}, use_global_device_ids=true | all-gather | bytes 327680 | tf_op jit(solution)/shard_map/all_gather | solution.py:30
  29.7 4.9 %fusion.4 = f32[64,2048]{1,0:T(8,128)S(1)} fusion(bf16[64,2048]{1,0:T(8,128)(2,1)S(1)} %all_gather.3, bf16[1,2048,2048]{2,1,0:T(8,128)(2,1)} %param.13), kind=kOutput, calls=%fused_computation.6 | convolution fusion | flops 536870912 | bytes 9175040 | tf_op jit(solution)/shard_map/dot_general | solution.py:31
  34.7 0.0 copy-start.1
  34.7 9.6 %fusion = f32[64,2048]{1,0:T(8,128)} fusion(bf16[1,2048,2048]{2,1,0:T(8,128)(2,1)} %param.15, bf16[64,2048]{1,0:T(8,128)(2,1)S(1)} %all_gather.3, bf16[1,2048,2048]{2,1,0:T(8,128)(2,1)} %param.14, f32[64,2048]{1,0:T(8,128)S(1)} %fusion.4), kind=kOutput, calls=%fused_computation.2 | convolution fusion | flops 1074528256 | bytes 18087936 | tf_op jit(solution)/shard_map/dot_general | solution.py:35
  44.3 0.0 reduce-scatter.2.cloned.1.call-update
  44.3 0.0 copy-done.1
  44.4 22.6 %reduce-scatter.2.cloned.1.call-done = f32[16,2048]{1,0:T(8,128)} async-done(((f32[64,2048]{1,0:T(8,128)}), f32[16,2048]{1,0:T(8,128)}) %reduce-scatter.2.cloned.1.call-update) | async-done | bytes 131088 | tf_op jit(solution)/shard_map/reduce_scatter | solution.py:34
  67.0 1.6 %reshape.22 = f32[4,4,2048]{2,1,0:T(4,128)} reshape(f32[16,2048]{1,0:T(8,128)} %reduce-scatter.2.cloned.1.call-done) | data formatting | bytes 262144 | tf_op jit(solution)/shard_map/reshape | solution.py:41
  68.6 3.3 %all-to-all-start.1 = ((f32[4,4,2048]{2,1,0:T(4,128)}), f32[4,4,2048]{2,1,0:T(4,128)S(1)}, u32[]{:S(2)}, u32[]{:S(2)}) async-start(f32[4,4,2048]{2,1,0:T(4,128)} %reshape.22), calls=%async_computation.2 | async-start | bytes 262144 | tf_op jit(solution)/shard_map/all_to_all | solution.py:40
  71.9 4.6 %all-to-all-done.1 = f32[4,4,2048]{2,1,0:T(4,128)S(1)} async-done(((f32[4,4,2048]{2,1,0:T(4,128)}), f32[4,4,2048]{2,1,0:T(4,128)S(1)}, u32[]{:S(2)}, u32[]{:S(2)}) %all-to-all-start.1) | async-done | bytes 131104 | tf_op jit(solution)/shard_map/all_to_all | solution.py:40
  76.5 0.6 gather_fusion
  77.1 0.6 gather_fusion.1
  77.7 0.7 fusion.21
  (9 shorter events, 0.2 us)
Async XLA Ops:
  6.5 0.7 copy-start
  6.5 60.5 %reduce-scatter.2.cloned.1.call-start = ((), (), s32[]{:S(2)}) async-start(), calls=%async_computation.3 | async-start | bytes 655360 | tf_op jit(solution)/shard_map/reduce_scatter | solution.py:34
  34.7 9.6 %copy-start.1 = (s32[4,2]{0,1:T(2,128)S(1)}, s32[4,2]{0,1:T(2,128)}, u32[]{:S(2)}) copy-start(s32[4,2]{0,1:T(2,128)} %param.12) | copy-start | bytes 100
  68.6 7.9 %all-to-all-start.1 = ((f32[4,4,2048]{2,1,0:T(4,128)}), f32[4,4,2048]{2,1,0:T(4,128)S(1)}, u32[]{:S(2)}, u32[]{:S(2)}) async-start(f32[4,4,2048]{2,1,0:T(4,128)} %reshape.22), calls=%async_computation.2 | async-start | bytes 262144 | tf_op jit(solution)/shard_map/all_to_all | solution.py:40
Sparse Core Ops, SparseCore 0:
  44.4 22.5 reduce-scatter.1
where the time goes:
time: 85.6 us; the launch traced here: 85.2 us
  waiting for transfers between devices  27.2 us (32%)
  blocking collectives  22.3 us (26%)
  matrix products  14.7 us (17%)
  between operations  13.5 us (16%)
  starting transfers between devices  3.32 us (4%)
  local copies, waits for them, and re-layouts  2.86 us (3%)
  other arithmetic  1.45 us (2%)
    reduce_scatter x1, waiting for transfers between devices, on_device(): lax.psum_scatter(jnp.dot(hidden, down_mat, preferred_element_type=jnp.flo...  22.6 us
    all_gather x1, blocking collectives, on_device(): gathered = lax.all_gather(arrived, 'blk', axis=0, tiled=True)  14.1 us
    dot_general x1, matrix products, on_device(): jnp.dot(hidden, down_mat, preferred_element_type=jnp.float32)  9.6 us
    all_to_all x1, blocking collectives, on_device(): lax.all_to_all(outgoing, 'expert', split_axis=0, concat_axis=0, tiled=True)  8.16 us
    dot_general x1, matrix products, on_device(): gate_part = jnp.dot(gathered, gate_mat, preferred_element_type=jnp.float32)  4.95 us
    all_to_all x1, waiting for transfers between devices, on_device(): lax.all_to_all(summed.reshape(experts, capacity, width), 'expert', split_...  4.55 us
    all_to_all x1, starting transfers between devices, on_device(): lax.all_to_all(summed.reshape(experts, capacity, width), 'expert', split_...  3.32 us
  transfers between devices with their start and end apart: 2, of which 2 were waited for; matrix products, arithmetic and copies ran while one was open for 0% of the time, Pallas kernels for 0%

commit v1 on v0

v1 whole, which is shorter than its diff:
```python
import functools

import jax
import jax.numpy as jnp
from jax import lax
from jax.experimental import pallas as pl
from jax.experimental.pallas import tpu as pltpu
from jax.sharding import PartitionSpec as P

VMEM = pl.BlockSpec(memory_space=pltpu.VMEM)
ANY = pl.BlockSpec(memory_space=pl.ANY)


def peer(i, d, n):
    return i ^ d if n & (n - 1) == 0 else (i + d) % n


def source(i, d, n):
    return i ^ d if n & (n - 1) == 0 else (i - d) % n


def fetch(x, axis, d):
    n = lax.axis_size(axis)
    return lax.ppermute(x, axis, [(peer(i, d, n), i) for i in range(n)])


def deliver(x, axis, d):
    n = lax.axis_size(axis)
    return lax.ppermute(x, axis, [(i, peer(i, d, n)) for i in range(n)])


def stack_kernel(*refs):
    out = refs[-1]
    rows = [r[...].astype(jnp.float32) for r in refs[:-1]]
    out[...] = jnp.concatenate(rows, axis=0).astype(out.dtype)


def stack(blocks):
    rows = sum(b.shape[0] for b in blocks)
    return pl.pallas_call(
        stack_kernel,
        name="stack",
        out_shape=jax.ShapeDtypeStruct((rows, blocks[0].shape[1]), blocks[0].dtype),
        in_specs=[VMEM] * len(blocks),
        out_specs=VMEM,
    )(*blocks)


def ffn_kernel(n_e, n_b, count, chunks, *refs):
    xs = refs[:n_e]
    gate_hbm, up_hbm, down_hbm = refs[n_e : n_e + 3]
    outs = refs[n_e + 3 : n_e + 3 + n_b]
    gate_w, up_w, down_w, gate_acc, up_acc, sems = refs[n_e + 3 + n_b :]
    depth, inner = gate_w.shape[0] // chunks, down_w.shape[0] // chunks
    copies = {}
    for c in range(chunks):
        for which, (src, dst) in enumerate(((gate_hbm, gate_w), (up_hbm, up_w))):
            rows = pl.ds(c * depth, depth)
            copies[which, c] = pltpu.make_async_copy(src.at[0, rows, :], dst.at[rows, :], sems.at[which, c])
            copies[which, c].start()
    for c in range(chunks):
        rows = pl.ds(c * inner, inner)
        copies[2, c] = pltpu.make_async_copy(down_hbm.at[0, rows, :], down_w.at[rows, :], sems.at[2, c])
        copies[2, c].start()
    x = jnp.concatenate([r[...] for r in xs], axis=0)
    for c in range(chunks):
        cut = slice(c * depth, (c + 1) * depth)
        for which, (w, acc) in enumerate(((gate_w, gate_acc), (up_w, up_acc))):
            copies[which, c].wait()
            part = jnp.dot(x[:, cut], w[cut, :], preferred_element_type=jnp.float32)
            acc[...] = part if c == 0 else acc[...] + part
    v = gate_acc[...]
    hidden = (v / (1.0 + jnp.exp(-v)) * up_acc[...]).astype(jnp.bfloat16)
    total = None
    for c in range(chunks):
        cut = slice(c * inner, (c + 1) * inner)
        copies[2, c].wait()
        part = jnp.dot(hidden[:, cut], down_w[cut, :], preferred_element_type=jnp.float32)
        total = part if c == 0 else total + part
    for d, out in enumerate(outs):
        rows = [total[(m * n_b + d) * count : (m * n_b + d + 1) * count] for m in range(n_e)]
        out[...] = jnp.concatenate(rows, axis=0).astype(out.dtype)


def ffn(xs, w_gate, w_up, w_down, n_b, count):
    n_e, (rows, width) = len(xs), xs[0].shape
    hidden = w_gate.shape[2]
    chunks = 4 if hidden % 512 == 0 else 1
    out_shape = [
        jax.ShapeDtypeStruct((n_e * count, width), jnp.float32 if d == 0 else jnp.bfloat16) for d in range(n_b)
    ]
    return pl.pallas_call(
        functools.partial(ffn_kernel, n_e, n_b, count, chunks),
        name="ffn",
        out_shape=out_shape,
        in_specs=[VMEM] * n_e + [ANY] * 3,
        out_specs=[VMEM] * n_b,
        scratch_shapes=[
            pltpu.VMEM(w_gate.shape[1:], w_gate.dtype),
            pltpu.VMEM(w_up.shape[1:], w_up.dtype),
            pltpu.VMEM(w_down.shape[1:], w_down.dtype),
            pltpu.VMEM((n_e * rows, hidden), jnp.float32),
            pltpu.VMEM((n_e * rows, hidden), jnp.float32),
            pltpu.SemaphoreType.DMA((3, chunks)),
        ],
    )(*xs, w_gate, w_up, w_down)


def merge_kernel(n_b, *refs):
    total = refs[0][...]
    for r in refs[1:n_b]:
        total = total + r[...].astype(jnp.float32)
    outs = refs[n_b:]
    count = total.shape[0] // len(outs)
    for m, out in enumerate(outs):
        out[...] = total[m * count : (m + 1) * count].astype(out.dtype)


def merge(parts, n_e):
    rows, width = parts[0].shape
    return pl.pallas_call(
        functools.partial(merge_kernel, len(parts)),
        name="merge",
        out_shape=[jax.ShapeDtypeStruct((rows // n_e, width), jnp.bfloat16)] * n_e,
        in_specs=[VMEM] * len(parts),
        out_specs=[VMEM] * n_e,
    )(*parts)


def on_device(tokens, route_ids, route_slots, gate_fixed, w_gate, w_up, w_down):
    count = tokens.shape[0]
    n_e, n_b = lax.axis_size("expert"), lax.axis_size("blk")
    fixed = gate_fixed.astype(jnp.float32)
    shares = fixed / jnp.sum(fixed, axis=1, keepdims=True)
    me = lax.axis_index("expert")
    mine = stack([tokens] + [fetch(tokens, "blk", d) for d in range(1, n_b)])
    xs = [mine] + [fetch(mine, "expert", m) for m in range(1, n_e)]
    parts = ffn(xs, w_gate, w_up, w_down, n_b, count)
    parts = [parts[0]] + [deliver(parts[d], "blk", d) for d in range(1, n_b)]
    blocks = merge(parts, n_e)
    blocks = [blocks[0]] + [deliver(blocks[m], "expert", m) for m in range(1, n_e)]
    mixed = 0.0
    for m, block in enumerate(blocks):
        share = jnp.sum(jnp.where(route_ids == source(me, m, n_e), shares, 0.0), axis=1, keepdims=True)
        mixed = mixed + share * block.astype(jnp.float32)
    return mixed.astype(jnp.bfloat16)


def solution(mesh):
    return jax.shard_map(
        on_device,
        mesh=mesh,
        in_specs=(
            P(("group", "expert", "blk"), None),
            P(("group", "expert", "blk"), None),
            P(("group", "expert", "blk"), None),
            P(("group", "expert", "blk"), None),
            P("expert", None, "blk"),
            P("expert", None, "blk"),
            P("expert", "blk", None),
        ),
        out_specs=P(("group", "expert", "blk"), None),
        check_vma=False,
    )
```

time: 85.6 us -> 48.2 us (0.56)
  blocking collectives: 22.3 us -> 0 us
  matrix products: 14.7 us -> 0 us
  Pallas kernels: 0 us -> 13.5 us
  between operations: 13.5 us -> 0.05 us
  starting transfers between devices: 3.32 us -> 14.1 us
  waiting for transfers between devices: 27.2 us -> 16.8 us
  local copies, waits for them, and re-layouts: 2.86 us -> 1.88 us
    reduce_scatter x1 -> x0, waiting for transfers between devices: 22.6 us -> none  [on_device(): lax.psum_scatter(jnp.dot(hidden, down_mat, preferred_element_type=jnp.flo...]
    ppermute x0 -> x12, waiting for transfers between devices: none -> 16.8 us  [the longest x6 9.6 us: fetch(): return lax.ppermute(x, axis, [(peer(i, d, n), i) for i in range(n)])]
    dot_general x3 -> x0, matrix products: 14.7 us -> none  [the longest x1 9.6 us: on_device(): jnp.dot(hidden, down_mat, preferred_element_type=jnp.float32)]
    all_gather x1 -> x0, blocking collectives: 14.1 us -> none  [on_device(): gathered = lax.all_gather(arrived, 'blk', axis=0, tiled=True)]
    ppermute x0 -> x12, starting transfers between devices: none -> 14.1 us  [the longest x6 7.5 us: fetch(): return lax.ppermute(x, axis, [(peer(i, d, n), i) for i in range(n)])]
    pallas_call x0 -> x3, Pallas kernels: none -> 13.5 us  [the longest x1 10.5 us: ffn(): pl.pallas_call(functools.partial(ffn_kernel, n_e, n_b, count, chunks), na...]
    all_to_all x1 -> x0, blocking collectives: 8.16 us -> none  [on_device(): lax.all_to_all(outgoing, 'expert', split_axis=0, concat_axis=0, tiled=True)]
    all_to_all x1 -> x0, waiting for transfers between devices: 4.55 us -> none  [on_device(): lax.all_to_all(summed.reshape(experts, capacity, width), 'expert', split_...]
  transfers between devices with their start and end apart: 2 -> 12, of which waited for: 2 -> 8; matrix products, arithmetic and copies ran while one was open for 0% -> 0% of each run, Pallas kernels for 0% -> 0%
where the time goes in v1:
time: 48.2 us; the launch traced here: 47.8 us
  waiting for transfers between devices  16.8 us (35%)
  starting transfers between devices  14.1 us (29%)
  Pallas kernels  13.5 us (28%)
  local copies, waits for them, and re-layouts  1.88 us (4%)
  other arithmetic  1.45 us (3%)
    pallas_call x1, Pallas kernels, ffn(): pl.pallas_call(functools.partial(ffn_kernel, n_e, n_b, count, chunks), na...  10.5 us
    ppermute x6, waiting for transfers between devices, fetch(): return lax.ppermute(x, axis, [(peer(i, d, n), i) for i in range(n)])  9.6 us
    ppermute x6, starting transfers between devices, fetch(): return lax.ppermute(x, axis, [(peer(i, d, n), i) for i in range(n)])  7.5 us
    ppermute x6, waiting for transfers between devices, deliver(): return lax.ppermute(x, axis, [(i, peer(i, d, n)) for i in range(n)])  7.19 us
    ppermute x6, starting transfers between devices, deliver(): return lax.ppermute(x, axis, [(i, peer(i, d, n)) for i in range(n)])  6.59 us
    unnamed x22, local copies, waits for them, and re-layouts  1.88 us
    pallas_call x1, Pallas kernels, merge(): pl.pallas_call(functools.partial(merge_kernel, len(parts)), name='merge',...  1.62 us
    pallas_call x1, Pallas kernels, stack(): pl.pallas_call(stack_kernel, name='stack', out_shape=jax.ShapeDtypeStruct...  1.41 us
  transfers between devices with their start and end apart: 12, of which 8 were waited for; matrix products, arithmetic and copies ran while one was open for 0% of the time, Pallas kernels for 0%

profile of v1, /device:TPU:0, one launch (start us, length us, event | category | flops | bytes accessed | tf_op | source)
XLA Modules:
  0.0 47.8 jit_solution(17593889089612446724)
XLA Ops:
  0.0 3.1 %collective-permute-start = (bf16[4,2048]{1,0:T(4,128)(2,1)}, bf16[4,2048]{1,0:T(4,128)(2,1)S(1)}, u32[]{:S(2)}, u32[]{:S(2)}) collective-permute-start(bf16[4,2048]{1,0:T(4,128)(2,1)} %refs_0_.1), channel_id=1, source_target_pairs={{1,0},{0,1},{3,2},{2,3},{5,4},{4,5},{7,6},{6,7},{9,8},{8,9},{11,10... | collective-permute-start | bytes 49160 | tf_op jit(solution)/shard_map/ppermute | solution.py:24
  3.1 2.6 %collective-permute-start.1 = (bf16[4,2048]{1,0:T(4,128)(2,1)}, bf16[4,2048]{1,0:T(4,128)(2,1)S(1)}, u32[]{:S(2)}, u32[]{:S(2)}) collective-permute-start(bf16[4,2048]{1,0:T(4,128)(2,1)} %refs_0_.1), channel_id=1, source_target_pairs={{2,0},{3,1},{0,2},{1,3},{6,4},{7,5},{4,6},{5,7},{10,8},{11,9},{8,1... | collective-permute-start | bytes 49160 | tf_op jit(solution)/shard_map/ppermute | solution.py:24
  5.7 2.3 %collective-permute-done.1.refs_2_ = bf16[4,2048]{1,0:T(4,128)(2,1)S(1)} collective-permute-done((bf16[4,2048]{1,0:T(4,128)(2,1)}, bf16[4,2048]{1,0:T(4,128)(2,1)S(1)}, u32[]{:S(2)}, u32[]{:S(2)}) %collective-permute-start.1) | collective-permute-done | bytes 16416 | tf_op jit(solution)/shard_map/ppermute | solution.py:24
  8.0 3.4 %collective-permute-done.2.refs_3_ = bf16[4,2048]{1,0:T(4,128)(2,1)S(1)} collective-permute-done((bf16[4,2048]{1,0:T(4,128)(2,1)}, bf16[4,2048]{1,0:T(4,128)(2,1)S(1)}, u32[]{:S(2)}, u32[]{:S(2)}) %collective-permute-start.2) | collective-permute-done | bytes 16416 | tf_op jit(solution)/shard_map/ppermute | solution.py:24
  11.4 0.6 %copy-done.8 = bf16[4,2048]{1,0:T(4,128)(2,1)} copy-done((bf16[4,2048]{1,0:T(4,128)(2,1)}, bf16[4,2048]{1,0:T(4,128)(2,1)S(1)}, u32[]{:S(2)}) %copy-start.8) | copy-done | bytes 16408
  12.0 1.4 %stack.1.refs_0_ = bf16[16,2048]{1,0:T(8,128)(2,1)} custom-call(bf16[4,2048]{1,0:T(4,128)(2,1)} %refs_0_.1, bf16[4,2048]{1,0:T(4,128)(2,1)} %copy-done.6, bf16[4,2048]{1,0:T(4,128)(2,1)} %copy-done.7, bf16[4,2048]{1,0:T(4,128)(2,1)} %copy-done.8), custom_call_target="tpu_custom_call" | custom-call | tf_op jit(solution)/shard_map/stack/pallas_call | solution.py:40
  13.4 1.5 %collective-permute-start.4 = (bf16[16,2048]{1,0:T(8,128)(2,1)}, bf16[16,2048]{1,0:T(8,128)(2,1)S(1)}, u32[]{:S(2)}, u32[]{:S(2)}) collective-permute-start(bf16[16,2048]{1,0:T(8,128)(2,1)} %stack.1.refs_0_), channel_id=1, source_target_pairs={{8,0},{12,4},{0,8},{4,12},{9,1},{13,5},{1,9},{5,13},{10,2},{14,6},... | collective-permute-start | bytes 196616 | tf_op jit(solution)/shard_map/ppermute | solution.py:24
  14.9 0.4 collective-permute-start.5
  15.3 2.9 %collective-permute-done.4.refs_2_ = bf16[16,2048]{1,0:T(8,128)(2,1)S(1)} collective-permute-done((bf16[16,2048]{1,0:T(8,128)(2,1)}, bf16[16,2048]{1,0:T(8,128)(2,1)S(1)}, u32[]{:S(2)}, u32[]{:S(2)}) %collective-permute-start.4) | collective-permute-done | bytes 65568 | tf_op jit(solution)/shard_map/ppermute | solution.py:24
  18.2 1.0 %collective-permute-done.5.refs_3_ = bf16[16,2048]{1,0:T(8,128)(2,1)S(1)} collective-permute-done((bf16[16,2048]{1,0:T(8,128)(2,1)}, bf16[16,2048]{1,0:T(8,128)(2,1)S(1)}, u32[]{:S(2)}, u32[]{:S(2)}) %collective-permute-start.5) | collective-permute-done | bytes 65568 | tf_op jit(solution)/shard_map/ppermute | solution.py:24
  19.2 0.6 %copy-done.2 = bf16[16,2048]{1,0:T(8,128)(2,1)} copy-done((bf16[16,2048]{1,0:T(8,128)(2,1)}, bf16[16,2048]{1,0:T(8,128)(2,1)S(1)}, u32[]{:S(2)}) %copy-start.2) | copy-done | bytes 65560
  19.8 10.5 %ffn.1 = (f32[16,2048]{1,0:T(8,128)}, bf16[16,2048]{1,0:T(8,128)(2,1)}, bf16[16,2048]{1,0:T(8,128)(2,1)}, bf16[16,2048]{1,0:T(8,128)(2,1)}) custom-call(bf16[16,2048]{1,0:T(8,128)(2,1)} %stack.1.refs_0_, bf16[16,2048]{1,0:T(8,128)(2,1)} %copy-done, bf16[16,2048]{1,0:T(8,128)(2,1)} %copy-done.1, bf16[16,2048]{1,0:T(8,128)(2,1)} %copy-done.2, ...), custom_call_target="tpu_custom_call" | custom-call | tf_op jit(solution)/shard_map/ffn/pallas_call | solution.py:92
  30.3 0.1 collective-permute-start.6
  30.3 0.7 %collective-permute-start.7 = (bf16[16,2048]{1,0:T(8,128)(2,1)}, bf16[16,2048]{1,0:T(8,128)(2,1)S(1)}, u32[]{:S(2)}, u32[]{:S(2)}) collective-permute-start(bf16[16,2048]{1,0:T(8,128)(2,1)} %get-tuple-element.15), channel_id=1, source_target_pairs={{0,2},{1,3},{2,0},{3,1},{4,6},{5,7},{6,4},{7,5},{8,10},{9,11},{10,... | collective-permute-start | bytes 196616 | tf_op jit(solution)/shard_map/ppermute | solution.py:29
  31.1 3.7 %collective-permute-start.8 = (bf16[16,2048]{1,0:T(8,128)(2,1)}, bf16[16,2048]{1,0:T(8,128)(2,1)S(1)}, u32[]{:S(2)}, u32[]{:S(2)}) collective-permute-start(bf16[16,2048]{1,0:T(8,128)(2,1)} %get-tuple-element.16), channel_id=1, source_target_pairs={{0,3},{1,2},{2,1},{3,0},{4,7},{5,6},{6,5},{7,4},{8,11},{9,10},{10,... | collective-permute-start | bytes 196616 | tf_op jit(solution)/shard_map/ppermute | solution.py:29
  34.7 1.0 %collective-permute-done.6.refs_1_ = bf16[16,2048]{1,0:T(8,128)(2,1)S(1)} collective-permute-done((bf16[16,2048]{1,0:T(8,128)(2,1)}, bf16[16,2048]{1,0:T(8,128)(2,1)S(1)}, u32[]{:S(2)}, u32[]{:S(2)}) %collective-permute-start.6) | collective-permute-done | bytes 65568 | tf_op jit(solution)/shard_map/ppermute | solution.py:29
  35.7 3.5 %collective-permute-done.7.refs_2_ = bf16[16,2048]{1,0:T(8,128)(2,1)S(1)} collective-permute-done((bf16[16,2048]{1,0:T(8,128)(2,1)}, bf16[16,2048]{1,0:T(8,128)(2,1)S(1)}, u32[]{:S(2)}, u32[]{:S(2)}) %collective-permute-start.7) | collective-permute-done | bytes 65568 | tf_op jit(solution)/shard_map/ppermute | solution.py:29
  39.2 0.6 %copy-done.4 = bf16[16,2048]{1,0:T(8,128)(2,1)} copy-done((bf16[16,2048]{1,0:T(8,128)(2,1)}, bf16[16,2048]{1,0:T(8,128)(2,1)S(1)}, u32[]{:S(2)}) %copy-start.4) | copy-done | bytes 65560
  39.9 1.6 %merge.1 = (bf16[4,2048]{1,0:T(4,128)(2,1)}, bf16[4,2048]{1,0:T(4,128)(2,1)}, bf16[4,2048]{1,0:T(4,128)(2,1)}, bf16[4,2048]{1,0:T(4,128)(2,1)}) custom-call(f32[16,2048]{1,0:T(8,128)} %get-tuple-element.13.refs_0_, bf16[16,2048]{1,0:T(8,128)(2,1)} %copy-done.3, bf16[16,2048]{1,0:T(8,128)(2,1)} %copy-done.4, bf16[16,2048]{1,0:T(8,128)(2,1)} %copy-done.5), custom_call_target="tpu_custom_call" | custom-call | tf_op jit(solution)/shard_map/merge/pallas_call | solution.py:121
  41.5 1.5 %collective-permute-start.10 = (bf16[4,2048]{1,0:T(4,128)(2,1)}, bf16[4,2048]{1,0:T(4,128)(2,1)S(1)}, u32[]{:S(2)}, u32[]{:S(2)}) collective-permute-start(bf16[4,2048]{1,0:T(4,128)(2,1)} %get-tuple-element.19), channel_id=1, source_target_pairs={{0,8},{4,12},{8,0},{12,4},{1,9},{5,13},{9,1},{13,5},{2,10},{6,14},... | collective-permute-start | bytes 49160 | tf_op jit(solution)/shard_map/ppermute | solution.py:29
  43.0 0.6 %collective-permute-start.9 = (bf16[4,2048]{1,0:T(4,128)(2,1)}, bf16[4,2048]{1,0:T(4,128)(2,1)S(1)}, u32[]{:S(2)}, u32[]{:S(2)}) collective-permute-start(bf16[4,2048]{1,0:T(4,128)(2,1)} %get-tuple-element.18), channel_id=1, source_target_pairs={{0,4},{4,0},{8,12},{12,8},{1,5},{5,1},{9,13},{13,9},{2,6},{6,2},{1... | collective-permute-start | bytes 49160 | tf_op jit(solution)/shard_map/ppermute | solution.py:29
  43.7 1.8 %collective-permute-done.10 = bf16[4,2048]{1,0:T(4,128)(2,1)S(1)} collective-permute-done((bf16[4,2048]{1,0:T(4,128)(2,1)}, bf16[4,2048]{1,0:T(4,128)(2,1)S(1)}, u32[]{:S(2)}, u32[]{:S(2)}) %collective-permute-start.10) | collective-permute-done | bytes 16416 | tf_op jit(solution)/shard_map/ppermute | solution.py:29
  45.4 0.9 %collective-permute-done.11 = bf16[4,2048]{1,0:T(4,128)(2,1)S(1)} collective-permute-done((bf16[4,2048]{1,0:T(4,128)(2,1)}, bf16[4,2048]{1,0:T(4,128)(2,1)S(1)}, u32[]{:S(2)}, u32[]{:S(2)}) %collective-permute-start.11) | collective-permute-done | bytes 16416 | tf_op jit(solution)/shard_map/ppermute | solution.py:29
  46.4 1.4 %add_convert_fusion = bf16[4,2048]{1,0:T(4,128)(2,1)} fusion(bf16[4,2048]{1,0:T(4,128)(2,1)S(1)} %collective-permute-done.11, bf16[4,2048]{1,0:T(4,128)(2,1)S(1)} %collective-permute-done.10, bf16[4,2048]{1,0:T(4,128)(2,1)S(1)} %collective-permute-done.9, bf16[4,2048]{1,0:T(4,128)(2,1)} %get-tuple-element.17, f32[4]{0:T(128)S(1)} %get-tuple-element.22, ...), kind=kLoop, calls=%fused_computation | loop fusion | flops 98304 | bytes 81984 | tf_op jit(solution)/shard_map/convert_element_type | solution.py:146
  (28 shorter events, 0.1 us)
Async XLA Ops:
  0.0 5.6 %collective-permute-start = (bf16[4,2048]{1,0:T(4,128)(2,1)}, bf16[4,2048]{1,0:T(4,128)(2,1)S(1)}, u32[]{:S(2)}, u32[]{:S(2)}) collective-permute-start(bf16[4,2048]{1,0:T(4,128)(2,1)} %refs_0_.1), channel_id=1, source_target_pairs={{1,0},{0,1},{3,2},{2,3},{5,4},{4,5},{7,6},{6,7},{9,8},{8,9},{11,10... | collective-permute-start | bytes 49160 | tf_op jit(solution)/shard_map/ppermute | solution.py:24
  3.1 4.9 %collective-permute-start.1 = (bf16[4,2048]{1,0:T(4,128)(2,1)}, bf16[4,2048]{1,0:T(4,128)(2,1)S(1)}, u32[]{:S(2)}, u32[]{:S(2)}) collective-permute-start(bf16[4,2048]{1,0:T(4,128)(2,1)} %refs_0_.1), channel_id=1, source_target_pairs={{2,0},{3,1},{0,2},{1,3},{6,4},{7,5},{4,6},{5,7},{10,8},{11,9},{8,1... | collective-permute-start | bytes 49160 | tf_op jit(solution)/shard_map/ppermute | solution.py:24
  5.6 5.7 %collective-permute-start.2 = (bf16[4,2048]{1,0:T(4,128)(2,1)}, bf16[4,2048]{1,0:T(4,128)(2,1)S(1)}, u32[]{:S(2)}, u32[]{:S(2)}) collective-permute-start(bf16[4,2048]{1,0:T(4,128)(2,1)} %refs_0_.1), channel_id=1, source_target_pairs={{3,0},{2,1},{1,2},{0,3},{7,4},{6,5},{5,6},{4,7},{11,8},{10,9},{9,1... | collective-permute-start | bytes 49160 | tf_op jit(solution)/shard_map/ppermute | solution.py:24
  5.6 5.7 %copy-start.6 = (bf16[4,2048]{1,0:T(4,128)(2,1)}, bf16[4,2048]{1,0:T(4,128)(2,1)S(1)}, u32[]{:S(2)}) copy-start(bf16[4,2048]{1,0:T(4,128)(2,1)S(1)} %collective-permute-done.refs_1_) | copy-start | bytes 49156
  8.0 3.4 %copy-start.7 = (bf16[4,2048]{1,0:T(4,128)(2,1)}, bf16[4,2048]{1,0:T(4,128)(2,1)S(1)}, u32[]{:S(2)}) copy-start(bf16[4,2048]{1,0:T(4,128)(2,1)S(1)} %collective-permute-done.1.refs_2_) | copy-start | bytes 49156
  11.4 0.6 %copy-start.8 = (bf16[4,2048]{1,0:T(4,128)(2,1)}, bf16[4,2048]{1,0:T(4,128)(2,1)S(1)}, u32[]{:S(2)}) copy-start(bf16[4,2048]{1,0:T(4,128)(2,1)S(1)} %collective-permute-done.2.refs_3_) | copy-start | bytes 49156
  13.4 1.9 %collective-permute-start.3 = (bf16[16,2048]{1,0:T(8,128)(2,1)}, bf16[16,2048]{1,0:T(8,128)(2,1)S(1)}, u32[]{:S(2)}, u32[]{:S(2)}) collective-permute-start(bf16[16,2048]{1,0:T(8,128)(2,1)} %stack.1.refs_0_), channel_id=1, source_target_pairs={{4,0},{0,4},{12,8},{8,12},{5,1},{1,5},{13,9},{9,13},{6,2},{2,6},{1... | collective-permute-start | bytes 196616 | tf_op jit(solution)/shard_map/ppermute | solution.py:24
  13.4 4.7 %collective-permute-start.4 = (bf16[16,2048]{1,0:T(8,128)(2,1)}, bf16[16,2048]{1,0:T(8,128)(2,1)S(1)}, u32[]{:S(2)}, u32[]{:S(2)}) collective-permute-start(bf16[16,2048]{1,0:T(8,128)(2,1)} %stack.1.refs_0_), channel_id=1, source_target_pairs={{8,0},{12,4},{0,8},{4,12},{9,1},{13,5},{1,9},{5,13},{10,2},{14,6},... | collective-permute-start | bytes 196616 | tf_op jit(solution)/shard_map/ppermute | solution.py:24
  14.9 4.2 %collective-permute-start.5 = (bf16[16,2048]{1,0:T(8,128)(2,1)}, bf16[16,2048]{1,0:T(8,128)(2,1)S(1)}, u32[]{:S(2)}, u32[]{:S(2)}) collective-permute-start(bf16[16,2048]{1,0:T(8,128)(2,1)} %stack.1.refs_0_), channel_id=1, source_target_pairs={{12,0},{8,4},{4,8},{0,12},{13,1},{9,5},{5,9},{1,13},{14,2},{10,6},... | collective-permute-start | bytes 196616 | tf_op jit(solution)/shard_map/ppermute | solution.py:24
  15.3 19.4 %copy-start.10 = (s32[4,2]{0,1:T(2,128)S(1)}, s32[4,2]{0,1:T(2,128)}, u32[]{:S(2)}) copy-start(s32[4,2]{0,1:T(2,128)} %param.9) | copy-start | bytes 100
  15.3 28.4 %copy-start.9 = (s32[4,2]{0,1:T(2,128)S(1)}, s32[4,2]{0,1:T(2,128)}, u32[]{:S(2)}) copy-start(s32[4,2]{0,1:T(2,128)} %param.8) | copy-start | bytes 100
  15.3 3.9 %copy-start = (bf16[16,2048]{1,0:T(8,128)(2,1)}, bf16[16,2048]{1,0:T(8,128)(2,1)S(1)}, u32[]{:S(2)}) copy-start(bf16[16,2048]{1,0:T(8,128)(2,1)S(1)} %collective-permute-done.3.refs_1_) | copy-start | bytes 196612
  18.1 1.0 %copy-start.1 = (bf16[16,2048]{1,0:T(8,128)(2,1)}, bf16[16,2048]{1,0:T(8,128)(2,1)S(1)}, u32[]{:S(2)}) copy-start(bf16[16,2048]{1,0:T(8,128)(2,1)S(1)} %collective-permute-done.4.refs_2_) | copy-start | bytes 196612
  19.2 0.6 %copy-start.2 = (bf16[16,2048]{1,0:T(8,128)(2,1)}, bf16[16,2048]{1,0:T(8,128)(2,1)S(1)}, u32[]{:S(2)}) copy-start(bf16[16,2048]{1,0:T(8,128)(2,1)S(1)} %collective-permute-done.5.refs_3_) | copy-start | bytes 196612
  30.3 5.5 %collective-permute-start.6 = (bf16[16,2048]{1,0:T(8,128)(2,1)}, bf16[16,2048]{1,0:T(8,128)(2,1)S(1)}, u32[]{:S(2)}, u32[]{:S(2)}) collective-permute-start(bf16[16,2048]{1,0:T(8,128)(2,1)} %get-tuple-element.14), channel_id=1, source_target_pairs={{0,1},{1,0},{2,3},{3,2},{4,5},{5,4},{6,7},{7,6},{8,9},{9,8},{10,11... | collective-permute-start | bytes 196616 | tf_op jit(solution)/shard_map/ppermute | solution.py:29
  30.3 8.9 %collective-permute-start.7 = (bf16[16,2048]{1,0:T(8,128)(2,1)}, bf16[16,2048]{1,0:T(8,128)(2,1)S(1)}, u32[]{:S(2)}, u32[]{:S(2)}) collective-permute-start(bf16[16,2048]{1,0:T(8,128)(2,1)} %get-tuple-element.15), channel_id=1, source_target_pairs={{0,2},{1,3},{2,0},{3,1},{4,6},{5,7},{6,4},{7,5},{8,10},{9,11},{10,... | collective-permute-start | bytes 196616 | tf_op jit(solution)/shard_map/ppermute | solution.py:29
  31.1 8.2 %collective-permute-start.8 = (bf16[16,2048]{1,0:T(8,128)(2,1)}, bf16[16,2048]{1,0:T(8,128)(2,1)S(1)}, u32[]{:S(2)}, u32[]{:S(2)}) collective-permute-start(bf16[16,2048]{1,0:T(8,128)(2,1)} %get-tuple-element.16), channel_id=1, source_target_pairs={{0,3},{1,2},{2,1},{3,0},{4,7},{5,6},{6,5},{7,4},{8,11},{9,10},{10,... | collective-permute-start | bytes 196616 | tf_op jit(solution)/shard_map/ppermute | solution.py:29
  35.7 3.5 %copy-start.3 = (bf16[16,2048]{1,0:T(8,128)(2,1)}, bf16[16,2048]{1,0:T(8,128)(2,1)S(1)}, u32[]{:S(2)}) copy-start(bf16[16,2048]{1,0:T(8,128)(2,1)S(1)} %collective-permute-done.6.refs_1_) | copy-start | bytes 196612
  39.2 0.6 %copy-start.4 = (bf16[16,2048]{1,0:T(8,128)(2,1)}, bf16[16,2048]{1,0:T(8,128)(2,1)S(1)}, u32[]{:S(2)}) copy-start(bf16[16,2048]{1,0:T(8,128)(2,1)S(1)} %collective-permute-done.7.refs_2_) | copy-start | bytes 196612
  39.2 0.6 %copy-start.5 = (bf16[16,2048]{1,0:T(8,128)(2,1)}, bf16[16,2048]{1,0:T(8,128)(2,1)S(1)}, u32[]{:S(2)}) copy-start(bf16[16,2048]{1,0:T(8,128)(2,1)S(1)} %collective-permute-done.8.refs_3_) | copy-start | bytes 196612
  41.5 3.9 %collective-permute-start.10 = (bf16[4,2048]{1,0:T(4,128)(2,1)}, bf16[4,2048]{1,0:T(4,128)(2,1)S(1)}, u32[]{:S(2)}, u32[]{:S(2)}) collective-permute-start(bf16[4,2048]{1,0:T(4,128)(2,1)} %get-tuple-element.19), channel_id=1, source_target_pairs={{0,8},{4,12},{8,0},{12,4},{1,9},{5,13},{9,1},{13,5},{2,10},{6,14},... | collective-permute-start | bytes 49160 | tf_op jit(solution)/shard_map/ppermute | solution.py:29
  43.0 3.4 %collective-permute-start.11 = (bf16[4,2048]{1,0:T(4,128)(2,1)}, bf16[4,2048]{1,0:T(4,128)(2,1)S(1)}, u32[]{:S(2)}, u32[]{:S(2)}) collective-permute-start(bf16[4,2048]{1,0:T(4,128)(2,1)} %get-tuple-element.20), channel_id=1, source_target_pairs={{0,12},{4,8},{8,4},{12,0},{1,13},{5,9},{9,5},{13,1},{2,14},{6,10},... | collective-permute-start | bytes 49160 | tf_op jit(solution)/shard_map/ppermute | solution.py:29
  43.0 3.4 %collective-permute-start.9 = (bf16[4,2048]{1,0:T(4,128)(2,1)}, bf16[4,2048]{1,0:T(4,128)(2,1)S(1)}, u32[]{:S(2)}, u32[]{:S(2)}) collective-permute-start(bf16[4,2048]{1,0:T(4,128)(2,1)} %get-tuple-element.18), channel_id=1, source_target_pairs={{0,4},{4,0},{8,12},{12,8},{1,5},{5,1},{9,13},{13,9},{2,6},{6,2},{1... | collective-permute-start | bytes 49160 | tf_op jit(solution)/shard_map/ppermute | solution.py:29

commit v2 on v1

v2 whole, which is shorter than its diff:
```python
import functools

import jax
import jax.numpy as jnp
from jax import lax
from jax.experimental import pallas as pl
from jax.experimental.pallas import tpu as pltpu
from jax.sharding import PartitionSpec as P

VMEM = pl.BlockSpec(memory_space=pltpu.VMEM)
ANY = pl.BlockSpec(memory_space=pl.ANY)


def peer(i, d, n):
    return i ^ d if n & (n - 1) == 0 else (i + d) % n


def source(i, d, n):
    return i ^ d if n & (n - 1) == 0 else (i - d) % n


def fetch(x, axis, d):
    n = lax.axis_size(axis)
    return lax.ppermute(x, axis, [(peer(i, d, n), i) for i in range(n)])


def deliver(x, axis, d):
    n = lax.axis_size(axis)
    return lax.ppermute(x, axis, [(i, peer(i, d, n)) for i in range(n)])


def stack_kernel(*refs):
    out = refs[-1]
    rows = [r[...].astype(jnp.float32) for r in refs[:-1]]
    out[...] = jnp.concatenate(rows, axis=0).astype(out.dtype)


def stack(blocks):
    rows = sum(b.shape[0] for b in blocks)
    return pl.pallas_call(
        stack_kernel,
        name="stack",
        compiler_params=pltpu.CompilerParams(vmem_limit_bytes=8 << 20),
        out_shape=jax.ShapeDtypeStruct((rows, blocks[0].shape[1]), blocks[0].dtype),
        in_specs=[VMEM] * len(blocks),
        out_specs=VMEM,
    )(*blocks)


def prefetch_kernel(chunks, with_rows, *refs):
    sems, dst = refs[-1], refs[-2 - with_rows]
    depth = dst.shape[0] // chunks
    copies = []
    if with_rows:
        copies.append(pltpu.make_async_copy(refs[1], refs[-2], sems.at[chunks]))
    for c in range(chunks):
        rows = pl.ds(c * depth, depth)
        copies.append(pltpu.make_async_copy(refs[0].at[0, rows, :], dst.at[rows, :], sems.at[c]))
    for copy in copies:
        copy.start()
    for copy in copies:
        copy.wait()


def in_hbm(w):
    return pltpu.with_memory_space_constraint(w, pltpu.HBM)


def in_vmem(w):
    return pltpu.with_memory_space_constraint(w, pltpu.VMEM)


def prefetch(w, rows=None, after=None):
    chunks = 4 if w.shape[1] % 512 == 0 else 1
    more = [x for x in (rows, after) if x is not None]
    out_shape = [pltpu.VMEM(w.shape[1:], w.dtype)]
    if rows is not None:
        out_shape.append(pltpu.VMEM(rows.shape, rows.dtype))
        more = [in_hbm(rows)]
    return pl.pallas_call(
        functools.partial(prefetch_kernel, chunks, rows is not None),
        name="prefetch",
        compiler_params=pltpu.CompilerParams(vmem_limit_bytes=1 << 20),
        cost_estimate=pl.CostEstimate(flops=0, transcendentals=0, bytes_accessed=w.size * 4),
        out_shape=out_shape,
        in_specs=[ANY] * (1 + len(more)),
        out_specs=[VMEM] * len(out_shape),
        scratch_shapes=[pltpu.SemaphoreType.DMA((chunks + 1,))],
    )(in_hbm(w), *more)


def ffn_kernel(n_e, n_b, count, chunks, *refs):
    xs = refs[:n_e]
    gate_w, up_w, down_hbm = refs[n_e : n_e + 3]
    outs = refs[n_e + 3 : n_e + 3 + n_b]
    down_w, sems = refs[n_e + 3 + n_b :]
    inner = down_w.shape[0] // chunks
    copies = []
    for c in range(chunks):
        rows = pl.ds(c * inner, inner)
        copies.append(pltpu.make_async_copy(down_hbm.at[0, rows, :], down_w.at[rows, :], sems.at[c]))
        copies[c].start()
    x = jnp.concatenate([r[...] for r in xs], axis=0)
    total = None
    for c in range(chunks):
        cut = slice(c * inner, (c + 1) * inner)
        v = jnp.dot(x, gate_w[:, cut], preferred_element_type=jnp.float32)
        u = jnp.dot(x, up_w[:, cut], preferred_element_type=jnp.float32)
        hidden = (v / (1.0 + jnp.exp(-v)) * u).astype(jnp.bfloat16)
        copies[c].wait()
        part = jnp.dot(hidden, down_w[cut, :], preferred_element_type=jnp.float32)
        total = part if c == 0 else total + part
    for d, out in enumerate(outs):
        rows = [total[(m * n_b + d) * count : (m * n_b + d + 1) * count] for m in range(n_e)]
        out[...] = jnp.concatenate(rows, axis=0).astype(out.dtype)


def ffn(xs, w_gate, w_up, w_down, n_b, count):
    n_e, width = len(xs), xs[0].shape[1]
    hidden = w_gate.shape[1]
    chunks = 4 if hidden % 512 == 0 else 1
    out_shape = [
        jax.ShapeDtypeStruct((n_e * count, width), jnp.float32 if d == 0 else jnp.bfloat16) for d in range(n_b)
    ]
    return pl.pallas_call(
        functools.partial(ffn_kernel, n_e, n_b, count, chunks),
        name="ffn",
        compiler_params=pltpu.CompilerParams(vmem_limit_bytes=16 << 20),
        out_shape=out_shape,
        in_specs=[VMEM] * (n_e + 2) + [ANY],
        out_specs=[VMEM] * n_b,
        scratch_shapes=[
            pltpu.VMEM(w_down.shape[1:], w_down.dtype),
            pltpu.SemaphoreType.DMA((chunks,)),
        ],
    )(*xs, in_vmem(w_gate), in_vmem(w_up), in_hbm(w_down))


def merge_kernel(n_b, *refs):
    total = refs[0][...]
    for r in refs[1:n_b]:
        total = total + r[...].astype(jnp.float32)
    outs = refs[n_b:]
    count = total.shape[0] // len(outs)
    for m, out in enumerate(outs):
        out[...] = total[m * count : (m + 1) * count].astype(out.dtype)


def merge(parts, n_e):
    rows, width = parts[0].shape
    return pl.pallas_call(
        functools.partial(merge_kernel, len(parts)),
        name="merge",
        compiler_params=pltpu.CompilerParams(vmem_limit_bytes=8 << 20),
        out_shape=[jax.ShapeDtypeStruct((rows // n_e, width), jnp.bfloat16)] * n_e,
        in_specs=[VMEM] * len(parts),
        out_specs=[VMEM] * n_e,
    )(*parts)


def mix_kernel(n_e, ids_ref, fixed_ref, *refs):
    blocks, out = refs[:-1], refs[-1]
    me = lax.axis_index("expert")
    ids = ids_ref[...]
    fixed = fixed_ref[...].astype(jnp.float32)
    shares = fixed / jnp.sum(fixed, axis=1, keepdims=True)
    mixed = None
    for m, block in enumerate(blocks):
        share = jnp.sum(jnp.where(ids == source(me, m, n_e), shares, 0.0), axis=1, keepdims=True)
        part = share * block[...].astype(jnp.float32)
        mixed = part if m == 0 else mixed + part
    out[...] = mixed.astype(out.dtype)


def mix(route_ids, gate_fixed, blocks):
    return pl.pallas_call(
        functools.partial(mix_kernel, len(blocks)),
        name="mix",
        compiler_params=pltpu.CompilerParams(vmem_limit_bytes=4 << 20),
        out_shape=jax.ShapeDtypeStruct(blocks[0].shape, jnp.bfloat16),
        in_specs=[VMEM] * (2 + len(blocks)),
        out_specs=VMEM,
    )(route_ids, gate_fixed, *blocks)


def on_device(tokens, route_ids, route_slots, gate_fixed, w_gate, w_up, w_down):
    count = tokens.shape[0]
    n_e, n_b = lax.axis_size("expert"), lax.axis_size("blk")
    others = [fetch(tokens, "blk", d) for d in range(1, n_b)]
    gate_w, own = prefetch(w_gate, rows=tokens)
    mine = stack([own] + others)
    (up_w,) = prefetch(w_up, after=mine)
    xs = [mine] + [fetch(mine, "expert", m) for m in range(1, n_e)]
    parts = ffn(xs, gate_w, up_w, w_down, n_b, count)
    parts = [parts[0]] + [deliver(parts[d], "blk", d) for d in range(1, n_b)]
    blocks = merge(parts, n_e)
    blocks = [blocks[0]] + [deliver(blocks[m], "expert", m) for m in range(1, n_e)]
    return mix(route_ids, gate_fixed, blocks)


def solution(mesh):
    return jax.shard_map(
        on_device,
        mesh=mesh,
        in_specs=(
            P(("group", "expert", "blk"), None),
            P(("group", "expert", "blk"), None),
            P(("group", "expert", "blk"), None),
            P(("group", "expert", "blk"), None),
            P("expert", None, "blk"),
            P("expert", None, "blk"),
            P("expert", "blk", None),
        ),
        out_specs=P(("group", "expert", "blk"), None),
        check_vma=False,
    )
```

time: 48.2 us -> 37.4 us (0.78)
  waiting for transfers between devices: 16.8 us -> 8.91 us
  local copies, waits for them, and re-layouts: 1.88 us -> 0.19 us
  other arithmetic: 1.45 us -> 0 us
    ppermute x6, waiting for transfers between devices: 9.6 us -> 2.43 us  [fetch(): return lax.ppermute(x, axis, [(peer(i, d, n), i) for i in range(n)])]
    pallas_call x1 -> x4, Pallas kernels: 1.41 us -> 7.84 us  [the longest x2 7.03 us: prefetch(): pl.pallas_call(functools.partial(prefetch_kernel, chunks, rows is not Non...]
    pallas_call x1, Pallas kernels: 10.5 us -> 5.88 us  [ffn(): pl.pallas_call(functools.partial(ffn_kernel, n_e, n_b, count, chunks), na...]
    unnamed x22 -> x6, local copies, waits for them, and re-layouts: 1.88 us -> 0.19 us
    pallas_call x1, Pallas kernels: 1.62 us -> 0.04 us  [merge(): pl.pallas_call(functools.partial(merge_kernel, len(parts)), name='merge',...]
    convert_element_type x1 -> x0, other arithmetic: 1.41 us -> none  [on_device(): return mixed.astype(jnp.bfloat16)]
    ppermute x6, waiting for transfers between devices: 7.19 us -> 6.48 us  [deliver(): return lax.ppermute(x, axis, [(i, peer(i, d, n)) for i in range(n)])]
  transfers between devices with their start and end apart: 12 -> 12, of which waited for: 8 -> 6; matrix products, arithmetic and copies ran while one was open for 0% -> 0% of each run, Pallas kernels for 0% -> 19%
where the time goes in v2:
time: 37.4 us; the launch traced here: 37.2 us
  starting transfers between devices  14.2 us (38%)
  Pallas kernels  13.8 us (37%)
  waiting for transfers between devices  8.91 us (24%)
    ppermute x6, starting transfers between devices, fetch(): return lax.ppermute(x, axis, [(peer(i, d, n), i) for i in range(n)])  7.56 us
    pallas_call x2, Pallas kernels, prefetch(): pl.pallas_call(functools.partial(prefetch_kernel, chunks, rows is not Non...  7.03 us
    ppermute x6, starting transfers between devices, deliver(): return lax.ppermute(x, axis, [(i, peer(i, d, n)) for i in range(n)])  6.65 us
    ppermute x6, waiting for transfers between devices, deliver(): return lax.ppermute(x, axis, [(i, peer(i, d, n)) for i in range(n)])  6.48 us
    pallas_call x1, Pallas kernels, ffn(): pl.pallas_call(functools.partial(ffn_kernel, n_e, n_b, count, chunks), na...  5.88 us
    ppermute x6, waiting for transfers between devices, fetch(): return lax.ppermute(x, axis, [(peer(i, d, n), i) for i in range(n)])  2.43 us
    pallas_call x1, Pallas kernels, mix(): pl.pallas_call(functools.partial(mix_kernel, len(blocks)), name='mix', co...  0.79 us
  transfers between devices with their start and end apart: 12, of which 6 were waited for; matrix products, arithmetic and copies ran while one was open for 0% of the time, Pallas kernels for 19%

profile of v2, /device:TPU:0, one launch (start us, length us, event | category | flops | bytes accessed | tf_op | source)
XLA Modules:
  0.0 37.2 jit_solution(7449030518862232731)
XLA Ops:
  0.0 3.1 %collective-permute-start = (bf16[4,2048]{1,0:T(4,128)(2,1)}, bf16[4,2048]{1,0:T(4,128)(2,1)S(1)}, u32[]{:S(2)}, u32[]{:S(2)}) collective-permute-start(bf16[4,2048]{1,0:T(4,128)(2,1)} %refs_1_.1), channel_id=1, source_target_pairs={{1,0},{0,1},{3,2},{2,3},{5,4},{4,5},{7,6},{6,7},{9,8},{8,9},{11,10... | collective-permute-start | bytes 49160 | tf_op jit(solution)/shard_map/ppermute | solution.py:24
  3.1 2.6 %collective-permute-start.1 = (bf16[4,2048]{1,0:T(4,128)(2,1)}, bf16[4,2048]{1,0:T(4,128)(2,1)S(1)}, u32[]{:S(2)}, u32[]{:S(2)}) collective-permute-start(bf16[4,2048]{1,0:T(4,128)(2,1)} %refs_1_.1), channel_id=1, source_target_pairs={{2,0},{3,1},{0,2},{1,3},{6,4},{7,5},{4,6},{5,7},{10,8},{11,9},{8,1... | collective-permute-start | bytes 49160 | tf_op jit(solution)/shard_map/ppermute | solution.py:24
  5.6 0.0 collective-permute-start.2
  5.6 3.5 %prefetch.2 = (bf16[2048,2048]{1,0:T(8,128)(2,1)S(1)}, bf16[4,2048]{1,0:T(4,128)(2,1)S(1)}) custom-call(bf16[1,2048,2048]{2,1,0:T(8,128)(2,1)} %refs_0_.2, bf16[4,2048]{1,0:T(4,128)(2,1)} %refs_1_.1), custom_call_target="tpu_custom_call" | custom-call | bytes 16777216 | tf_op jit(solution)/shard_map/prefetch/pallas_call | solution.py:80
  9.2 0.0 collective-permute-done.1.refs_2_
  9.2 2.2 %collective-permute-done.2.refs_3_ = bf16[4,2048]{1,0:T(4,128)(2,1)S(1)} collective-permute-done((bf16[4,2048]{1,0:T(4,128)(2,1)}, bf16[4,2048]{1,0:T(4,128)(2,1)S(1)}, u32[]{:S(2)}, u32[]{:S(2)}) %collective-permute-start.2) | collective-permute-done | bytes 16416 | tf_op jit(solution)/shard_map/ppermute | solution.py:24
  11.4 0.1 collective-permute-start.3
  11.5 1.6 %collective-permute-start.4 = (bf16[16,2048]{1,0:T(8,128)(2,1)S(1)}, bf16[16,2048]{1,0:T(8,128)(2,1)S(1)}, u32[]{:S(2)}, u32[]{:S(2)}) collective-permute-start(bf16[16,2048]{1,0:T(8,128)(2,1)S(1)} %stack.1.refs_1_.refs_0_), channel_id=1, source_target_pairs={{8,0},{12,4},{0,8},{4,12},{9,1},{13,5},{1,9},{5,13},{10,2},{14,6},... | collective-permute-start | bytes 196616 | tf_op jit(solution)/shard_map/ppermute | solution.py:24
  13.0 0.3 collective-permute-start.5
  13.3 3.5 %prefetch.3.refs_5_ = bf16[2048,2048]{1,0:T(8,128)(2,1)S(1)} custom-call(bf16[1,2048,2048]{2,1,0:T(8,128)(2,1)} %refs_0_.3, bf16[16,2048]{1,0:T(8,128)(2,1)S(1)} %stack.1.refs_1_.refs_0_), custom_call_target="tpu_custom_call" | custom-call | bytes 16777216 | tf_op jit(solution)/shard_map/prefetch/pallas_call | solution.py:80
  16.9 0.2 collective-permute-done.5.refs_3_
  17.1 5.9 %ffn.1 = (f32[16,2048]{1,0:T(8,128)S(1)}, bf16[16,2048]{1,0:T(8,128)(2,1)S(1)}, bf16[16,2048]{1,0:T(8,128)(2,1)S(1)}, bf16[16,2048]{1,0:T(8,128)(2,1)S(1)}) custom-call(bf16[16,2048]{1,0:T(8,128)(2,1)S(1)} %stack.1.refs_1_.refs_0_, bf16[16,2048]{1,0:T(8,128)(2,1)S(1)} %collective-permute-done.3.refs_1_, bf16[16,2048]{1,0:T(8,128)(2,1)S(1)} %collective-permute-done.4.refs_2_, ...), custom_call_target="tpu_custom_call" | custom-call | tf_op jit(solution)/shard_map/ffn/pallas_call | solution.py:125
  23.0 0.1 collective-permute-start.6
  23.1 2.2 %collective-permute-start.7 = (bf16[16,2048]{1,0:T(8,128)(2,1)S(1)}, bf16[16,2048]{1,0:T(8,128)(2,1)S(1)}, u32[]{:S(2)}, u32[]{:S(2)}) collective-permute-start(bf16[16,2048]{1,0:T(8,128)(2,1)S(1)} %get-tuple-element.19), channel_id=1, source_target_pairs={{0,2},{1,3},{2,0},{3,1},{4,6},{5,7},{6,4},{7,5},{8,10},{9,11},{10,... | collective-permute-start | bytes 196616 | tf_op jit(solution)/shard_map/ppermute | solution.py:29
  25.3 2.2 %collective-permute-start.8 = (bf16[16,2048]{1,0:T(8,128)(2,1)S(1)}, bf16[16,2048]{1,0:T(8,128)(2,1)S(1)}, u32[]{:S(2)}, u32[]{:S(2)}) collective-permute-start(bf16[16,2048]{1,0:T(8,128)(2,1)S(1)} %get-tuple-element.20), channel_id=1, source_target_pairs={{0,3},{1,2},{2,1},{3,0},{4,7},{5,6},{6,5},{7,4},{8,11},{9,10},{10,... | collective-permute-start | bytes 196616 | tf_op jit(solution)/shard_map/ppermute | solution.py:29
  27.5 0.8 %collective-permute-done.6.refs_1_ = bf16[16,2048]{1,0:T(8,128)(2,1)S(1)} collective-permute-done((bf16[16,2048]{1,0:T(8,128)(2,1)S(1)}, bf16[16,2048]{1,0:T(8,128)(2,1)S(1)}, u32[]{:S(2)}, u32[]{:S(2)}) %collective-permute-start.6) | collective-permute-done | bytes 65568 | tf_op jit(solution)/shard_map/ppermute | solution.py:29
  28.2 3.5 %collective-permute-done.7.refs_2_ = bf16[16,2048]{1,0:T(8,128)(2,1)S(1)} collective-permute-done((bf16[16,2048]{1,0:T(8,128)(2,1)S(1)}, bf16[16,2048]{1,0:T(8,128)(2,1)S(1)}, u32[]{:S(2)}, u32[]{:S(2)}) %collective-permute-start.7) | collective-permute-done | bytes 65568 | tf_op jit(solution)/shard_map/ppermute | solution.py:29
  31.8 1.5 %collective-permute-start.10 = (bf16[4,2048]{1,0:T(4,128)(2,1)S(1)}, bf16[4,2048]{1,0:T(4,128)(2,1)S(1)}, u32[]{:S(2)}, u32[]{:S(2)}) collective-permute-start(bf16[4,2048]{1,0:T(4,128)(2,1)S(1)} %get-tuple-element.23), channel_id=1, source_target_pairs={{0,8},{4,12},{8,0},{12,4},{1,9},{5,13},{9,1},{13,5},{2,10},{6,14},... | collective-permute-start | bytes 49160 | tf_op jit(solution)/shard_map/ppermute | solution.py:29
  33.2 0.8 %collective-permute-start.9 = (bf16[4,2048]{1,0:T(4,128)(2,1)S(1)}, bf16[4,2048]{1,0:T(4,128)(2,1)S(1)}, u32[]{:S(2)}, u32[]{:S(2)}) collective-permute-start(bf16[4,2048]{1,0:T(4,128)(2,1)S(1)} %get-tuple-element.22), channel_id=1, source_target_pairs={{0,4},{4,0},{8,12},{12,8},{1,5},{5,1},{9,13},{13,9},{2,6},{6,2},{1... | collective-permute-start | bytes 49160 | tf_op jit(solution)/shard_map/ppermute | solution.py:29
  34.0 0.1 copy.7.ids_ref
  34.1 0.1 copy.8.fixed_ref
  34.2 1.4 %collective-permute-done.10.refs_2_ = bf16[4,2048]{1,0:T(4,128)(2,1)S(1)} collective-permute-done((bf16[4,2048]{1,0:T(4,128)(2,1)S(1)}, bf16[4,2048]{1,0:T(4,128)(2,1)S(1)}, u32[]{:S(2)}, u32[]{:S(2)}) %collective-permute-start.10) | collective-permute-done | bytes 16416 | tf_op jit(solution)/shard_map/ppermute | solution.py:29
  35.6 0.8 %collective-permute-done.11.refs_3_ = bf16[4,2048]{1,0:T(4,128)(2,1)S(1)} collective-permute-done((bf16[4,2048]{1,0:T(4,128)(2,1)S(1)}, bf16[4,2048]{1,0:T(4,128)(2,1)S(1)}, u32[]{:S(2)}, u32[]{:S(2)}) %collective-permute-start.11) | collective-permute-done | bytes 16416 | tf_op jit(solution)/shard_map/ppermute | solution.py:29
  36.4 0.8 %mix.1 = bf16[4,2048]{1,0:T(4,128)(2,1)} custom-call(s32[4,2]{1,0:T(4,128)S(1)} %copy.7.ids_ref, s32[4,2]{1,0:T(4,128)S(1)} %copy.8.fixed_ref, bf16[4,2048]{1,0:T(4,128)(2,1)S(1)} %get-tuple-element.21.refs_0_, bf16[4,2048]{1,0:T(4,128)(2,1)S(1)} %collective-permute-done.9.refs_1_, bf16[4,2048]{1,0:T(4,128)(2,1)S(1)} %collective-permute-done.10.refs_2_, ...), custom_call_target="tpu_custom_call" | custom-call | tf_op jit(solution)/shard_map/mix/pallas_call | solution.py:176
  (12 shorter events, 0.1 us)
Async XLA Ops:
  0.0 9.2 %collective-permute-start = (bf16[4,2048]{1,0:T(4,128)(2,1)}, bf16[4,2048]{1,0:T(4,128)(2,1)S(1)}, u32[]{:S(2)}, u32[]{:S(2)}) collective-permute-start(bf16[4,2048]{1,0:T(4,128)(2,1)} %refs_1_.1), channel_id=1, source_target_pairs={{1,0},{0,1},{3,2},{2,3},{5,4},{4,5},{7,6},{6,7},{9,8},{8,9},{11,10... | collective-permute-start | bytes 49160 | tf_op jit(solution)/shard_map/ppermute | solution.py:24
  3.1 6.1 %collective-permute-start.1 = (bf16[4,2048]{1,0:T(4,128)(2,1)}, bf16[4,2048]{1,0:T(4,128)(2,1)S(1)}, u32[]{:S(2)}, u32[]{:S(2)}) collective-permute-start(bf16[4,2048]{1,0:T(4,128)(2,1)} %refs_1_.1), channel_id=1, source_target_pairs={{2,0},{3,1},{0,2},{1,3},{6,4},{7,5},{4,6},{5,7},{10,8},{11,9},{8,1... | collective-permute-start | bytes 49160 | tf_op jit(solution)/shard_map/ppermute | solution.py:24
  5.6 5.7 %collective-permute-start.2 = (bf16[4,2048]{1,0:T(4,128)(2,1)}, bf16[4,2048]{1,0:T(4,128)(2,1)S(1)}, u32[]{:S(2)}, u32[]{:S(2)}) collective-permute-start(bf16[4,2048]{1,0:T(4,128)(2,1)} %refs_1_.1), channel_id=1, source_target_pairs={{3,0},{2,1},{1,2},{0,3},{7,4},{6,5},{5,6},{4,7},{11,8},{10,9},{9,1... | collective-permute-start | bytes 49160 | tf_op jit(solution)/shard_map/ppermute | solution.py:24
  11.4 5.4 %collective-permute-start.3 = (bf16[16,2048]{1,0:T(8,128)(2,1)S(1)}, bf16[16,2048]{1,0:T(8,128)(2,1)S(1)}, u32[]{:S(2)}, u32[]{:S(2)}) collective-permute-start(bf16[16,2048]{1,0:T(8,128)(2,1)S(1)} %stack.1.refs_1_.refs_0_), channel_id=1, source_target_pairs={{4,0},{0,4},{12,8},{8,12},{5,1},{1,5},{13,9},{9,13},{6,2},{2,6},{1... | collective-permute-start | bytes 196616 | tf_op jit(solution)/shard_map/ppermute | solution.py:24
  11.5 5.4 %collective-permute-start.4 = (bf16[16,2048]{1,0:T(8,128)(2,1)S(1)}, bf16[16,2048]{1,0:T(8,128)(2,1)S(1)}, u32[]{:S(2)}, u32[]{:S(2)}) collective-permute-start(bf16[16,2048]{1,0:T(8,128)(2,1)S(1)} %stack.1.refs_1_.refs_0_), channel_id=1, source_target_pairs={{8,0},{12,4},{0,8},{4,12},{9,1},{13,5},{1,9},{5,13},{10,2},{14,6},... | collective-permute-start | bytes 196616 | tf_op jit(solution)/shard_map/ppermute | solution.py:24
  13.0 4.1 %collective-permute-start.5 = (bf16[16,2048]{1,0:T(8,128)(2,1)S(1)}, bf16[16,2048]{1,0:T(8,128)(2,1)S(1)}, u32[]{:S(2)}, u32[]{:S(2)}) collective-permute-start(bf16[16,2048]{1,0:T(8,128)(2,1)S(1)} %stack.1.refs_1_.refs_0_), channel_id=1, source_target_pairs={{12,0},{8,4},{4,8},{0,12},{13,1},{9,5},{5,9},{1,13},{14,2},{10,6},... | collective-permute-start | bytes 196616 | tf_op jit(solution)/shard_map/ppermute | solution.py:24
  17.1 16.9 %copy-start = (s32[4,2]{0,1:T(2,128)S(1)}, s32[4,2]{0,1:T(2,128)}, u32[]{:S(2)}) copy-start(s32[4,2]{0,1:T(2,128)} %param.8) | copy-start | bytes 100
  17.1 17.0 %copy-start.1 = (s32[4,2]{0,1:T(2,128)S(1)}, s32[4,2]{0,1:T(2,128)}, u32[]{:S(2)}) copy-start(s32[4,2]{0,1:T(2,128)} %param.9) | copy-start | bytes 100
  23.0 5.2 %collective-permute-start.6 = (bf16[16,2048]{1,0:T(8,128)(2,1)S(1)}, bf16[16,2048]{1,0:T(8,128)(2,1)S(1)}, u32[]{:S(2)}, u32[]{:S(2)}) collective-permute-start(bf16[16,2048]{1,0:T(8,128)(2,1)S(1)} %get-tuple-element.18), channel_id=1, source_target_pairs={{0,1},{1,0},{2,3},{3,2},{4,5},{5,4},{6,7},{7,6},{8,9},{9,8},{10,11... | collective-permute-start | bytes 196616 | tf_op jit(solution)/shard_map/ppermute | solution.py:29
  23.1 8.6 %collective-permute-start.7 = (bf16[16,2048]{1,0:T(8,128)(2,1)S(1)}, bf16[16,2048]{1,0:T(8,128)(2,1)S(1)}, u32[]{:S(2)}, u32[]{:S(2)}) collective-permute-start(bf16[16,2048]{1,0:T(8,128)(2,1)S(1)} %get-tuple-element.19), channel_id=1, source_target_pairs={{0,2},{1,3},{2,0},{3,1},{4,6},{5,7},{6,4},{7,5},{8,10},{9,11},{10,... | collective-permute-start | bytes 196616 | tf_op jit(solution)/shard_map/ppermute | solution.py:29
  25.3 6.4 %collective-permute-start.8 = (bf16[16,2048]{1,0:T(8,128)(2,1)S(1)}, bf16[16,2048]{1,0:T(8,128)(2,1)S(1)}, u32[]{:S(2)}, u32[]{:S(2)}) collective-permute-start(bf16[16,2048]{1,0:T(8,128)(2,1)S(1)} %get-tuple-element.20), channel_id=1, source_target_pairs={{0,3},{1,2},{2,1},{3,0},{4,7},{5,6},{6,5},{7,4},{8,11},{9,10},{10,... | collective-permute-start | bytes 196616 | tf_op jit(solution)/shard_map/ppermute | solution.py:29
  31.8 3.8 %collective-permute-start.10 = (bf16[4,2048]{1,0:T(4,128)(2,1)S(1)}, bf16[4,2048]{1,0:T(4,128)(2,1)S(1)}, u32[]{:S(2)}, u32[]{:S(2)}) collective-permute-start(bf16[4,2048]{1,0:T(4,128)(2,1)S(1)} %get-tuple-element.23), channel_id=1, source_target_pairs={{0,8},{4,12},{8,0},{12,4},{1,9},{5,13},{9,1},{13,5},{2,10},{6,14},... | collective-permute-start | bytes 49160 | tf_op jit(solution)/shard_map/ppermute | solution.py:29
  33.2 3.2 %collective-permute-start.11 = (bf16[4,2048]{1,0:T(4,128)(2,1)S(1)}, bf16[4,2048]{1,0:T(4,128)(2,1)S(1)}, u32[]{:S(2)}, u32[]{:S(2)}) collective-permute-start(bf16[4,2048]{1,0:T(4,128)(2,1)S(1)} %get-tuple-element.24), channel_id=1, source_target_pairs={{0,12},{4,8},{8,4},{12,0},{1,13},{5,9},{9,5},{13,1},{2,14},{6,10},... | collective-permute-start | bytes 49160 | tf_op jit(solution)/shard_map/ppermute | solution.py:29
  33.2 3.2 %collective-permute-start.9 = (bf16[4,2048]{1,0:T(4,128)(2,1)S(1)}, bf16[4,2048]{1,0:T(4,128)(2,1)S(1)}, u32[]{:S(2)}, u32[]{:S(2)}) collective-permute-start(bf16[4,2048]{1,0:T(4,128)(2,1)S(1)} %get-tuple-element.22), channel_id=1, source_target_pairs={{0,4},{4,0},{8,12},{12,8},{1,5},{5,1},{9,13},{13,9},{2,6},{6,2},{1... | collective-permute-start | bytes 49160 | tf_op jit(solution)/shard_map/ppermute | solution.py:29

commit v3 on v2

--- a/solution.py
+++ b/solution.py
@@ -1,4 +1,5 @@
 import functools
+import math
 
 import jax
 import jax.numpy as jnp
@@ -7,6 +8,7 @@
 from jax.experimental.pallas import tpu as pltpu
 from jax.sharding import PartitionSpec as P
 
+ROWS = 128
 VMEM = pl.BlockSpec(memory_space=pltpu.VMEM)
 ANY = pl.BlockSpec(memory_space=pl.ANY)
 
@@ -47,17 +49,13 @@
     )(*blocks)
 
 
-def prefetch_kernel(chunks, with_rows, *refs):
-    sems, dst = refs[-1], refs[-2 - with_rows]
-    depth = dst.shape[0] // chunks
+def prefetch_kernel(cuts, *refs):
+    sems, dsts = refs[-1], refs[-1 - len(cuts) : -1]
     copies = []
-    if with_rows:
-        copies.append(pltpu.make_async_copy(refs[1], refs[-2], sems.at[chunks]))
-    for c in range(chunks):
-        rows = pl.ds(c * depth, depth)
-        copies.append(pltpu.make_async_copy(refs[0].at[0, rows, :], dst.at[rows, :], sems.at[c]))
-    for copy in copies:
-        copy.start()
+    for i, (cut, dst) in enumerate(zip(cuts, dsts, strict=True)):
+        src = refs[i] if cut is None else refs[i].at[0, pl.ds(cut, dst.shape[0]), :]
+        copies.append(pltpu.make_async_copy(src, dst, sems.at[i]))
+        copies[i].start()
     for copy in copies:
         copy.wait()
 
@@ -70,70 +68,87 @@
     return pltpu.with_memory_space_constraint(w, pltpu.VMEM)
 
 
-def prefetch(w, rows=None, after=None):
-    chunks = 4 if w.shape[1] % 512 == 0 else 1
-    more = [x for x in (rows, after) if x is not None]
-    out_shape = [pltpu.VMEM(w.shape[1:], w.dtype)]
-    if rows is not None:
-        out_shape.append(pltpu.VMEM(rows.shape, rows.dtype))
-        more = [in_hbm(rows)]
-    return pl.pallas_call(
-        functools.partial(prefetch_kernel, chunks, rows is not None),
+def halves(w):
+    rows = w.shape[1] // 2
+    return (w, 0, rows), (w, rows, rows)
+
+
+def prefetch(*pieces, after=None):
+    arrays, cuts, out_shape = [], [], []
+    for w, first, rows in pieces:
+        arrays.append(in_hbm(w))
+        cuts.append(first)
+        out_shape.append(pltpu.VMEM(w.shape if first is None else (rows, w.shape[2]), w.dtype))
+    if after is not None:
+        arrays.append(after)
+    moved = sum(2 * math.prod(o.shape) * o.dtype.itemsize for o in out_shape)
+    return pl.pallas_call(
+        functools.partial(prefetch_kernel, tuple(cuts)),
         name="prefetch",
         compiler_params=pltpu.CompilerParams(vmem_limit_bytes=1 << 20),
-        cost_estimate=pl.CostEstimate(flops=0, transcendentals=0, bytes_accessed=w.size * 4),
+        cost_estimate=pl.CostEstimate(flops=0, transcendentals=0, bytes_accessed=moved),
         out_shape=out_shape,
-        in_specs=[ANY] * (1 + len(more)),
-        out_specs=[VMEM] * len(out_shape),
-        scratch_shapes=[pltpu.SemaphoreType.DMA((chunks + 1,))],
-    )(in_hbm(w), *more)
-
-
-def ffn_kernel(n_e, n_b, count, chunks, *refs):
-    xs = refs[:n_e]
-    gate_w, up_w, down_hbm = refs[n_e : n_e + 3]
-    outs = refs[n_e + 3 : n_e + 3 + n_b]
-    down_w, sems = refs[n_e + 3 + n_b :]
-    inner = down_w.shape[0] // chunks
+        in_specs=[ANY] * len(arrays),
+        out_specs=[VMEM] * len(pieces),
+        scratch_shapes=[pltpu.SemaphoreType.DMA((len(pieces),))],
+    )(*arrays)
+
+
+def product(x, pieces):
+    total, first = None, 0
+    for w in pieces:
+        part = jnp.dot(x[:, first : first + w.shape[0]], w[...], preferred_element_type=jnp.float32)
+        total = part if total is None else total + part
+        first += w.shape[0]
+    return total
+
+
+def ffn_kernel(n_e, n_b, count, held, cuts, *refs):
+    xs, refs = refs[:n_e], refs[n_e:]
+    loaded, refs = refs[: sum(held)], refs[sum(held) :]
+    sources, refs = refs[: len(cuts)], refs[len(cuts) :]
+    outs, refs = refs[:n_b], refs[n_b:]
+    rest, sems = refs[:-1], refs[-1]
     copies = []
-    for c in range(chunks):
-        rows = pl.ds(c * inner, inner)
-        copies.append(pltpu.make_async_copy(down_hbm.at[0, rows, :], down_w.at[rows, :], sems.at[c]))
-        copies[c].start()
+    for i, (cut, src, dst) in enumerate(zip(cuts, sources, rest, strict=True)):
+        copies.append(pltpu.make_async_copy(src.at[0, pl.ds(cut, dst.shape[0]), :], dst, sems.at[i]))
+        copies[i].start()
+    gate_w, up_w, down_w = loaded[: held[0]], loaded[held[0] : held[0] + held[1]], loaded[held[0] + held[1] :]
     x = jnp.concatenate([r[...] for r in xs], axis=0)
-    total = None
-    for c in range(chunks):
-        cut = slice(c * inner, (c + 1) * inner)
-        v = jnp.dot(x, gate_w[:, cut], preferred_element_type=jnp.float32)
-        u = jnp.dot(x, up_w[:, cut], preferred_element_type=jnp.float32)
-        hidden = (v / (1.0 + jnp.exp(-v)) * u).astype(jnp.bfloat16)
-        copies[c].wait()
-        part = jnp.dot(hidden, down_w[cut, :], preferred_element_type=jnp.float32)
-        total = part if c == 0 else total + part
+    rows = x.shape[0]
+    spare = -rows % ROWS
+    if spare:
+        x = jnp.concatenate([x, jnp.zeros((spare, x.shape[1]), x.dtype)], axis=0)
+    v, u = product(x, gate_w), product(x, up_w)
+    hidden = (v / (1.0 + jnp.exp(-v)) * u).astype(jnp.bfloat16)
+    total = product(hidden, down_w) if down_w else 0.0
+    first = sum(w.shape[0] for w in down_w)
+    for copy, w in zip(copies, rest, strict=True):
+        copy.wait()
+        total = total + product(hidden[:, first : first + w.shape[0]], [w])
+        first += w.shape[0]
     for d, out in enumerate(outs):
-        rows = [total[(m * n_b + d) * count : (m * n_b + d + 1) * count] for m in range(n_e)]
-        out[...] = jnp.concatenate(rows, axis=0).astype(out.dtype)
-
-
-def ffn(xs, w_gate, w_up, w_down, n_b, count):
+        part = [total[(m * n_b + d) * count : (m * n_b + d + 1) * count] for m in range(n_e)]
+        out[...] = jnp.concatenate(part, axis=0).astype(out.dtype)
+
+
+def ffn(xs, gate_w, up_w, down_w, rest, n_b, count):
     n_e, width = len(xs), xs[0].shape[1]
-    hidden = w_gate.shape[1]
-    chunks = 4 if hidden % 512 == 0 else 1
     out_shape = [
         jax.ShapeDtypeStruct((n_e * count, width), jnp.float32 if d == 0 else jnp.bfloat16) for d in range(n_b)
     ]
-    return pl.pallas_call(
-        functools.partial(ffn_kernel, n_e, n_b, count, chunks),
+    loaded = [in_vmem(w) for w in (*gate_w, *up_w, *down_w)]
+    held = (len(gate_w), len(up_w), len(down_w))
+    return pl.pallas_call(
+        functools.partial(ffn_kernel, n_e, n_b, count, held, tuple(first for _, first, _ in rest)),
         name="ffn",
-        compiler_params=pltpu.CompilerParams(vmem_limit_bytes=16 << 20),
+        compiler_params=pltpu.CompilerParams(vmem_limit_bytes=20 << 20),
         out_shape=out_shape,
-        in_specs=[VMEM] * (n_e + 2) + [ANY],
+        in_specs=[VMEM] * (n_e + len(loaded)) + [ANY] * len(rest),
         out_specs=[VMEM] * n_b,
-        scratch_shapes=[
-            pltpu.VMEM(w_down.shape[1:], w_down.dtype),
-            pltpu.SemaphoreType.DMA((chunks,)),
-        ],
-    )(*xs, in_vmem(w_gate), in_vmem(w_up), in_hbm(w_down))
+        scratch_shapes=[pltpu.VMEM((rows, w.shape[2]), w.dtype) for w, _, rows in rest]
+        + [pltpu.SemaphoreType.DMA((max(len(rest), 1),))],
+    )(*xs, *loaded, *[in_hbm(w) for w, _, _ in rest])
 
 
 def merge_kernel(n_b, *refs):
@@ -187,11 +202,11 @@
     count = tokens.shape[0]
     n_e, n_b = lax.axis_size("expert"), lax.axis_size("blk")
     others = [fetch(tokens, "blk", d) for d in range(1, n_b)]
-    gate_w, own = prefetch(w_gate, rows=tokens)
+    gate_a, gate_b, up_a, own = prefetch(*halves(w_gate), halves(w_up)[0], (tokens, None, 0))
     mine = stack([own] + others)
-    (up_w,) = prefetch(w_up, after=mine)
+    up_b, down_a = prefetch(halves(w_up)[1], halves(w_down)[0], after=mine)
     xs = [mine] + [fetch(mine, "expert", m) for m in range(1, n_e)]
-    parts = ffn(xs, gate_w, up_w, w_down, n_b, count)
+    parts = ffn(xs, [gate_a, gate_b], [up_a, up_b], [down_a], halves(w_down)[1:], n_b, count)
     parts = [parts[0]] + [deliver(parts[d], "blk", d) for d in range(1, n_b)]
     blocks = merge(parts, n_e)
     blocks = [blocks[0]] + [deliver(blocks[m], "expert", m) for m in range(1, n_e)]

time: 37.4 us -> 35.9 us (0.960)
  Pallas kernels: 13.8 us -> 12.8 us
  waiting for transfers between devices: 8.91 us -> 8.45 us
    ppermute x6, waiting for transfers between devices: 2.43 us -> 1.29 us  [fetch(): return lax.ppermute(x, axis, [(peer(i, d, n), i) for i in range(n)])]
    pallas_call x3, Pallas kernels: 12.9 us -> 12 us  [the longest x2 8.18 us: prefetch(): pl.pallas_call(functools.partial(prefetch_kernel, tuple(cuts)), name='pre...]
    ppermute x6, waiting for transfers between devices: 6.48 us -> 7.17 us  [deliver(): return lax.ppermute(x, axis, [(i, peer(i, d, n)) for i in range(n)])]
  transfers between devices with their start and end apart: 12 -> 12, of which waited for: 6 -> 7; matrix products, arithmetic and copies ran while one was open for 0% -> 1% of each run, Pallas kernels for 19% -> 23%
where the time goes in v3:
time: 35.9 us; the launch traced here: 35.8 us
  starting transfers between devices  14.2 us (40%)
  Pallas kernels  12.8 us (36%)
  waiting for transfers between devices  8.45 us (24%)
    pallas_call x2, Pallas kernels, prefetch(): pl.pallas_call(functools.partial(prefetch_kernel, tuple(cuts)), name='pre...  8.18 us
    ppermute x6, starting transfers between devices, fetch(): return lax.ppermute(x, axis, [(peer(i, d, n), i) for i in range(n)])  7.56 us
    ppermute x6, waiting for transfers between devices, deliver(): return lax.ppermute(x, axis, [(i, peer(i, d, n)) for i in range(n)])  7.17 us
    ppermute x6, starting transfers between devices, deliver(): return lax.ppermute(x, axis, [(i, peer(i, d, n)) for i in range(n)])  6.65 us
    pallas_call x1, Pallas kernels, ffn(): pl.pallas_call(functools.partial(ffn_kernel, n_e, n_b, count, held, tuple...  3.82 us
    ppermute x6, waiting for transfers between devices, fetch(): return lax.ppermute(x, axis, [(peer(i, d, n), i) for i in range(n)])  1.29 us
    pallas_call x1, Pallas kernels, mix(): pl.pallas_call(functools.partial(mix_kernel, len(blocks)), name='mix', co...  0.79 us
  transfers between devices with their start and end apart: 12, of which 7 were waited for; matrix products, arithmetic and copies ran while one was open for 1% of the time, Pallas kernels for 23%

profile of v3, /device:TPU:0, one launch (start us, length us, event | category | flops | bytes accessed | tf_op | source)
XLA Modules:
  0.0 35.8 jit_solution(14792427306445098207)
XLA Ops:
  0.0 3.1 %collective-permute-start = (bf16[4,2048]{1,0:T(4,128)(2,1)}, bf16[4,2048]{1,0:T(4,128)(2,1)S(1)}, u32[]{:S(2)}, u32[]{:S(2)}) collective-permute-start(bf16[4,2048]{1,0:T(4,128)(2,1)} %refs_3_.1), channel_id=1, source_target_pairs={{1,0},{0,1},{3,2},{2,3},{5,4},{4,5},{7,6},{6,7},{9,8},{8,9},{11,10... | collective-permute-start | bytes 49160 | tf_op jit(solution)/shard_map/ppermute | solution.py:26
  3.1 2.6 %collective-permute-start.1 = (bf16[4,2048]{1,0:T(4,128)(2,1)}, bf16[4,2048]{1,0:T(4,128)(2,1)S(1)}, u32[]{:S(2)}, u32[]{:S(2)}) collective-permute-start(bf16[4,2048]{1,0:T(4,128)(2,1)} %refs_3_.1), channel_id=1, source_target_pairs={{2,0},{3,1},{0,2},{1,3},{6,4},{7,5},{4,6},{5,7},{10,8},{11,9},{8,1... | collective-permute-start | bytes 49160 | tf_op jit(solution)/shard_map/ppermute | solution.py:26
  5.6 0.0 collective-permute-start.2
  5.6 4.7 %prefetch.2 = (bf16[1024,2048]{1,0:T(8,128)(2,1)S(1)}, bf16[1024,2048]{1,0:T(8,128)(2,1)S(1)}, bf16[1024,2048]{1,0:T(8,128)(2,1)S(1)}, bf16[4,2048]{1,0:T(4,128)(2,1)S(1)}) custom-call(bf16[1,2048,2048]{2,1,0:T(8,128)(2,1)} %refs_1_.2, bf16[1,2048,2048]{2,1,0:T(8,128)(2,1)} %refs_1_.2, bf16[1,2048,2048]{2,1,0:T(8,128)(2,1)} %refs_0_.3, bf16[4,2048]{1,0:T(4,128)(2,1)} %refs_3_.1), custom_call_target="tpu_custom_call" | custom-call | bytes 25198592 | tf_op jit(solution)/shard_map/prefetch/pallas_call | solution.py:85
  10.4 1.0 %collective-permute-done.2.refs_3_ = bf16[4,2048]{1,0:T(4,128)(2,1)S(1)} collective-permute-done((bf16[4,2048]{1,0:T(4,128)(2,1)}, bf16[4,2048]{1,0:T(4,128)(2,1)S(1)}, u32[]{:S(2)}, u32[]{:S(2)}) %collective-permute-start.2) | collective-permute-done | bytes 16416 | tf_op jit(solution)/shard_map/ppermute | solution.py:26
  11.4 0.1 collective-permute-start.3
  11.5 1.6 %collective-permute-start.4 = (bf16[16,2048]{1,0:T(8,128)(2,1)S(1)}, bf16[16,2048]{1,0:T(8,128)(2,1)S(1)}, u32[]{:S(2)}, u32[]{:S(2)}) collective-permute-start(bf16[16,2048]{1,0:T(8,128)(2,1)S(1)} %stack.1.refs_2_.refs_0_), channel_id=1, source_target_pairs={{8,0},{12,4},{0,8},{4,12},{9,1},{13,5},{1,9},{5,13},{10,2},{14,6},... | collective-permute-start | bytes 196616 | tf_op jit(solution)/shard_map/ppermute | solution.py:26
  13.0 0.3 collective-permute-start.5
  13.3 3.5 %prefetch.3 = (bf16[1024,2048]{1,0:T(8,128)(2,1)S(1)}, bf16[1024,2048]{1,0:T(8,128)(2,1)S(1)}) custom-call(bf16[1,2048,2048]{2,1,0:T(8,128)(2,1)} %refs_0_.3, bf16[1,2048,2048]{2,1,0:T(8,128)(2,1)} %refs_9_.1, bf16[16,2048]{1,0:T(8,128)(2,1)S(1)} %stack.1.refs_2_.refs_0_), custom_call_target="tpu_custom_call" | custom-call | bytes 16777216 | tf_op jit(solution)/shard_map/prefetch/pallas_call | solution.py:85
  16.9 0.3 collective-permute-done.5.refs_3_
  17.1 3.8 %ffn.1 = (f32[16,2048]{1,0:T(8,128)S(1)}, bf16[16,2048]{1,0:T(8,128)(2,1)S(1)}, bf16[16,2048]{1,0:T(8,128)(2,1)S(1)}, bf16[16,2048]{1,0:T(8,128)(2,1)S(1)}) custom-call(bf16[16,2048]{1,0:T(8,128)(2,1)S(1)} %stack.1.refs_2_.refs_0_, bf16[16,2048]{1,0:T(8,128)(2,1)S(1)} %collective-permute-done.3.refs_1_, bf16[16,2048]{1,0:T(8,128)(2,1)S(1)} %collective-permute-done.4.refs_2_, ...), custom_call_target="tpu_custom_call" | custom-call | tf_op jit(solution)/shard_map/ffn/pallas_call | solution.py:142
  20.9 0.1 collective-permute-start.6
  21.0 3.4 %collective-permute-start.7 = (bf16[16,2048]{1,0:T(8,128)(2,1)S(1)}, bf16[16,2048]{1,0:T(8,128)(2,1)S(1)}, u32[]{:S(2)}, u32[]{:S(2)}) collective-permute-start(bf16[16,2048]{1,0:T(8,128)(2,1)S(1)} %get-tuple-element.27), channel_id=1, source_target_pairs={{0,2},{1,3},{2,0},{3,1},{4,6},{5,7},{6,4},{7,5},{8,10},{9,11},{10,... | collective-permute-start | bytes 196616 | tf_op jit(solution)/shard_map/ppermute | solution.py:31
  24.4 1.0 %collective-permute-start.8 = (bf16[16,2048]{1,0:T(8,128)(2,1)S(1)}, bf16[16,2048]{1,0:T(8,128)(2,1)S(1)}, u32[]{:S(2)}, u32[]{:S(2)}) collective-permute-start(bf16[16,2048]{1,0:T(8,128)(2,1)S(1)} %get-tuple-element.28), channel_id=1, source_target_pairs={{0,3},{1,2},{2,1},{3,0},{4,7},{5,6},{6,5},{7,4},{8,11},{9,10},{10,... | collective-permute-start | bytes 196616 | tf_op jit(solution)/shard_map/ppermute | solution.py:31
  25.4 0.6 %collective-permute-done.6.refs_1_ = bf16[16,2048]{1,0:T(8,128)(2,1)S(1)} collective-permute-done((bf16[16,2048]{1,0:T(8,128)(2,1)S(1)}, bf16[16,2048]{1,0:T(8,128)(2,1)S(1)}, u32[]{:S(2)}, u32[]{:S(2)}) %collective-permute-start.6) | collective-permute-done | bytes 65568 | tf_op jit(solution)/shard_map/ppermute | solution.py:31
  26.0 2.5 %collective-permute-done.7.refs_2_ = bf16[16,2048]{1,0:T(8,128)(2,1)S(1)} collective-permute-done((bf16[16,2048]{1,0:T(8,128)(2,1)S(1)}, bf16[16,2048]{1,0:T(8,128)(2,1)S(1)}, u32[]{:S(2)}, u32[]{:S(2)}) %collective-permute-start.7) | collective-permute-done | bytes 65568 | tf_op jit(solution)/shard_map/ppermute | solution.py:31
  28.5 2.1 %collective-permute-done.8.refs_3_ = bf16[16,2048]{1,0:T(8,128)(2,1)S(1)} collective-permute-done((bf16[16,2048]{1,0:T(8,128)(2,1)S(1)}, bf16[16,2048]{1,0:T(8,128)(2,1)S(1)}, u32[]{:S(2)}, u32[]{:S(2)}) %collective-permute-start.8) | collective-permute-done | bytes 65568 | tf_op jit(solution)/shard_map/ppermute | solution.py:31
  30.6 1.2 %collective-permute-start.10 = (bf16[4,2048]{1,0:T(4,128)(2,1)S(1)}, bf16[4,2048]{1,0:T(4,128)(2,1)S(1)}, u32[]{:S(2)}, u32[]{:S(2)}) collective-permute-start(bf16[4,2048]{1,0:T(4,128)(2,1)S(1)} %get-tuple-element.31), channel_id=1, source_target_pairs={{0,8},{4,12},{8,0},{12,4},{1,9},{5,13},{9,1},{13,5},{2,10},{6,14},... | collective-permute-start | bytes 49160 | tf_op jit(solution)/shard_map/ppermute | solution.py:31
  31.8 1.0 %collective-permute-start.9 = (bf16[4,2048]{1,0:T(4,128)(2,1)S(1)}, bf16[4,2048]{1,0:T(4,128)(2,1)S(1)}, u32[]{:S(2)}, u32[]{:S(2)}) collective-permute-start(bf16[4,2048]{1,0:T(4,128)(2,1)S(1)} %get-tuple-element.30), channel_id=1, source_target_pairs={{0,4},{4,0},{8,12},{12,8},{1,5},{5,1},{9,13},{13,9},{2,6},{6,2},{1... | collective-permute-start | bytes 49160 | tf_op jit(solution)/shard_map/ppermute | solution.py:31
  32.8 0.1 copy.7.ids_ref
  32.9 0.1 copy.8.fixed_ref
  33.0 1.4 %collective-permute-done.10.refs_2_ = bf16[4,2048]{1,0:T(4,128)(2,1)S(1)} collective-permute-done((bf16[4,2048]{1,0:T(4,128)(2,1)S(1)}, bf16[4,2048]{1,0:T(4,128)(2,1)S(1)}, u32[]{:S(2)}, u32[]{:S(2)}) %collective-permute-start.10) | collective-permute-done | bytes 16416 | tf_op jit(solution)/shard_map/ppermute | solution.py:31
  34.4 0.6 %collective-permute-done.11.refs_3_ = bf16[4,2048]{1,0:T(4,128)(2,1)S(1)} collective-permute-done((bf16[4,2048]{1,0:T(4,128)(2,1)S(1)}, bf16[4,2048]{1,0:T(4,128)(2,1)S(1)}, u32[]{:S(2)}, u32[]{:S(2)}) %collective-permute-start.11) | collective-permute-done | bytes 16416 | tf_op jit(solution)/shard_map/ppermute | solution.py:31
  35.0 0.8 %mix.1 = bf16[4,2048]{1,0:T(4,128)(2,1)} custom-call(s32[4,2]{1,0:T(4,128)S(1)} %copy.7.ids_ref, s32[4,2]{1,0:T(4,128)S(1)} %copy.8.fixed_ref, bf16[4,2048]{1,0:T(4,128)(2,1)S(1)} %get-tuple-element.29.refs_0_, bf16[4,2048]{1,0:T(4,128)(2,1)S(1)} %collective-permute-done.9.refs_1_, bf16[4,2048]{1,0:T(4,128)(2,1)S(1)} %collective-permute-done.10.refs_2_, ...), custom_call_target="tpu_custom_call" | custom-call | tf_op jit(solution)/shard_map/mix/pallas_call | solution.py:191
  (12 shorter events, 0.1 us)
Async XLA Ops:
  0.0 10.4 %collective-permute-start = (bf16[4,2048]{1,0:T(4,128)(2,1)}, bf16[4,2048]{1,0:T(4,128)(2,1)S(1)}, u32[]{:S(2)}, u32[]{:S(2)}) collective-permute-start(bf16[4,2048]{1,0:T(4,128)(2,1)} %refs_3_.1), channel_id=1, source_target_pairs={{1,0},{0,1},{3,2},{2,3},{5,4},{4,5},{7,6},{6,7},{9,8},{8,9},{11,10... | collective-permute-start | bytes 49160 | tf_op jit(solution)/shard_map/ppermute | solution.py:26
  3.1 7.3 %collective-permute-start.1 = (bf16[4,2048]{1,0:T(4,128)(2,1)}, bf16[4,2048]{1,0:T(4,128)(2,1)S(1)}, u32[]{:S(2)}, u32[]{:S(2)}) collective-permute-start(bf16[4,2048]{1,0:T(4,128)(2,1)} %refs_3_.1), channel_id=1, source_target_pairs={{2,0},{3,1},{0,2},{1,3},{6,4},{7,5},{4,6},{5,7},{10,8},{11,9},{8,1... | collective-permute-start | bytes 49160 | tf_op jit(solution)/shard_map/ppermute | solution.py:26
  5.6 5.7 %collective-permute-start.2 = (bf16[4,2048]{1,0:T(4,128)(2,1)}, bf16[4,2048]{1,0:T(4,128)(2,1)S(1)}, u32[]{:S(2)}, u32[]{:S(2)}) collective-permute-start(bf16[4,2048]{1,0:T(4,128)(2,1)} %refs_3_.1), channel_id=1, source_target_pairs={{3,0},{2,1},{1,2},{0,3},{7,4},{6,5},{5,6},{4,7},{11,8},{10,9},{9,1... | collective-permute-start | bytes 49160 | tf_op jit(solution)/shard_map/ppermute | solution.py:26
  11.4 5.4 %collective-permute-start.3 = (bf16[16,2048]{1,0:T(8,128)(2,1)S(1)}, bf16[16,2048]{1,0:T(8,128)(2,1)S(1)}, u32[]{:S(2)}, u32[]{:S(2)}) collective-permute-start(bf16[16,2048]{1,0:T(8,128)(2,1)S(1)} %stack.1.refs_2_.refs_0_), channel_id=1, source_target_pairs={{4,0},{0,4},{12,8},{8,12},{5,1},{1,5},{13,9},{9,13},{6,2},{2,6},{1... | collective-permute-start | bytes 196616 | tf_op jit(solution)/shard_map/ppermute | solution.py:26
  11.5 5.4 %collective-permute-start.4 = (bf16[16,2048]{1,0:T(8,128)(2,1)S(1)}, bf16[16,2048]{1,0:T(8,128)(2,1)S(1)}, u32[]{:S(2)}, u32[]{:S(2)}) collective-permute-start(bf16[16,2048]{1,0:T(8,128)(2,1)S(1)} %stack.1.refs_2_.refs_0_), channel_id=1, source_target_pairs={{8,0},{12,4},{0,8},{4,12},{9,1},{13,5},{1,9},{5,13},{10,2},{14,6},... | collective-permute-start | bytes 196616 | tf_op jit(solution)/shard_map/ppermute | solution.py:26
  13.0 4.1 %collective-permute-start.5 = (bf16[16,2048]{1,0:T(8,128)(2,1)S(1)}, bf16[16,2048]{1,0:T(8,128)(2,1)S(1)}, u32[]{:S(2)}, u32[]{:S(2)}) collective-permute-start(bf16[16,2048]{1,0:T(8,128)(2,1)S(1)} %stack.1.refs_2_.refs_0_), channel_id=1, source_target_pairs={{12,0},{8,4},{4,8},{0,12},{13,1},{9,5},{5,9},{1,13},{14,2},{10,6},... | collective-permute-start | bytes 196616 | tf_op jit(solution)/shard_map/ppermute | solution.py:26
  17.1 15.7 %copy-start = (s32[4,2]{0,1:T(2,128)S(1)}, s32[4,2]{0,1:T(2,128)}, u32[]{:S(2)}) copy-start(s32[4,2]{0,1:T(2,128)} %param.8) | copy-start | bytes 100
  17.1 15.8 %copy-start.1 = (s32[4,2]{0,1:T(2,128)S(1)}, s32[4,2]{0,1:T(2,128)}, u32[]{:S(2)}) copy-start(s32[4,2]{0,1:T(2,128)} %param.9) | copy-start | bytes 100
  20.9 5.1 %collective-permute-start.6 = (bf16[16,2048]{1,0:T(8,128)(2,1)S(1)}, bf16[16,2048]{1,0:T(8,128)(2,1)S(1)}, u32[]{:S(2)}, u32[]{:S(2)}) collective-permute-start(bf16[16,2048]{1,0:T(8,128)(2,1)S(1)} %get-tuple-element.26), channel_id=1, source_target_pairs={{0,1},{1,0},{2,3},{3,2},{4,5},{5,4},{6,7},{7,6},{8,9},{9,8},{10,11... | collective-permute-start | bytes 196616 | tf_op jit(solution)/shard_map/ppermute | solution.py:31
  21.0 7.5 %collective-permute-start.7 = (bf16[16,2048]{1,0:T(8,128)(2,1)S(1)}, bf16[16,2048]{1,0:T(8,128)(2,1)S(1)}, u32[]{:S(2)}, u32[]{:S(2)}) collective-permute-start(bf16[16,2048]{1,0:T(8,128)(2,1)S(1)} %get-tuple-element.27), channel_id=1, source_target_pairs={{0,2},{1,3},{2,0},{3,1},{4,6},{5,7},{6,4},{7,5},{8,10},{9,11},{10,... | collective-permute-start | bytes 196616 | tf_op jit(solution)/shard_map/ppermute | solution.py:31
  24.4 6.2 %collective-permute-start.8 = (bf16[16,2048]{1,0:T(8,128)(2,1)S(1)}, bf16[16,2048]{1,0:T(8,128)(2,1)S(1)}, u32[]{:S(2)}, u32[]{:S(2)}) collective-permute-start(bf16[16,2048]{1,0:T(8,128)(2,1)S(1)} %get-tuple-element.28), channel_id=1, source_target_pairs={{0,3},{1,2},{2,1},{3,0},{4,7},{5,6},{6,5},{7,4},{8,11},{9,10},{10,... | collective-permute-start | bytes 196616 | tf_op jit(solution)/shard_map/ppermute | solution.py:31
  30.6 3.8 %collective-permute-start.10 = (bf16[4,2048]{1,0:T(4,128)(2,1)S(1)}, bf16[4,2048]{1,0:T(4,128)(2,1)S(1)}, u32[]{:S(2)}, u32[]{:S(2)}) collective-permute-start(bf16[4,2048]{1,0:T(4,128)(2,1)S(1)} %get-tuple-element.31), channel_id=1, source_target_pairs={{0,8},{4,12},{8,0},{12,4},{1,9},{5,13},{9,1},{13,5},{2,10},{6,14},... | collective-permute-start | bytes 49160 | tf_op jit(solution)/shard_map/ppermute | solution.py:31
  31.8 3.2 %collective-permute-start.11 = (bf16[4,2048]{1,0:T(4,128)(2,1)S(1)}, bf16[4,2048]{1,0:T(4,128)(2,1)S(1)}, u32[]{:S(2)}, u32[]{:S(2)}) collective-permute-start(bf16[4,2048]{1,0:T(4,128)(2,1)S(1)} %get-tuple-element.32), channel_id=1, source_target_pairs={{0,12},{4,8},{8,4},{12,0},{1,13},{5,9},{9,5},{13,1},{2,14},{6,10},... | collective-permute-start | bytes 49160 | tf_op jit(solution)/shard_map/ppermute | solution.py:31
  31.8 3.2 %collective-permute-start.9 = (bf16[4,2048]{1,0:T(4,128)(2,1)S(1)}, bf16[4,2048]{1,0:T(4,128)(2,1)S(1)}, u32[]{:S(2)}, u32[]{:S(2)}) collective-permute-start(bf16[4,2048]{1,0:T(4,128)(2,1)S(1)} %get-tuple-element.30), channel_id=1, source_target_pairs={{0,4},{4,0},{8,12},{12,8},{1,5},{5,1},{9,13},{13,9},{2,6},{6,2},{1... | collective-permute-start | bytes 49160 | tf_op jit(solution)/shard_map/ppermute | solution.py:31

commit v4 on v1

v4 whole, which is shorter than its diff:
```python
import functools

import jax
import jax.numpy as jnp
from jax import lax
from jax.experimental import pallas as pl
from jax.experimental.pallas import tpu as pltpu
from jax.sharding import PartitionSpec as P

ROWS = 128
HINT = 2 * 10**10
VMEM = pl.BlockSpec(memory_space=pltpu.VMEM)
ANY = pl.BlockSpec(memory_space=pl.ANY)


def limit(mib):
    return pltpu.CompilerParams(vmem_limit_bytes=mib << 20)


def peer(i, d, n):
    return i ^ d if n & (n - 1) == 0 else (i + d) % n


def source(i, d, n):
    return i ^ d if n & (n - 1) == 0 else (i - d) % n


def fetch(x, axis, d):
    n = lax.axis_size(axis)
    return lax.ppermute(x, axis, [(peer(i, d, n), i) for i in range(n)])


def deliver(x, axis, d):
    n = lax.axis_size(axis)
    return lax.ppermute(x, axis, [(i, peer(i, d, n)) for i in range(n)])


def last_first(n):
    return [0, n - 1, *range(1, n - 1)]


def first_last(n):
    return [0, *range(2, n), 1]


def half_first(n):
    return [0, n // 2, *(i for i in range(1, n) if i != n // 2)]


def restored(refs, order):
    got = [None] * len(order)
    for ref, i in zip(refs, order, strict=True):
        got[i] = ref
    return got


def rows_kernel(src, dst, sem):
    copy = pltpu.make_async_copy(src, dst, sem)
    copy.start()
    copy.wait()


def on_chip(x):
    return pl.pallas_call(
        rows_kernel,
        name="rows",
        compiler_params=limit(1),
        cost_estimate=pl.CostEstimate(flops=0, transcendentals=0, bytes_accessed=4 * x.size),
        out_shape=pltpu.VMEM(x.shape, x.dtype),
        in_specs=[ANY],
        out_specs=VMEM,
        scratch_shapes=[pltpu.SemaphoreType.DMA],
    )(pltpu.with_memory_space_constraint(x, pltpu.HBM))


def stack_kernel(upper, lower, out):
    rows = [r[...].astype(jnp.float32) for r in (upper, lower)]
    out[...] = jnp.concatenate(rows, axis=0).astype(out.dtype)


def stack(upper, lower):
    rows = upper.shape[0] + lower.shape[0]
    return pl.pallas_call(
        stack_kernel,
        name="stack",
        compiler_params=limit(1 if rows * upper.shape[1] < 2**16 else 8),
        cost_estimate=pl.CostEstimate(flops=HINT, transcendentals=0, bytes_accessed=0),
        out_shape=jax.ShapeDtypeStruct((rows, upper.shape[1]), upper.dtype),
        in_specs=[VMEM] * 2,
        out_specs=VMEM,
    )(upper, lower)


def ffn_kernel(order, n_b, count, *refs):
    n_e = len(order)
    xs, (gate_w, up_w, down_w), outs = restored(refs[:n_e], order), refs[n_e : n_e + 3], refs[n_e + 3 :]
    x = jnp.concatenate([r[...] for r in xs], axis=0)
    spare = -x.shape[0] % ROWS
    if spare:
        x = jnp.concatenate([x, jnp.zeros((spare, x.shape[1]), x.dtype)], axis=0)
    v = jnp.dot(x, gate_w[0], preferred_element_type=jnp.float32)
    u = jnp.dot(x, up_w[0], preferred_element_type=jnp.float32)
    hidden = (v / (1.0 + jnp.exp(-v)) * u).astype(jnp.bfloat16)
    total = jnp.dot(hidden, down_w[0], preferred_element_type=jnp.float32)
    for d, out in enumerate(outs):
        part = [total[(m * n_b + d) * count : (m * n_b + d + 1) * count] for m in range(n_e)]
        out[...] = jnp.concatenate(part, axis=0).astype(out.dtype)


def ffn(xs, w_gate, w_up, w_down, n_b, count):
    n_e, (rows, width) = len(xs), xs[0].shape
    order = last_first(n_e)
    out_shape = [
        jax.ShapeDtypeStruct((n_e * count, width), jnp.float32 if d == 0 else jnp.bfloat16) for d in range(n_b)
    ]
    return pl.pallas_call(
        functools.partial(ffn_kernel, order, n_b, count),
        name="ffn",
        compiler_params=limit(20 if n_e * rows <= ROWS else 40),
        cost_estimate=pl.CostEstimate(
            flops=6 * n_e * rows * w_gate.size, transcendentals=0, bytes_accessed=6 * w_gate.size
        ),
        out_shape=out_shape,
        in_specs=[VMEM] * (n_e + 3),
        out_specs=[VMEM] * n_b,
    )(*[xs[i] for i in order], w_gate, w_up, w_down)


def merge_kernel(order, *refs):
    parts, outs = restored(refs[: len(order)], order), refs[len(order) :]
    total = parts[0][...]
    for r in parts[1:]:
        total = total + r[...].astype(jnp.float32)
    count = total.shape[0] // len(outs)
    for m, out in enumerate(outs):
        out[...] = total[m * count : (m + 1) * count].astype(out.dtype)


def merge(parts, n_e):
    rows, width = parts[0].shape
    order = first_last(len(parts))
    return pl.pallas_call(
        functools.partial(merge_kernel, order),
        name="merge",
        compiler_params=limit(8),
        out_shape=[jax.ShapeDtypeStruct((rows // n_e, width), jnp.bfloat16)] * n_e,
        in_specs=[VMEM] * len(parts),
        out_specs=[VMEM] * n_e,
    )(*[parts[i] for i in order])


def mix_kernel(order, ids_ref, fixed_ref, *refs):
    blocks, out, n_e = restored(refs[:-1], order), refs[-1], len(order)
    me = lax.axis_index("expert")
    ids = ids_ref[...]
    fixed = fixed_ref[...].astype(jnp.float32)
    shares = fixed / jnp.sum(fixed, axis=1, keepdims=True)
    mixed = None
    for m, block in enumerate(blocks):
        share = jnp.sum(jnp.where(ids == source(me, m, n_e), shares, 0.0), axis=1, keepdims=True)
        part = share * block[...].astype(jnp.float32)
        mixed = part if m == 0 else mixed + part
    out[...] = mixed.astype(out.dtype)


def mix(route_ids, gate_fixed, blocks):
    order = half_first(len(blocks))
    return pl.pallas_call(
        functools.partial(mix_kernel, order),
        name="mix",
        compiler_params=limit(4),
        out_shape=jax.ShapeDtypeStruct(blocks[0].shape, jnp.bfloat16),
        in_specs=[VMEM] * (2 + len(blocks)),
        out_specs=VMEM,
    )(route_ids, gate_fixed, *[blocks[i] for i in order])


def on_device(tokens, route_ids, route_slots, gate_fixed, w_gate, w_up, w_down):
    count = tokens.shape[0]
    n_e, n_b = lax.axis_size("expert"), lax.axis_size("blk")
    mine, step = tokens, 1
    while step < n_b:
        more = fetch(mine[: (n_b - step) * count], "blk", step)
        mine = stack(on_chip(mine) if step == 1 else mine, more)
        step *= 2
    xs = [mine] + [fetch(mine, "expert", m) for m in range(1, n_e)]
    parts = ffn(xs, w_gate, w_up, w_down, n_b, count)
    parts = [parts[0]] + [deliver(parts[d], "blk", d) for d in range(1, n_b)]
    blocks = merge(parts, n_e)
    blocks = [blocks[0]] + [deliver(blocks[m], "expert", m) for m in range(1, n_e)]
    return mix(route_ids, gate_fixed, blocks)


def solution(mesh):
    return jax.shard_map(
        on_device,
        mesh=mesh,
        in_specs=(
            P(("group", "expert", "blk"), None),
            P(("group", "expert", "blk"), None),
            P(("group", "expert", "blk"), None),
            P(("group", "expert", "blk"), None),
            P("expert", None, "blk"),
            P("expert", None, "blk"),
            P("expert", "blk", None),
        ),
        out_specs=P(("group", "expert", "blk"), None),
        check_vma=False,
    )
```

time: 48.2 us -> 33.8 us (0.70)
  Pallas kernels: 13.5 us -> 5.06 us
  waiting for transfers between devices: 16.8 us -> 13.4 us
  local copies, waits for them, and re-layouts: 1.88 us -> 0.23 us
  other arithmetic: 1.45 us -> 0.01 us
  starting transfers between devices: 14.1 us -> 14.7 us
    pallas_call x3 -> x6, Pallas kernels: 13.5 us -> 5.06 us  [the longest x1 3.46 us: ffn(): pl.pallas_call(functools.partial(ffn_kernel, order, n_b, count), name='ff...]
    ppermute x6 -> x5, waiting for transfers between devices: 9.6 us -> 7.11 us  [fetch(): return lax.ppermute(x, axis, [(peer(i, d, n), i) for i in range(n)])]
    unnamed x22 -> x18, local copies, waits for them, and re-layouts: 1.88 us -> 0.23 us
    convert_element_type x1 -> x0, other arithmetic: 1.41 us -> none  [on_device(): return mixed.astype(jnp.bfloat16)]
    ppermute x6, waiting for transfers between devices: 7.19 us -> 6.26 us  [deliver(): return lax.ppermute(x, axis, [(i, peer(i, d, n)) for i in range(n)])]
    ppermute x6 -> x5, starting transfers between devices: 7.5 us -> 8.35 us  [fetch(): return lax.ppermute(x, axis, [(peer(i, d, n), i) for i in range(n)])]
  transfers between devices with their start and end apart: 12 -> 11, of which waited for: 8 -> 9; matrix products, arithmetic and copies ran while one was open for 0% -> 1% of each run, Pallas kernels for 0% -> 2%
where the time goes in v4:
time: 33.8 us; the launch traced here: 33.6 us
  starting transfers between devices  14.7 us (43%)
  waiting for transfers between devices  13.4 us (40%)
  Pallas kernels  5.06 us (15%)
    ppermute x5, starting transfers between devices, fetch(): return lax.ppermute(x, axis, [(peer(i, d, n), i) for i in range(n)])  8.35 us
    ppermute x5, waiting for transfers between devices, fetch(): return lax.ppermute(x, axis, [(peer(i, d, n), i) for i in range(n)])  7.11 us
    ppermute x6, starting transfers between devices, deliver(): return lax.ppermute(x, axis, [(i, peer(i, d, n)) for i in range(n)])  6.39 us
    ppermute x6, waiting for transfers between devices, deliver(): return lax.ppermute(x, axis, [(i, peer(i, d, n)) for i in range(n)])  6.26 us
    pallas_call x1, Pallas kernels, ffn(): pl.pallas_call(functools.partial(ffn_kernel, order, n_b, count), name='ff...  3.46 us
    pallas_call x1, Pallas kernels, mix(): pl.pallas_call(functools.partial(mix_kernel, order), name='mix', compiler...  0.79 us
    pallas_call x1, Pallas kernels, on_chip(): pl.pallas_call(rows_kernel, name='rows', compiler_params=limit(1), cost_e...  0.76 us
  transfers between devices with their start and end apart: 11, of which 9 were waited for; matrix products, arithmetic and copies ran while one was open for 1% of the time, Pallas kernels for 2%

profile of v4, /device:TPU:0, one launch (start us, length us, event | category | flops | bytes accessed | tf_op | source)
XLA Modules:
  0.0 33.6 jit_solution(17009927731168944279)
XLA Ops:
  0.0 3.1 %collective-permute-start = (bf16[4,2048]{1,0:T(4,128)(2,1)}, bf16[4,2048]{1,0:T(4,128)(2,1)S(1)}, u32[]{:S(2)}, u32[]{:S(2)}) collective-permute-start(bf16[4,2048]{1,0:T(4,128)(2,1)} %src.1), channel_id=1, source_target_pairs={{1,0},{0,1},{3,2},{2,3},{5,4},{4,5},{7,6},{6,7},{9,8},{8,9},{11,10... | collective-permute-start | bytes 49160 | tf_op jit(solution)/shard_map/ppermute | solution.py:30
  3.1 0.8 %rows.1.upper = bf16[4,2048]{1,0:T(4,128)(2,1)S(1)} custom-call(bf16[4,2048]{1,0:T(4,128)(2,1)} %src.1), custom_call_target="tpu_custom_call" | custom-call | bytes 32768 | tf_op jit(solution)/shard_map/rows/pallas_call | solution.py:64
  3.8 1.2 %collective-permute-done.lower = bf16[4,2048]{1,0:T(4,128)(2,1)S(1)} collective-permute-done((bf16[4,2048]{1,0:T(4,128)(2,1)}, bf16[4,2048]{1,0:T(4,128)(2,1)S(1)}, u32[]{:S(2)}, u32[]{:S(2)}) %collective-permute-start) | collective-permute-done | bytes 16416 | tf_op jit(solution)/shard_map/ppermute | solution.py:30
  5.0 3.1 %collective-permute-start.1 = (bf16[8,2048]{1,0:T(8,128)(2,1)S(1)}, bf16[8,2048]{1,0:T(8,128)(2,1)S(1)}, u32[]{:S(2)}, u32[]{:S(2)}) collective-permute-start(bf16[8,2048]{1,0:T(8,128)(2,1)S(1)} %stack.2.upper), channel_id=1, source_target_pairs={{2,0},{3,1},{0,2},{1,3},{6,4},{7,5},{4,6},{5,7},{10,8},{11,9},{8,1... | collective-permute-start | bytes 98312 | tf_op jit(solution)/shard_map/ppermute | solution.py:30
  8.1 1.9 %collective-permute-done.1.lower = bf16[8,2048]{1,0:T(8,128)(2,1)S(1)} collective-permute-done((bf16[8,2048]{1,0:T(8,128)(2,1)S(1)}, bf16[8,2048]{1,0:T(8,128)(2,1)S(1)}, u32[]{:S(2)}, u32[]{:S(2)}) %collective-permute-start.1) | collective-permute-done | bytes 32800 | tf_op jit(solution)/shard_map/ppermute | solution.py:30
  10.1 0.1 collective-permute-start.2
  10.1 1.9 %collective-permute-start.3 = (bf16[16,2048]{1,0:T(8,128)(2,1)S(1)}, bf16[16,2048]{1,0:T(8,128)(2,1)S(1)}, u32[]{:S(2)}, u32[]{:S(2)}) collective-permute-start(bf16[16,2048]{1,0:T(8,128)(2,1)S(1)} %stack.3.refs_0_), channel_id=1, source_target_pairs={{4,0},{0,4},{12,8},{8,12},{5,1},{1,5},{13,9},{9,13},{6,2},{2,6},{1... | collective-permute-start | bytes 196616 | tf_op jit(solution)/shard_map/ppermute | solution.py:30
  12.1 0.2 collective-permute-start.4
  12.3 1.9 %collective-permute-done.2.refs_1_ = bf16[16,2048]{1,0:T(8,128)(2,1)S(1)} collective-permute-done((bf16[16,2048]{1,0:T(8,128)(2,1)S(1)}, bf16[16,2048]{1,0:T(8,128)(2,1)S(1)}, u32[]{:S(2)}, u32[]{:S(2)}) %collective-permute-start.2) | collective-permute-done | bytes 65568 | tf_op jit(solution)/shard_map/ppermute | solution.py:30
  14.1 2.2 %collective-permute-done.4.refs_3_ = bf16[16,2048]{1,0:T(8,128)(2,1)S(1)} collective-permute-done((bf16[16,2048]{1,0:T(8,128)(2,1)S(1)}, bf16[16,2048]{1,0:T(8,128)(2,1)S(1)}, u32[]{:S(2)}, u32[]{:S(2)}) %collective-permute-start.4) | collective-permute-done | bytes 65568 | tf_op jit(solution)/shard_map/ppermute | solution.py:30
  16.4 3.5 %ffn.1 = (f32[16,2048]{1,0:T(8,128)S(1)}, bf16[16,2048]{1,0:T(8,128)(2,1)S(1)}, bf16[16,2048]{1,0:T(8,128)(2,1)S(1)}, bf16[16,2048]{1,0:T(8,128)(2,1)S(1)}) custom-call(bf16[16,2048]{1,0:T(8,128)(2,1)S(1)} %stack.3.refs_0_, bf16[16,2048]{1,0:T(8,128)(2,1)S(1)} %collective-permute-done.2.refs_1_, bf16[16,2048]{1,0:T(8,128)(2,1)S(1)} %collective-permute-done.3.refs_2_, ...), custom_call_target="tpu_custom_call" | custom-call | flops 1610612736 | bytes 25165824 | tf_op jit(solution)/shard_map/ffn/pallas_call | solution.py:116
  19.9 2.7 %collective-permute-start.5 = (bf16[16,2048]{1,0:T(8,128)(2,1)S(1)}, bf16[16,2048]{1,0:T(8,128)(2,1)S(1)}, u32[]{:S(2)}, u32[]{:S(2)}) collective-permute-start(bf16[16,2048]{1,0:T(8,128)(2,1)S(1)} %get-tuple-element.14), channel_id=1, source_target_pairs={{0,2},{1,3},{2,0},{3,1},{4,6},{5,7},{6,4},{7,5},{8,10},{9,11},{10,... | collective-permute-start | bytes 196616 | tf_op jit(solution)/shard_map/ppermute | solution.py:35
  22.5 1.3 %collective-permute-start.6 = (bf16[16,2048]{1,0:T(8,128)(2,1)S(1)}, bf16[16,2048]{1,0:T(8,128)(2,1)S(1)}, u32[]{:S(2)}, u32[]{:S(2)}) collective-permute-start(bf16[16,2048]{1,0:T(8,128)(2,1)S(1)} %get-tuple-element.15), channel_id=1, source_target_pairs={{0,3},{1,2},{2,1},{3,0},{4,7},{5,6},{6,5},{7,4},{8,11},{9,10},{10,... | collective-permute-start | bytes 196616 | tf_op jit(solution)/shard_map/ppermute | solution.py:35
  23.9 0.5 %collective-permute-start.7 = (bf16[16,2048]{1,0:T(8,128)(2,1)S(1)}, bf16[16,2048]{1,0:T(8,128)(2,1)S(1)}, u32[]{:S(2)}, u32[]{:S(2)}) collective-permute-start(bf16[16,2048]{1,0:T(8,128)(2,1)S(1)} %get-tuple-element.16), channel_id=1, source_target_pairs={{0,1},{1,0},{2,3},{3,2},{4,5},{5,4},{6,7},{7,6},{8,9},{9,8},{10,11... | collective-permute-start | bytes 196616 | tf_op jit(solution)/shard_map/ppermute | solution.py:35
  24.3 0.8 %collective-permute-done.5.refs_1_ = bf16[16,2048]{1,0:T(8,128)(2,1)S(1)} collective-permute-done((bf16[16,2048]{1,0:T(8,128)(2,1)S(1)}, bf16[16,2048]{1,0:T(8,128)(2,1)S(1)}, u32[]{:S(2)}, u32[]{:S(2)}) %collective-permute-start.5) | collective-permute-done | bytes 65568 | tf_op jit(solution)/shard_map/ppermute | solution.py:35
  25.1 3.6 %collective-permute-done.6.refs_2_ = bf16[16,2048]{1,0:T(8,128)(2,1)S(1)} collective-permute-done((bf16[16,2048]{1,0:T(8,128)(2,1)S(1)}, bf16[16,2048]{1,0:T(8,128)(2,1)S(1)}, u32[]{:S(2)}, u32[]{:S(2)}) %collective-permute-start.6) | collective-permute-done | bytes 65568 | tf_op jit(solution)/shard_map/ppermute | solution.py:35
  28.7 0.1 collective-permute-done.7.refs_3_
  29.0 0.8 %collective-permute-start.8 = (bf16[4,2048]{1,0:T(4,128)(2,1)S(1)}, bf16[4,2048]{1,0:T(4,128)(2,1)S(1)}, u32[]{:S(2)}, u32[]{:S(2)}) collective-permute-start(bf16[4,2048]{1,0:T(4,128)(2,1)S(1)} %get-tuple-element.18), channel_id=1, source_target_pairs={{0,8},{4,12},{8,0},{12,4},{1,9},{5,13},{9,1},{13,5},{2,10},{6,14},... | collective-permute-start | bytes 49160 | tf_op jit(solution)/shard_map/ppermute | solution.py:35
  29.7 1.1 %collective-permute-start.9 = (bf16[4,2048]{1,0:T(4,128)(2,1)S(1)}, bf16[4,2048]{1,0:T(4,128)(2,1)S(1)}, u32[]{:S(2)}, u32[]{:S(2)}) collective-permute-start(bf16[4,2048]{1,0:T(4,128)(2,1)S(1)} %get-tuple-element.19), channel_id=1, source_target_pairs={{0,4},{4,0},{8,12},{12,8},{1,5},{5,1},{9,13},{13,9},{2,6},{6,2},{1... | collective-permute-start | bytes 49160 | tf_op jit(solution)/shard_map/ppermute | solution.py:35
  30.8 0.1 copy.7.ids_ref
  30.9 0.1 copy.8.fixed_ref
  31.0 1.1 %collective-permute-done.10.refs_3_ = bf16[4,2048]{1,0:T(4,128)(2,1)S(1)} collective-permute-done((bf16[4,2048]{1,0:T(4,128)(2,1)S(1)}, bf16[4,2048]{1,0:T(4,128)(2,1)S(1)}, u32[]{:S(2)}, u32[]{:S(2)}) %collective-permute-start.10) | collective-permute-done | bytes 16416 | tf_op jit(solution)/shard_map/ppermute | solution.py:35
  32.1 0.7 %collective-permute-done.8.refs_1_ = bf16[4,2048]{1,0:T(4,128)(2,1)S(1)} collective-permute-done((bf16[4,2048]{1,0:T(4,128)(2,1)S(1)}, bf16[4,2048]{1,0:T(4,128)(2,1)S(1)}, u32[]{:S(2)}, u32[]{:S(2)}) %collective-permute-start.8) | collective-permute-done | bytes 16416 | tf_op jit(solution)/shard_map/ppermute | solution.py:35
  32.8 0.8 %mix.1 = bf16[4,2048]{1,0:T(4,128)(2,1)} custom-call(s32[4,2]{1,0:T(4,128)S(1)} %copy.7.ids_ref, s32[4,2]{1,0:T(4,128)S(1)} %copy.8.fixed_ref, bf16[4,2048]{1,0:T(4,128)(2,1)S(1)} %get-tuple-element.17.refs_0_, bf16[4,2048]{1,0:T(4,128)(2,1)S(1)} %collective-permute-done.8.refs_1_, bf16[4,2048]{1,0:T(4,128)(2,1)S(1)} %collective-permute-done.9.refs_2_, ...), custom_call_target="tpu_custom_call" | custom-call | tf_op jit(solution)/shard_map/mix/pallas_call | solution.py:168
  (25 shorter events, 0.2 us)
Async XLA Ops:
  0.0 5.0 %collective-permute-start = (bf16[4,2048]{1,0:T(4,128)(2,1)}, bf16[4,2048]{1,0:T(4,128)(2,1)S(1)}, u32[]{:S(2)}, u32[]{:S(2)}) collective-permute-start(bf16[4,2048]{1,0:T(4,128)(2,1)} %src.1), channel_id=1, source_target_pairs={{1,0},{0,1},{3,2},{2,3},{5,4},{4,5},{7,6},{6,7},{9,8},{8,9},{11,10... | collective-permute-start | bytes 49160 | tf_op jit(solution)/shard_map/ppermute | solution.py:30
  5.0 11.4 %slice-start = ((s8[8388608]{0:T(1024)(128)(4,1)}), s8[4194304]{0:T(1024)(128)(4,1)S(1)}, s32[]{:S(2)}) async-start(s8[8388608]{0:T(1024)(128)(4,1)} %bitcast), calls=%async_computation | async-start | bytes 8388608
  5.0 11.4 %slice-start.2 = ((s8[8388608]{0:T(1024)(128)(4,1)}), s8[4194304]{0:T(1024)(128)(4,1)S(1)}, s32[]{:S(2)}) async-start(s8[8388608]{0:T(1024)(128)(4,1)} %bitcast.2), calls=%async_computation.2 | async-start | bytes 8388608
  5.0 11.4 %slice-start.4 = ((s8[8388608]{0:T(1024)(128)(4,1)}), s8[4194304]{0:T(1024)(128)(4,1)S(1)}, s32[]{:S(2)}) async-start(s8[8388608]{0:T(1024)(128)(4,1)} %bitcast.4), calls=%async_computation.4 | async-start | bytes 8388608
  5.0 11.3 %slice-start.1 = ((s8[8388608]{0:T(1024)(128)(4,1)}), s8[4194304]{0:T(1024)(128)(4,1)S(1)}, s32[]{:S(2)}) async-start(s8[8388608]{0:T(1024)(128)(4,1)} %bitcast), calls=%async_computation.1 | async-start | bytes 8388608
  5.0 11.3 %slice-start.3 = ((s8[8388608]{0:T(1024)(128)(4,1)}), s8[4194304]{0:T(1024)(128)(4,1)S(1)}, s32[]{:S(2)}) async-start(s8[8388608]{0:T(1024)(128)(4,1)} %bitcast.2), calls=%async_computation.3 | async-start | bytes 8388608
  5.0 11.3 %slice-start.5 = ((s8[8388608]{0:T(1024)(128)(4,1)}), s8[4194304]{0:T(1024)(128)(4,1)S(1)}, s32[]{:S(2)}) async-start(s8[8388608]{0:T(1024)(128)(4,1)} %bitcast.4), calls=%async_computation.5 | async-start | bytes 8388608
  5.0 5.0 %collective-permute-start.1 = (bf16[8,2048]{1,0:T(8,128)(2,1)S(1)}, bf16[8,2048]{1,0:T(8,128)(2,1)S(1)}, u32[]{:S(2)}, u32[]{:S(2)}) collective-permute-start(bf16[8,2048]{1,0:T(8,128)(2,1)S(1)} %stack.2.upper), channel_id=1, source_target_pairs={{2,0},{3,1},{0,2},{1,3},{6,4},{7,5},{4,6},{5,7},{10,8},{11,9},{8,1... | collective-permute-start | bytes 98312 | tf_op jit(solution)/shard_map/ppermute | solution.py:30
  10.0 20.8 %copy-start = (s32[4,2]{0,1:T(2,128)S(1)}, s32[4,2]{0,1:T(2,128)}, u32[]{:S(2)}) copy-start(s32[4,2]{0,1:T(2,128)} %param.8) | copy-start | bytes 100
  10.0 20.9 %copy-start.1 = (s32[4,2]{0,1:T(2,128)S(1)}, s32[4,2]{0,1:T(2,128)}, u32[]{:S(2)}) copy-start(s32[4,2]{0,1:T(2,128)} %param.9) | copy-start | bytes 100
  10.1 4.1 %collective-permute-start.2 = (bf16[16,2048]{1,0:T(8,128)(2,1)S(1)}, bf16[16,2048]{1,0:T(8,128)(2,1)S(1)}, u32[]{:S(2)}, u32[]{:S(2)}) collective-permute-start(bf16[16,2048]{1,0:T(8,128)(2,1)S(1)} %stack.3.refs_0_), channel_id=1, source_target_pairs={{12,0},{8,4},{4,8},{0,12},{13,1},{9,5},{5,9},{1,13},{14,2},{10,6},... | collective-permute-start | bytes 196616 | tf_op jit(solution)/shard_map/ppermute | solution.py:30
  10.1 4.0 %collective-permute-start.3 = (bf16[16,2048]{1,0:T(8,128)(2,1)S(1)}, bf16[16,2048]{1,0:T(8,128)(2,1)S(1)}, u32[]{:S(2)}, u32[]{:S(2)}) collective-permute-start(bf16[16,2048]{1,0:T(8,128)(2,1)S(1)} %stack.3.refs_0_), channel_id=1, source_target_pairs={{4,0},{0,4},{12,8},{8,12},{5,1},{1,5},{13,9},{9,13},{6,2},{2,6},{1... | collective-permute-start | bytes 196616 | tf_op jit(solution)/shard_map/ppermute | solution.py:30
  12.1 4.3 %collective-permute-start.4 = (bf16[16,2048]{1,0:T(8,128)(2,1)S(1)}, bf16[16,2048]{1,0:T(8,128)(2,1)S(1)}, u32[]{:S(2)}, u32[]{:S(2)}) collective-permute-start(bf16[16,2048]{1,0:T(8,128)(2,1)S(1)} %stack.3.refs_0_), channel_id=1, source_target_pairs={{8,0},{12,4},{0,8},{4,12},{9,1},{13,5},{1,9},{5,13},{10,2},{14,6},... | collective-permute-start | bytes 196616 | tf_op jit(solution)/shard_map/ppermute | solution.py:30
  19.9 5.2 %collective-permute-start.5 = (bf16[16,2048]{1,0:T(8,128)(2,1)S(1)}, bf16[16,2048]{1,0:T(8,128)(2,1)S(1)}, u32[]{:S(2)}, u32[]{:S(2)}) collective-permute-start(bf16[16,2048]{1,0:T(8,128)(2,1)S(1)} %get-tuple-element.14), channel_id=1, source_target_pairs={{0,2},{1,3},{2,0},{3,1},{4,6},{5,7},{6,4},{7,5},{8,10},{9,11},{10,... | collective-permute-start | bytes 196616 | tf_op jit(solution)/shard_map/ppermute | solution.py:35
  22.5 6.2 %collective-permute-start.6 = (bf16[16,2048]{1,0:T(8,128)(2,1)S(1)}, bf16[16,2048]{1,0:T(8,128)(2,1)S(1)}, u32[]{:S(2)}, u32[]{:S(2)}) collective-permute-start(bf16[16,2048]{1,0:T(8,128)(2,1)S(1)} %get-tuple-element.15), channel_id=1, source_target_pairs={{0,3},{1,2},{2,1},{3,0},{4,7},{5,6},{6,5},{7,4},{8,11},{9,10},{10,... | collective-permute-start | bytes 196616 | tf_op jit(solution)/shard_map/ppermute | solution.py:35
  23.9 5.0 %collective-permute-start.7 = (bf16[16,2048]{1,0:T(8,128)(2,1)S(1)}, bf16[16,2048]{1,0:T(8,128)(2,1)S(1)}, u32[]{:S(2)}, u32[]{:S(2)}) collective-permute-start(bf16[16,2048]{1,0:T(8,128)(2,1)S(1)} %get-tuple-element.16), channel_id=1, source_target_pairs={{0,1},{1,0},{2,3},{3,2},{4,5},{5,4},{6,7},{7,6},{8,9},{9,8},{10,11... | collective-permute-start | bytes 196616 | tf_op jit(solution)/shard_map/ppermute | solution.py:35
  28.9 3.2 %collective-permute-start.10 = (bf16[4,2048]{1,0:T(4,128)(2,1)S(1)}, bf16[4,2048]{1,0:T(4,128)(2,1)S(1)}, u32[]{:S(2)}, u32[]{:S(2)}) collective-permute-start(bf16[4,2048]{1,0:T(4,128)(2,1)S(1)} %get-tuple-element.20), channel_id=1, source_target_pairs={{0,12},{4,8},{8,4},{12,0},{1,13},{5,9},{9,5},{13,1},{2,14},{6,10},... | collective-permute-start | bytes 49160 | tf_op jit(solution)/shard_map/ppermute | solution.py:35
  29.0 3.8 %collective-permute-start.8 = (bf16[4,2048]{1,0:T(4,128)(2,1)S(1)}, bf16[4,2048]{1,0:T(4,128)(2,1)S(1)}, u32[]{:S(2)}, u32[]{:S(2)}) collective-permute-start(bf16[4,2048]{1,0:T(4,128)(2,1)S(1)} %get-tuple-element.18), channel_id=1, source_target_pairs={{0,8},{4,12},{8,0},{12,4},{1,9},{5,13},{9,1},{13,5},{2,10},{6,14},... | collective-permute-start | bytes 49160 | tf_op jit(solution)/shard_map/ppermute | solution.py:35
  29.7 3.0 %collective-permute-start.9 = (bf16[4,2048]{1,0:T(4,128)(2,1)S(1)}, bf16[4,2048]{1,0:T(4,128)(2,1)S(1)}, u32[]{:S(2)}, u32[]{:S(2)}) collective-permute-start(bf16[4,2048]{1,0:T(4,128)(2,1)S(1)} %get-tuple-element.19), channel_id=1, source_target_pairs={{0,4},{4,0},{8,12},{12,8},{1,5},{5,1},{9,13},{13,9},{2,6},{6,2},{1... | collective-permute-start | bytes 49160 | tf_op jit(solution)/shard_map/ppermute | solution.py:35

commit v5 on v4

--- a/solution.py
+++ b/solution.py
@@ -37,10 +37,6 @@
 
 def last_first(n):
     return [0, n - 1, *range(1, n - 1)]
-
-
-def first_last(n):
-    return [0, *range(2, n), 1]
 
 
 def half_first(n):
@@ -91,9 +87,9 @@
     )(upper, lower)
 
 
-def ffn_kernel(order, n_b, count, *refs):
-    n_e = len(order)
-    xs, (gate_w, up_w, down_w), outs = restored(refs[:n_e], order), refs[n_e : n_e + 3], refs[n_e + 3 :]
+def ffn_kernel(order, n_e, n_b, count, *refs):
+    xs, refs = restored(refs[: len(order)], order), refs[len(order) :]
+    (gate_w, up_w, down_w), outs = refs[:3], refs[3:]
     x = jnp.concatenate([r[...] for r in xs], axis=0)
     spare = -x.shape[0] % ROWS
     if spare:
@@ -107,21 +103,22 @@
         out[...] = jnp.concatenate(part, axis=0).astype(out.dtype)
 
 
-def ffn(xs, w_gate, w_up, w_down, n_b, count):
-    n_e, (rows, width) = len(xs), xs[0].shape
-    order = last_first(n_e)
+def ffn(xs, w_gate, w_up, w_down, n_e, n_b, count):
+    rows, width = n_b * count, xs[0].shape[1]
+    pieces = len(xs) // n_e
+    order = [m * pieces + p for p in range(pieces) for m in range(n_e)]
     out_shape = [
         jax.ShapeDtypeStruct((n_e * count, width), jnp.float32 if d == 0 else jnp.bfloat16) for d in range(n_b)
     ]
     return pl.pallas_call(
-        functools.partial(ffn_kernel, order, n_b, count),
+        functools.partial(ffn_kernel, order, n_e, n_b, count),
         name="ffn",
         compiler_params=limit(20 if n_e * rows <= ROWS else 40),
         cost_estimate=pl.CostEstimate(
             flops=6 * n_e * rows * w_gate.size, transcendentals=0, bytes_accessed=6 * w_gate.size
         ),
         out_shape=out_shape,
-        in_specs=[VMEM] * (n_e + 3),
+        in_specs=[VMEM] * (len(xs) + 3),
         out_specs=[VMEM] * n_b,
     )(*[xs[i] for i in order], w_gate, w_up, w_down)
 
@@ -138,7 +135,7 @@
 
 def merge(parts, n_e):
     rows, width = parts[0].shape
-    order = first_last(len(parts))
+    order = last_first(len(parts))
     return pl.pallas_call(
         functools.partial(merge_kernel, order),
         name="merge",
@@ -179,12 +176,13 @@
     count = tokens.shape[0]
     n_e, n_b = lax.axis_size("expert"), lax.axis_size("blk")
     mine, step = tokens, 1
-    while step < n_b:
+    while 2 * step < n_b:
         more = fetch(mine[: (n_b - step) * count], "blk", step)
         mine = stack(on_chip(mine) if step == 1 else mine, more)
         step *= 2
-    xs = [mine] + [fetch(mine, "expert", m) for m in range(1, n_e)]
-    parts = ffn(xs, w_gate, w_up, w_down, n_b, count)
+    pieces = [mine] if n_b == step else [mine, fetch(mine[: (n_b - step) * count], "blk", step)]
+    xs = [fetch(piece, "expert", m) if m else piece for m in range(n_e) for piece in pieces]
+    parts = ffn(xs, w_gate, w_up, w_down, n_e, n_b, count)
     parts = [parts[0]] + [deliver(parts[d], "blk", d) for d in range(1, n_b)]
     blocks = merge(parts, n_e)
     blocks = [blocks[0]] + [deliver(blocks[m], "expert", m) for m in range(1, n_e)]

time: 33.8 us -> 33.3 us (0.985)
  waiting for transfers between devices: 13.4 us -> 10.9 us
  starting transfers between devices: 14.7 us -> 16.6 us
    ppermute x5 -> x8, waiting for transfers between devices: 7.11 us -> 4.25 us  [fetch(): return lax.ppermute(x, axis, [(peer(i, d, n), i) for i in range(n)])]
    ppermute x5 -> x8, starting transfers between devices: 8.35 us -> 9.95 us  [fetch(): return lax.ppermute(x, axis, [(peer(i, d, n), i) for i in range(n)])]
    ppermute x6, waiting for transfers between devices: 6.26 us -> 6.64 us  [deliver(): return lax.ppermute(x, axis, [(i, peer(i, d, n)) for i in range(n)])]
  transfers between devices with their start and end apart: 11 -> 14, of which waited for: 9 -> 10; matrix products, arithmetic and copies ran while one was open for 1% -> 1% of each run, Pallas kernels for 2% -> 3%
where the time goes in v5:
time: 33.3 us; the launch traced here: 33.1 us
  starting transfers between devices  16.6 us (50%)
  waiting for transfers between devices  10.9 us (33%)
  Pallas kernels  5.17 us (16%)
    ppermute x8, starting transfers between devices, fetch(): return lax.ppermute(x, axis, [(peer(i, d, n), i) for i in range(n)])  9.95 us
    ppermute x6, starting transfers between devices, deliver(): return lax.ppermute(x, axis, [(i, peer(i, d, n)) for i in range(n)])  6.67 us
    ppermute x6, waiting for transfers between devices, deliver(): return lax.ppermute(x, axis, [(i, peer(i, d, n)) for i in range(n)])  6.64 us
    ppermute x8, waiting for transfers between devices, fetch(): return lax.ppermute(x, axis, [(peer(i, d, n), i) for i in range(n)])  4.25 us
    pallas_call x1, Pallas kernels, ffn(): pl.pallas_call(functools.partial(ffn_kernel, order, n_e, n_b, count), nam...  3.47 us
    pallas_call x1, Pallas kernels, on_chip(): pl.pallas_call(rows_kernel, name='rows', compiler_params=limit(1), cost_e...  0.87 us
    pallas_call x1, Pallas kernels, mix(): pl.pallas_call(functools.partial(mix_kernel, order), name='mix', compiler...  0.79 us
  transfers between devices with their start and end apart: 14, of which 10 were waited for; matrix products, arithmetic and copies ran while one was open for 1% of the time, Pallas kernels for 3%

profile of v5, /device:TPU:0, one launch (start us, length us, event | category | flops | bytes accessed | tf_op | source)
XLA Modules:
  0.0 33.1 jit_solution(147088711445801254)
XLA Ops:
  0.0 3.1 %collective-permute-start = (bf16[4,2048]{1,0:T(4,128)(2,1)}, bf16[4,2048]{1,0:T(4,128)(2,1)S(1)}, u32[]{:S(2)}, u32[]{:S(2)}) collective-permute-start(bf16[4,2048]{1,0:T(4,128)(2,1)} %src.1), channel_id=1, source_target_pairs={{1,0},{0,1},{3,2},{2,3},{5,4},{4,5},{7,6},{6,7},{9,8},{8,9},{11,10... | collective-permute-start | bytes 49160 | tf_op jit(solution)/shard_map/ppermute | solution.py:30
  3.1 0.9 %rows.1.upper = bf16[4,2048]{1,0:T(4,128)(2,1)S(1)} custom-call(bf16[4,2048]{1,0:T(4,128)(2,1)} %src.1), custom_call_target="tpu_custom_call" | custom-call | bytes 32768 | tf_op jit(solution)/shard_map/rows/pallas_call | solution.py:60
  4.0 1.0 %collective-permute-done.lower = bf16[4,2048]{1,0:T(4,128)(2,1)S(1)} collective-permute-done((bf16[4,2048]{1,0:T(4,128)(2,1)}, bf16[4,2048]{1,0:T(4,128)(2,1)S(1)}, u32[]{:S(2)}, u32[]{:S(2)}) %collective-permute-start) | collective-permute-done | bytes 16416 | tf_op jit(solution)/shard_map/ppermute | solution.py:30
  5.0 3.1 %collective-permute-start.4 = (bf16[8,2048]{1,0:T(8,128)(2,1)S(1)}, bf16[8,2048]{1,0:T(8,128)(2,1)S(1)}, u32[]{:S(2)}, u32[]{:S(2)}) collective-permute-start(bf16[8,2048]{1,0:T(8,128)(2,1)S(1)} %stack.1.refs_0_), channel_id=1, source_target_pairs={{2,0},{3,1},{0,2},{1,3},{6,4},{7,5},{4,6},{5,7},{10,8},{11,9},{8,1... | collective-permute-start | bytes 98312 | tf_op jit(solution)/shard_map/ppermute | solution.py:30
  8.1 1.5 %collective-permute-start.2 = (bf16[8,2048]{1,0:T(8,128)(2,1)S(1)}, bf16[8,2048]{1,0:T(8,128)(2,1)S(1)}, u32[]{:S(2)}, u32[]{:S(2)}) collective-permute-start(bf16[8,2048]{1,0:T(8,128)(2,1)S(1)} %stack.1.refs_0_), channel_id=1, source_target_pairs={{8,0},{12,4},{0,8},{4,12},{9,1},{13,5},{1,9},{5,13},{10,2},{14,6},... | collective-permute-start | bytes 98312 | tf_op jit(solution)/shard_map/ppermute | solution.py:30
  9.6 0.4 %collective-permute-start.3 = (bf16[8,2048]{1,0:T(8,128)(2,1)S(1)}, bf16[8,2048]{1,0:T(8,128)(2,1)S(1)}, u32[]{:S(2)}, u32[]{:S(2)}) collective-permute-start(bf16[8,2048]{1,0:T(8,128)(2,1)S(1)} %stack.1.refs_0_), channel_id=1, source_target_pairs={{12,0},{8,4},{4,8},{0,12},{13,1},{9,5},{5,9},{1,13},{14,2},{10,6},... | collective-permute-start | bytes 98312 | tf_op jit(solution)/shard_map/ppermute | solution.py:30
  10.0 0.3 collective-permute-start.5
  10.3 1.6 %collective-permute-start.6 = (bf16[8,2048]{1,0:T(8,128)(2,1)S(1)}, bf16[8,2048]{1,0:T(8,128)(2,1)S(1)}, u32[]{:S(2)}, u32[]{:S(2)}) collective-permute-start(bf16[8,2048]{1,0:T(8,128)(2,1)S(1)} %collective-permute-done.4.refs_4_), channel_id=1, source_target_pairs={{8,0},{12,4},{0,8},{4,12},{9,1},{13,5},{1,9},{5,13},{10,2},{14,6},... | collective-permute-start | bytes 98312 | tf_op jit(solution)/shard_map/ppermute | solution.py:30
  11.8 0.1 collective-permute-start.7
  12.0 0.9 %collective-permute-done.3.refs_3_ = bf16[8,2048]{1,0:T(8,128)(2,1)S(1)} collective-permute-done((bf16[8,2048]{1,0:T(8,128)(2,1)S(1)}, bf16[8,2048]{1,0:T(8,128)(2,1)S(1)}, u32[]{:S(2)}, u32[]{:S(2)}) %collective-permute-start.3) | collective-permute-done | bytes 32800 | tf_op jit(solution)/shard_map/ppermute | solution.py:30
  13.0 1.2 %collective-permute-done.6.refs_6_ = bf16[8,2048]{1,0:T(8,128)(2,1)S(1)} collective-permute-done((bf16[8,2048]{1,0:T(8,128)(2,1)S(1)}, bf16[8,2048]{1,0:T(8,128)(2,1)S(1)}, u32[]{:S(2)}, u32[]{:S(2)}) %collective-permute-start.6) | collective-permute-done | bytes 32800 | tf_op jit(solution)/shard_map/ppermute | solution.py:30
  14.2 1.0 %collective-permute-done.7.refs_7_ = bf16[8,2048]{1,0:T(8,128)(2,1)S(1)} collective-permute-done((bf16[8,2048]{1,0:T(8,128)(2,1)S(1)}, bf16[8,2048]{1,0:T(8,128)(2,1)S(1)}, u32[]{:S(2)}, u32[]{:S(2)}) %collective-permute-start.7) | collective-permute-done | bytes 32800 | tf_op jit(solution)/shard_map/ppermute | solution.py:30
  15.2 3.5 %ffn.1 = (f32[16,2048]{1,0:T(8,128)S(1)}, bf16[16,2048]{1,0:T(8,128)(2,1)S(1)}, bf16[16,2048]{1,0:T(8,128)(2,1)S(1)}, bf16[16,2048]{1,0:T(8,128)(2,1)S(1)}) custom-call(bf16[8,2048]{1,0:T(8,128)(2,1)S(1)} %stack.1.refs_0_, bf16[8,2048]{1,0:T(8,128)(2,1)S(1)} %collective-permute-done.1.refs_1_, bf16[8,2048]{1,0:T(8,128)(2,1)S(1)} %collective-permute-done.2.refs_2_, ...), custom_call_target="tpu_custom_call" | custom-call | flops 1610612736 | bytes 25165824 | tf_op jit(solution)/shard_map/ffn/pallas_call | solution.py:113
  18.7 2.7 %collective-permute-start.10 = (bf16[16,2048]{1,0:T(8,128)(2,1)S(1)}, bf16[16,2048]{1,0:T(8,128)(2,1)S(1)}, u32[]{:S(2)}, u32[]{:S(2)}) collective-permute-start(bf16[16,2048]{1,0:T(8,128)(2,1)S(1)} %get-tuple-element.16), channel_id=1, source_target_pairs={{0,2},{1,3},{2,0},{3,1},{4,6},{5,7},{6,4},{7,5},{8,10},{9,11},{10,... | collective-permute-start | bytes 196616 | tf_op jit(solution)/shard_map/ppermute | solution.py:35
  21.4 1.3 %collective-permute-start.8 = (bf16[16,2048]{1,0:T(8,128)(2,1)S(1)}, bf16[16,2048]{1,0:T(8,128)(2,1)S(1)}, u32[]{:S(2)}, u32[]{:S(2)}) collective-permute-start(bf16[16,2048]{1,0:T(8,128)(2,1)S(1)} %get-tuple-element.14), channel_id=1, source_target_pairs={{0,3},{1,2},{2,1},{3,0},{4,7},{5,6},{6,5},{7,4},{8,11},{9,10},{10,... | collective-permute-start | bytes 196616 | tf_op jit(solution)/shard_map/ppermute | solution.py:35
  22.7 0.5 %collective-permute-start.9 = (bf16[16,2048]{1,0:T(8,128)(2,1)S(1)}, bf16[16,2048]{1,0:T(8,128)(2,1)S(1)}, u32[]{:S(2)}, u32[]{:S(2)}) collective-permute-start(bf16[16,2048]{1,0:T(8,128)(2,1)S(1)} %get-tuple-element.15), channel_id=1, source_target_pairs={{0,1},{1,0},{2,3},{3,2},{4,5},{5,4},{6,7},{7,6},{8,9},{9,8},{10,11... | collective-permute-start | bytes 196616 | tf_op jit(solution)/shard_map/ppermute | solution.py:35
  23.2 2.3 %collective-permute-done.10.refs_3_ = bf16[16,2048]{1,0:T(8,128)(2,1)S(1)} collective-permute-done((bf16[16,2048]{1,0:T(8,128)(2,1)S(1)}, bf16[16,2048]{1,0:T(8,128)(2,1)S(1)}, u32[]{:S(2)}, u32[]{:S(2)}) %collective-permute-start.10) | collective-permute-done | bytes 65568 | tf_op jit(solution)/shard_map/ppermute | solution.py:35
  25.5 2.3 %collective-permute-done.8.refs_1_ = bf16[16,2048]{1,0:T(8,128)(2,1)S(1)} collective-permute-done((bf16[16,2048]{1,0:T(8,128)(2,1)S(1)}, bf16[16,2048]{1,0:T(8,128)(2,1)S(1)}, u32[]{:S(2)}, u32[]{:S(2)}) %collective-permute-start.8) | collective-permute-done | bytes 65568 | tf_op jit(solution)/shard_map/ppermute | solution.py:35
  27.9 0.3 %collective-permute-done.9.refs_2_ = bf16[16,2048]{1,0:T(8,128)(2,1)S(1)} collective-permute-done((bf16[16,2048]{1,0:T(8,128)(2,1)S(1)}, bf16[16,2048]{1,0:T(8,128)(2,1)S(1)}, u32[]{:S(2)}, u32[]{:S(2)}) %collective-permute-start.9) | collective-permute-done | bytes 65568 | tf_op jit(solution)/shard_map/ppermute | solution.py:35
  28.2 0.9 %collective-permute-start.11 = (bf16[4,2048]{1,0:T(4,128)(2,1)S(1)}, bf16[4,2048]{1,0:T(4,128)(2,1)S(1)}, u32[]{:S(2)}, u32[]{:S(2)}) collective-permute-start(bf16[4,2048]{1,0:T(4,128)(2,1)S(1)} %get-tuple-element.18), channel_id=1, source_target_pairs={{0,8},{4,12},{8,0},{12,4},{1,9},{5,13},{9,1},{13,5},{2,10},{6,14},... | collective-permute-start | bytes 49160 | tf_op jit(solution)/shard_map/ppermute | solution.py:35
  29.1 1.3 %collective-permute-start.13 = (bf16[4,2048]{1,0:T(4,128)(2,1)S(1)}, bf16[4,2048]{1,0:T(4,128)(2,1)S(1)}, u32[]{:S(2)}, u32[]{:S(2)}) collective-permute-start(bf16[4,2048]{1,0:T(4,128)(2,1)S(1)} %get-tuple-element.20), channel_id=1, source_target_pairs={{0,12},{4,8},{8,4},{12,0},{1,13},{5,9},{9,5},{13,1},{2,14},{6,10},... | collective-permute-start | bytes 49160 | tf_op jit(solution)/shard_map/ppermute | solution.py:35
  30.6 1.4 %collective-permute-done.11.refs_1_ = bf16[4,2048]{1,0:T(4,128)(2,1)S(1)} collective-permute-done((bf16[4,2048]{1,0:T(4,128)(2,1)S(1)}, bf16[4,2048]{1,0:T(4,128)(2,1)S(1)}, u32[]{:S(2)}, u32[]{:S(2)}) %collective-permute-start.11) | collective-permute-done | bytes 16416 | tf_op jit(solution)/shard_map/ppermute | solution.py:35
  32.0 0.2 collective-permute-done.13.refs_3_
  32.3 0.8 %mix.1 = bf16[4,2048]{1,0:T(4,128)(2,1)} custom-call(s32[4,2]{1,0:T(4,128)S(1)} %copy.7.ids_ref, s32[4,2]{1,0:T(4,128)S(1)} %copy.8.fixed_ref, bf16[4,2048]{1,0:T(4,128)(2,1)S(1)} %get-tuple-element.17.refs_0_, bf16[4,2048]{1,0:T(4,128)(2,1)S(1)} %collective-permute-done.11.refs_1_, bf16[4,2048]{1,0:T(4,128)(2,1)S(1)} %collective-permute-done.12.refs_2_, ...), custom_call_target="tpu_custom_call" | custom-call | tf_op jit(solution)/shard_map/mix/pallas_call | solution.py:165
  (30 shorter events, 0.4 us)
Async XLA Ops:
  0.0 5.0 %collective-permute-start = (bf16[4,2048]{1,0:T(4,128)(2,1)}, bf16[4,2048]{1,0:T(4,128)(2,1)S(1)}, u32[]{:S(2)}, u32[]{:S(2)}) collective-permute-start(bf16[4,2048]{1,0:T(4,128)(2,1)} %src.1), channel_id=1, source_target_pairs={{1,0},{0,1},{3,2},{2,3},{5,4},{4,5},{7,6},{6,7},{9,8},{8,9},{11,10... | collective-permute-start | bytes 49160 | tf_op jit(solution)/shard_map/ppermute | solution.py:30
  3.1 12.1 %slice-start = ((s8[8388608]{0:T(1024)(128)(4,1)}), s8[4194304]{0:T(1024)(128)(4,1)S(1)}, s32[]{:S(2)}) async-start(s8[8388608]{0:T(1024)(128)(4,1)} %bitcast), calls=%async_computation | async-start | bytes 8388608
  3.1 12.1 %slice-start.2 = ((s8[8388608]{0:T(1024)(128)(4,1)}), s8[4194304]{0:T(1024)(128)(4,1)S(1)}, s32[]{:S(2)}) async-start(s8[8388608]{0:T(1024)(128)(4,1)} %bitcast.2), calls=%async_computation.2 | async-start | bytes 8388608
  3.1 12.1 %slice-start.4 = ((s8[8388608]{0:T(1024)(128)(4,1)}), s8[4194304]{0:T(1024)(128)(4,1)S(1)}, s32[]{:S(2)}) async-start(s8[8388608]{0:T(1024)(128)(4,1)} %bitcast.4), calls=%async_computation.4 | async-start | bytes 8388608
  3.9 11.3 %slice-start.1 = ((s8[8388608]{0:T(1024)(128)(4,1)}), s8[4194304]{0:T(1024)(128)(4,1)S(1)}, s32[]{:S(2)}) async-start(s8[8388608]{0:T(1024)(128)(4,1)} %bitcast), calls=%async_computation.1 | async-start | bytes 8388608
  4.0 11.3 %slice-start.3 = ((s8[8388608]{0:T(1024)(128)(4,1)}), s8[4194304]{0:T(1024)(128)(4,1)S(1)}, s32[]{:S(2)}) async-start(s8[8388608]{0:T(1024)(128)(4,1)} %bitcast.2), calls=%async_computation.3 | async-start | bytes 8388608
  4.0 11.2 %slice-start.5 = ((s8[8388608]{0:T(1024)(128)(4,1)}), s8[4194304]{0:T(1024)(128)(4,1)S(1)}, s32[]{:S(2)}) async-start(s8[8388608]{0:T(1024)(128)(4,1)} %bitcast.4), calls=%async_computation.5 | async-start | bytes 8388608
  5.0 25.4 %copy-start = (s32[4,2]{0,1:T(2,128)S(1)}, s32[4,2]{0,1:T(2,128)}, u32[]{:S(2)}) copy-start(s32[4,2]{0,1:T(2,128)} %param.8) | copy-start | bytes 100
  5.0 25.5 %copy-start.1 = (s32[4,2]{0,1:T(2,128)S(1)}, s32[4,2]{0,1:T(2,128)}, u32[]{:S(2)}) copy-start(s32[4,2]{0,1:T(2,128)} %param.9) | copy-start | bytes 100
  5.0 5.0 %collective-permute-start.4 = (bf16[8,2048]{1,0:T(8,128)(2,1)S(1)}, bf16[8,2048]{1,0:T(8,128)(2,1)S(1)}, u32[]{:S(2)}, u32[]{:S(2)}) collective-permute-start(bf16[8,2048]{1,0:T(8,128)(2,1)S(1)} %stack.1.refs_0_), channel_id=1, source_target_pairs={{2,0},{3,1},{0,2},{1,3},{6,4},{7,5},{4,6},{5,7},{10,8},{11,9},{8,1... | collective-permute-start | bytes 98312 | tf_op jit(solution)/shard_map/ppermute | solution.py:30
  8.1 3.7 %collective-permute-start.1 = (bf16[8,2048]{1,0:T(8,128)(2,1)S(1)}, bf16[8,2048]{1,0:T(8,128)(2,1)S(1)}, u32[]{:S(2)}, u32[]{:S(2)}) collective-permute-start(bf16[8,2048]{1,0:T(8,128)(2,1)S(1)} %stack.1.refs_0_), channel_id=1, source_target_pairs={{4,0},{0,4},{12,8},{8,12},{5,1},{1,5},{13,9},{9,13},{6,2},{2,6},{1... | collective-permute-start | bytes 98312 | tf_op jit(solution)/shard_map/ppermute | solution.py:30
  8.1 3.9 %collective-permute-start.2 = (bf16[8,2048]{1,0:T(8,128)(2,1)S(1)}, bf16[8,2048]{1,0:T(8,128)(2,1)S(1)}, u32[]{:S(2)}, u32[]{:S(2)}) collective-permute-start(bf16[8,2048]{1,0:T(8,128)(2,1)S(1)} %stack.1.refs_0_), channel_id=1, source_target_pairs={{8,0},{12,4},{0,8},{4,12},{9,1},{13,5},{1,9},{5,13},{10,2},{14,6},... | collective-permute-start | bytes 98312 | tf_op jit(solution)/shard_map/ppermute | solution.py:30
  9.6 3.3 %collective-permute-start.3 = (bf16[8,2048]{1,0:T(8,128)(2,1)S(1)}, bf16[8,2048]{1,0:T(8,128)(2,1)S(1)}, u32[]{:S(2)}, u32[]{:S(2)}) collective-permute-start(bf16[8,2048]{1,0:T(8,128)(2,1)S(1)} %stack.1.refs_0_), channel_id=1, source_target_pairs={{12,0},{8,4},{4,8},{0,12},{13,1},{9,5},{5,9},{1,13},{14,2},{10,6},... | collective-permute-start | bytes 98312 | tf_op jit(solution)/shard_map/ppermute | solution.py:30
  10.0 2.9 %collective-permute-start.5 = (bf16[8,2048]{1,0:T(8,128)(2,1)S(1)}, bf16[8,2048]{1,0:T(8,128)(2,1)S(1)}, u32[]{:S(2)}, u32[]{:S(2)}) collective-permute-start(bf16[8,2048]{1,0:T(8,128)(2,1)S(1)} %collective-permute-done.4.refs_4_), channel_id=1, source_target_pairs={{4,0},{0,4},{12,8},{8,12},{5,1},{1,5},{13,9},{9,13},{6,2},{2,6},{1... | collective-permute-start | bytes 98312 | tf_op jit(solution)/shard_map/ppermute | solution.py:30
  10.3 3.9 %collective-permute-start.6 = (bf16[8,2048]{1,0:T(8,128)(2,1)S(1)}, bf16[8,2048]{1,0:T(8,128)(2,1)S(1)}, u32[]{:S(2)}, u32[]{:S(2)}) collective-permute-start(bf16[8,2048]{1,0:T(8,128)(2,1)S(1)} %collective-permute-done.4.refs_4_), channel_id=1, source_target_pairs={{8,0},{12,4},{0,8},{4,12},{9,1},{13,5},{1,9},{5,13},{10,2},{14,6},... | collective-permute-start | bytes 98312 | tf_op jit(solution)/shard_map/ppermute | solution.py:30
  11.8 3.3 %collective-permute-start.7 = (bf16[8,2048]{1,0:T(8,128)(2,1)S(1)}, bf16[8,2048]{1,0:T(8,128)(2,1)S(1)}, u32[]{:S(2)}, u32[]{:S(2)}) collective-permute-start(bf16[8,2048]{1,0:T(8,128)(2,1)S(1)} %collective-permute-done.4.refs_4_), channel_id=1, source_target_pairs={{12,0},{8,4},{4,8},{0,12},{13,1},{9,5},{5,9},{1,13},{14,2},{10,6},... | collective-permute-start | bytes 98312 | tf_op jit(solution)/shard_map/ppermute | solution.py:30
  18.7 6.8 %collective-permute-start.10 = (bf16[16,2048]{1,0:T(8,128)(2,1)S(1)}, bf16[16,2048]{1,0:T(8,128)(2,1)S(1)}, u32[]{:S(2)}, u32[]{:S(2)}) collective-permute-start(bf16[16,2048]{1,0:T(8,128)(2,1)S(1)} %get-tuple-element.16), channel_id=1, source_target_pairs={{0,2},{1,3},{2,0},{3,1},{4,6},{5,7},{6,4},{7,5},{8,10},{9,11},{10,... | collective-permute-start | bytes 196616 | tf_op jit(solution)/shard_map/ppermute | solution.py:35
  21.4 6.5 %collective-permute-start.8 = (bf16[16,2048]{1,0:T(8,128)(2,1)S(1)}, bf16[16,2048]{1,0:T(8,128)(2,1)S(1)}, u32[]{:S(2)}, u32[]{:S(2)}) collective-permute-start(bf16[16,2048]{1,0:T(8,128)(2,1)S(1)} %get-tuple-element.14), channel_id=1, source_target_pairs={{0,3},{1,2},{2,1},{3,0},{4,7},{5,6},{6,5},{7,4},{8,11},{9,10},{10,... | collective-permute-start | bytes 196616 | tf_op jit(solution)/shard_map/ppermute | solution.py:35
  22.7 5.5 %collective-permute-start.9 = (bf16[16,2048]{1,0:T(8,128)(2,1)S(1)}, bf16[16,2048]{1,0:T(8,128)(2,1)S(1)}, u32[]{:S(2)}, u32[]{:S(2)}) collective-permute-start(bf16[16,2048]{1,0:T(8,128)(2,1)S(1)} %get-tuple-element.15), channel_id=1, source_target_pairs={{0,1},{1,0},{2,3},{3,2},{4,5},{5,4},{6,7},{7,6},{8,9},{9,8},{10,11... | collective-permute-start | bytes 196616 | tf_op jit(solution)/shard_map/ppermute | solution.py:35
  28.2 3.8 %collective-permute-start.11 = (bf16[4,2048]{1,0:T(4,128)(2,1)S(1)}, bf16[4,2048]{1,0:T(4,128)(2,1)S(1)}, u32[]{:S(2)}, u32[]{:S(2)}) collective-permute-start(bf16[4,2048]{1,0:T(4,128)(2,1)S(1)} %get-tuple-element.18), channel_id=1, source_target_pairs={{0,8},{4,12},{8,0},{12,4},{1,9},{5,13},{9,1},{13,5},{2,10},{6,14},... | collective-permute-start | bytes 49160 | tf_op jit(solution)/shard_map/ppermute | solution.py:35
  29.1 2.9 %collective-permute-start.12 = (bf16[4,2048]{1,0:T(4,128)(2,1)S(1)}, bf16[4,2048]{1,0:T(4,128)(2,1)S(1)}, u32[]{:S(2)}, u32[]{:S(2)}) collective-permute-start(bf16[4,2048]{1,0:T(4,128)(2,1)S(1)} %get-tuple-element.19), channel_id=1, source_target_pairs={{0,4},{4,0},{8,12},{12,8},{1,5},{5,1},{9,13},{13,9},{2,6},{6,2},{1... | collective-permute-start | bytes 49160 | tf_op jit(solution)/shard_map/ppermute | solution.py:35
  29.1 3.2 %collective-permute-start.13 = (bf16[4,2048]{1,0:T(4,128)(2,1)S(1)}, bf16[4,2048]{1,0:T(4,128)(2,1)S(1)}, u32[]{:S(2)}, u32[]{:S(2)}) collective-permute-start(bf16[4,2048]{1,0:T(4,128)(2,1)S(1)} %get-tuple-element.20), channel_id=1, source_target_pairs={{0,12},{4,8},{8,4},{12,0},{1,13},{5,9},{9,5},{13,1},{2,14},{6,10},... | collective-permute-start | bytes 49160 | tf_op jit(solution)/shard_map/ppermute | solution.py:35

commit v6 on v5

--- a/solution.py
+++ b/solution.py
@@ -39,8 +39,8 @@
     return [0, n - 1, *range(1, n - 1)]
 
 
-def half_first(n):
-    return [0, n // 2, *(i for i in range(1, n) if i != n // 2)]
+def falling(n):
+    return [0, *range(n - 1, 0, -1)]
 
 
 def restored(refs, order):
@@ -161,7 +161,7 @@
 
 
 def mix(route_ids, gate_fixed, blocks):
-    order = half_first(len(blocks))
+    order = falling(len(blocks))
     return pl.pallas_call(
         functools.partial(mix_kernel, order),
         name="mix",

time: 33.3 us -> 33.2 us (level)
  no operation moved by 1% of the time
where the time goes in v6:
time: 33.2 us; the launch traced here: 33 us
  starting transfers between devices  16.3 us (49%)
  waiting for transfers between devices  11.1 us (33%)
  Pallas kernels  5.17 us (16%)
    ppermute x8, starting transfers between devices, fetch(): return lax.ppermute(x, axis, [(peer(i, d, n), i) for i in range(n)])  9.95 us
    ppermute x6, waiting for transfers between devices, deliver(): return lax.ppermute(x, axis, [(i, peer(i, d, n)) for i in range(n)])  6.82 us
    ppermute x6, starting transfers between devices, deliver(): return lax.ppermute(x, axis, [(i, peer(i, d, n)) for i in range(n)])  6.39 us
    ppermute x8, waiting for transfers between devices, fetch(): return lax.ppermute(x, axis, [(peer(i, d, n), i) for i in range(n)])  4.25 us
    pallas_call x1, Pallas kernels, ffn(): pl.pallas_call(functools.partial(ffn_kernel, order, n_e, n_b, count), nam...  3.47 us
    pallas_call x1, Pallas kernels, on_chip(): pl.pallas_call(rows_kernel, name='rows', compiler_params=limit(1), cost_e...  0.87 us
    pallas_call x1, Pallas kernels, mix(): pl.pallas_call(functools.partial(mix_kernel, order), name='mix', compiler...  0.79 us
  transfers between devices with their start and end apart: 14, of which 10 were waited for; matrix products, arithmetic and copies ran while one was open for 1% of the time, Pallas kernels for 3%

profile of v6, /device:TPU:0, one launch (start us, length us, event | category | flops | bytes accessed | tf_op | source)
XLA Modules:
  0.0 33.0 jit_solution(4162343840485036754)
XLA Ops:
  0.0 3.1 %collective-permute-start = (bf16[4,2048]{1,0:T(4,128)(2,1)}, bf16[4,2048]{1,0:T(4,128)(2,1)S(1)}, u32[]{:S(2)}, u32[]{:S(2)}) collective-permute-start(bf16[4,2048]{1,0:T(4,128)(2,1)} %src.1), channel_id=1, source_target_pairs={{1,0},{0,1},{3,2},{2,3},{5,4},{4,5},{7,6},{6,7},{9,8},{8,9},{11,10... | collective-permute-start | bytes 49160 | tf_op jit(solution)/shard_map/ppermute | solution.py:30
  3.1 0.9 %rows.1.upper = bf16[4,2048]{1,0:T(4,128)(2,1)S(1)} custom-call(bf16[4,2048]{1,0:T(4,128)(2,1)} %src.1), custom_call_target="tpu_custom_call" | custom-call | bytes 32768 | tf_op jit(solution)/shard_map/rows/pallas_call | solution.py:60
  4.0 1.0 %collective-permute-done.lower = bf16[4,2048]{1,0:T(4,128)(2,1)S(1)} collective-permute-done((bf16[4,2048]{1,0:T(4,128)(2,1)}, bf16[4,2048]{1,0:T(4,128)(2,1)S(1)}, u32[]{:S(2)}, u32[]{:S(2)}) %collective-permute-start) | collective-permute-done | bytes 16416 | tf_op jit(solution)/shard_map/ppermute | solution.py:30
  5.0 3.1 %collective-permute-start.4 = (bf16[8,2048]{1,0:T(8,128)(2,1)S(1)}, bf16[8,2048]{1,0:T(8,128)(2,1)S(1)}, u32[]{:S(2)}, u32[]{:S(2)}) collective-permute-start(bf16[8,2048]{1,0:T(8,128)(2,1)S(1)} %stack.1.refs_0_), channel_id=1, source_target_pairs={{2,0},{3,1},{0,2},{1,3},{6,4},{7,5},{4,6},{5,7},{10,8},{11,9},{8,1... | collective-permute-start | bytes 98312 | tf_op jit(solution)/shard_map/ppermute | solution.py:30
  8.1 1.5 %collective-permute-start.2 = (bf16[8,2048]{1,0:T(8,128)(2,1)S(1)}, bf16[8,2048]{1,0:T(8,128)(2,1)S(1)}, u32[]{:S(2)}, u32[]{:S(2)}) collective-permute-start(bf16[8,2048]{1,0:T(8,128)(2,1)S(1)} %stack.1.refs_0_), channel_id=1, source_target_pairs={{8,0},{12,4},{0,8},{4,12},{9,1},{13,5},{1,9},{5,13},{10,2},{14,6},... | collective-permute-start | bytes 98312 | tf_op jit(solution)/shard_map/ppermute | solution.py:30
  9.6 0.4 %collective-permute-start.3 = (bf16[8,2048]{1,0:T(8,128)(2,1)S(1)}, bf16[8,2048]{1,0:T(8,128)(2,1)S(1)}, u32[]{:S(2)}, u32[]{:S(2)}) collective-permute-start(bf16[8,2048]{1,0:T(8,128)(2,1)S(1)} %stack.1.refs_0_), channel_id=1, source_target_pairs={{12,0},{8,4},{4,8},{0,12},{13,1},{9,5},{5,9},{1,13},{14,2},{10,6},... | collective-permute-start | bytes 98312 | tf_op jit(solution)/shard_map/ppermute | solution.py:30
  10.0 0.3 collective-permute-start.5
  10.3 1.6 %collective-permute-start.6 = (bf16[8,2048]{1,0:T(8,128)(2,1)S(1)}, bf16[8,2048]{1,0:T(8,128)(2,1)S(1)}, u32[]{:S(2)}, u32[]{:S(2)}) collective-permute-start(bf16[8,2048]{1,0:T(8,128)(2,1)S(1)} %collective-permute-done.4.refs_4_), channel_id=1, source_target_pairs={{8,0},{12,4},{0,8},{4,12},{9,1},{13,5},{1,9},{5,13},{10,2},{14,6},... | collective-permute-start | bytes 98312 | tf_op jit(solution)/shard_map/ppermute | solution.py:30
  11.8 0.1 collective-permute-start.7
  12.0 0.9 %collective-permute-done.3.refs_3_ = bf16[8,2048]{1,0:T(8,128)(2,1)S(1)} collective-permute-done((bf16[8,2048]{1,0:T(8,128)(2,1)S(1)}, bf16[8,2048]{1,0:T(8,128)(2,1)S(1)}, u32[]{:S(2)}, u32[]{:S(2)}) %collective-permute-start.3) | collective-permute-done | bytes 32800 | tf_op jit(solution)/shard_map/ppermute | solution.py:30
  13.0 1.2 %collective-permute-done.6.refs_6_ = bf16[8,2048]{1,0:T(8,128)(2,1)S(1)} collective-permute-done((bf16[8,2048]{1,0:T(8,128)(2,1)S(1)}, bf16[8,2048]{1,0:T(8,128)(2,1)S(1)}, u32[]{:S(2)}, u32[]{:S(2)}) %collective-permute-start.6) | collective-permute-done | bytes 32800 | tf_op jit(solution)/shard_map/ppermute | solution.py:30
  14.2 1.0 %collective-permute-done.7.refs_7_ = bf16[8,2048]{1,0:T(8,128)(2,1)S(1)} collective-permute-done((bf16[8,2048]{1,0:T(8,128)(2,1)S(1)}, bf16[8,2048]{1,0:T(8,128)(2,1)S(1)}, u32[]{:S(2)}, u32[]{:S(2)}) %collective-permute-start.7) | collective-permute-done | bytes 32800 | tf_op jit(solution)/shard_map/ppermute | solution.py:30
  15.2 3.5 %ffn.1 = (f32[16,2048]{1,0:T(8,128)S(1)}, bf16[16,2048]{1,0:T(8,128)(2,1)S(1)}, bf16[16,2048]{1,0:T(8,128)(2,1)S(1)}, bf16[16,2048]{1,0:T(8,128)(2,1)S(1)}) custom-call(bf16[8,2048]{1,0:T(8,128)(2,1)S(1)} %stack.1.refs_0_, bf16[8,2048]{1,0:T(8,128)(2,1)S(1)} %collective-permute-done.1.refs_1_, bf16[8,2048]{1,0:T(8,128)(2,1)S(1)} %collective-permute-done.2.refs_2_, ...), custom_call_target="tpu_custom_call" | custom-call | flops 1610612736 | bytes 25165824 | tf_op jit(solution)/shard_map/ffn/pallas_call | solution.py:113
  18.7 2.7 %collective-permute-start.10 = (bf16[16,2048]{1,0:T(8,128)(2,1)S(1)}, bf16[16,2048]{1,0:T(8,128)(2,1)S(1)}, u32[]{:S(2)}, u32[]{:S(2)}) collective-permute-start(bf16[16,2048]{1,0:T(8,128)(2,1)S(1)} %get-tuple-element.16), channel_id=1, source_target_pairs={{0,2},{1,3},{2,0},{3,1},{4,6},{5,7},{6,4},{7,5},{8,10},{9,11},{10,... | collective-permute-start | bytes 196616 | tf_op jit(solution)/shard_map/ppermute | solution.py:35
  21.4 1.3 %collective-permute-start.8 = (bf16[16,2048]{1,0:T(8,128)(2,1)S(1)}, bf16[16,2048]{1,0:T(8,128)(2,1)S(1)}, u32[]{:S(2)}, u32[]{:S(2)}) collective-permute-start(bf16[16,2048]{1,0:T(8,128)(2,1)S(1)} %get-tuple-element.14), channel_id=1, source_target_pairs={{0,3},{1,2},{2,1},{3,0},{4,7},{5,6},{6,5},{7,4},{8,11},{9,10},{10,... | collective-permute-start | bytes 196616 | tf_op jit(solution)/shard_map/ppermute | solution.py:35
  22.7 0.5 %collective-permute-start.9 = (bf16[16,2048]{1,0:T(8,128)(2,1)S(1)}, bf16[16,2048]{1,0:T(8,128)(2,1)S(1)}, u32[]{:S(2)}, u32[]{:S(2)}) collective-permute-start(bf16[16,2048]{1,0:T(8,128)(2,1)S(1)} %get-tuple-element.15), channel_id=1, source_target_pairs={{0,1},{1,0},{2,3},{3,2},{4,5},{5,4},{6,7},{7,6},{8,9},{9,8},{10,11... | collective-permute-start | bytes 196616 | tf_op jit(solution)/shard_map/ppermute | solution.py:35
  23.2 2.3 %collective-permute-done.10.refs_3_ = bf16[16,2048]{1,0:T(8,128)(2,1)S(1)} collective-permute-done((bf16[16,2048]{1,0:T(8,128)(2,1)S(1)}, bf16[16,2048]{1,0:T(8,128)(2,1)S(1)}, u32[]{:S(2)}, u32[]{:S(2)}) %collective-permute-start.10) | collective-permute-done | bytes 65568 | tf_op jit(solution)/shard_map/ppermute | solution.py:35
  25.5 2.3 %collective-permute-done.8.refs_1_ = bf16[16,2048]{1,0:T(8,128)(2,1)S(1)} collective-permute-done((bf16[16,2048]{1,0:T(8,128)(2,1)S(1)}, bf16[16,2048]{1,0:T(8,128)(2,1)S(1)}, u32[]{:S(2)}, u32[]{:S(2)}) %collective-permute-start.8) | collective-permute-done | bytes 65568 | tf_op jit(solution)/shard_map/ppermute | solution.py:35
  27.9 0.3 %collective-permute-done.9.refs_2_ = bf16[16,2048]{1,0:T(8,128)(2,1)S(1)} collective-permute-done((bf16[16,2048]{1,0:T(8,128)(2,1)S(1)}, bf16[16,2048]{1,0:T(8,128)(2,1)S(1)}, u32[]{:S(2)}, u32[]{:S(2)}) %collective-permute-start.9) | collective-permute-done | bytes 65568 | tf_op jit(solution)/shard_map/ppermute | solution.py:35
  28.3 0.9 %collective-permute-start.12 = (bf16[4,2048]{1,0:T(4,128)(2,1)S(1)}, bf16[4,2048]{1,0:T(4,128)(2,1)S(1)}, u32[]{:S(2)}, u32[]{:S(2)}) collective-permute-start(bf16[4,2048]{1,0:T(4,128)(2,1)S(1)} %get-tuple-element.19), channel_id=1, source_target_pairs={{0,8},{4,12},{8,0},{12,4},{1,9},{5,13},{9,1},{13,5},{2,10},{6,14},... | collective-permute-start | bytes 49160 | tf_op jit(solution)/shard_map/ppermute | solution.py:35
  29.2 1.0 %collective-permute-start.13 = (bf16[4,2048]{1,0:T(4,128)(2,1)S(1)}, bf16[4,2048]{1,0:T(4,128)(2,1)S(1)}, u32[]{:S(2)}, u32[]{:S(2)}) collective-permute-start(bf16[4,2048]{1,0:T(4,128)(2,1)S(1)} %get-tuple-element.20), channel_id=1, source_target_pairs={{0,4},{4,0},{8,12},{12,8},{1,5},{5,1},{9,13},{13,9},{2,6},{6,2},{1... | collective-permute-start | bytes 49160 | tf_op jit(solution)/shard_map/ppermute | solution.py:35
  30.3 1.1 %collective-permute-done.11.refs_1_ = bf16[4,2048]{1,0:T(4,128)(2,1)S(1)} collective-permute-done((bf16[4,2048]{1,0:T(4,128)(2,1)S(1)}, bf16[4,2048]{1,0:T(4,128)(2,1)S(1)}, u32[]{:S(2)}, u32[]{:S(2)}) %collective-permute-start.11) | collective-permute-done | bytes 16416 | tf_op jit(solution)/shard_map/ppermute | solution.py:35
  31.5 0.7 %collective-permute-done.12.refs_2_ = bf16[4,2048]{1,0:T(4,128)(2,1)S(1)} collective-permute-done((bf16[4,2048]{1,0:T(4,128)(2,1)S(1)}, bf16[4,2048]{1,0:T(4,128)(2,1)S(1)}, u32[]{:S(2)}, u32[]{:S(2)}) %collective-permute-start.12) | collective-permute-done | bytes 16416 | tf_op jit(solution)/shard_map/ppermute | solution.py:35
  32.2 0.8 %mix.1 = bf16[4,2048]{1,0:T(4,128)(2,1)} custom-call(s32[4,2]{1,0:T(4,128)S(1)} %copy.7.ids_ref, s32[4,2]{1,0:T(4,128)S(1)} %copy.8.fixed_ref, bf16[4,2048]{1,0:T(4,128)(2,1)S(1)} %get-tuple-element.17.refs_0_, bf16[4,2048]{1,0:T(4,128)(2,1)S(1)} %collective-permute-done.11.refs_1_, bf16[4,2048]{1,0:T(4,128)(2,1)S(1)} %collective-permute-done.12.refs_2_, ...), custom_call_target="tpu_custom_call" | custom-call | tf_op jit(solution)/shard_map/mix/pallas_call | solution.py:165
  (30 shorter events, 0.5 us)
Async XLA Ops:
  0.0 5.0 %collective-permute-start = (bf16[4,2048]{1,0:T(4,128)(2,1)}, bf16[4,2048]{1,0:T(4,128)(2,1)S(1)}, u32[]{:S(2)}, u32[]{:S(2)}) collective-permute-start(bf16[4,2048]{1,0:T(4,128)(2,1)} %src.1), channel_id=1, source_target_pairs={{1,0},{0,1},{3,2},{2,3},{5,4},{4,5},{7,6},{6,7},{9,8},{8,9},{11,10... | collective-permute-start | bytes 49160 | tf_op jit(solution)/shard_map/ppermute | solution.py:30
  3.1 12.1 %slice-start = ((s8[8388608]{0:T(1024)(128)(4,1)}), s8[4194304]{0:T(1024)(128)(4,1)S(1)}, s32[]{:S(2)}) async-start(s8[8388608]{0:T(1024)(128)(4,1)} %bitcast), calls=%async_computation | async-start | bytes 8388608
  3.1 12.1 %slice-start.2 = ((s8[8388608]{0:T(1024)(128)(4,1)}), s8[4194304]{0:T(1024)(128)(4,1)S(1)}, s32[]{:S(2)}) async-start(s8[8388608]{0:T(1024)(128)(4,1)} %bitcast.2), calls=%async_computation.2 | async-start | bytes 8388608
  3.1 12.1 %slice-start.4 = ((s8[8388608]{0:T(1024)(128)(4,1)}), s8[4194304]{0:T(1024)(128)(4,1)S(1)}, s32[]{:S(2)}) async-start(s8[8388608]{0:T(1024)(128)(4,1)} %bitcast.4), calls=%async_computation.4 | async-start | bytes 8388608
  3.9 11.3 %slice-start.1 = ((s8[8388608]{0:T(1024)(128)(4,1)}), s8[4194304]{0:T(1024)(128)(4,1)S(1)}, s32[]{:S(2)}) async-start(s8[8388608]{0:T(1024)(128)(4,1)} %bitcast), calls=%async_computation.1 | async-start | bytes 8388608
  4.0 11.3 %slice-start.3 = ((s8[8388608]{0:T(1024)(128)(4,1)}), s8[4194304]{0:T(1024)(128)(4,1)S(1)}, s32[]{:S(2)}) async-start(s8[8388608]{0:T(1024)(128)(4,1)} %bitcast.2), calls=%async_computation.3 | async-start | bytes 8388608
  4.0 11.2 %slice-start.5 = ((s8[8388608]{0:T(1024)(128)(4,1)}), s8[4194304]{0:T(1024)(128)(4,1)S(1)}, s32[]{:S(2)}) async-start(s8[8388608]{0:T(1024)(128)(4,1)} %bitcast.4), calls=%async_computation.5 | async-start | bytes 8388608
  5.0 25.2 %copy-start = (s32[4,2]{0,1:T(2,128)S(1)}, s32[4,2]{0,1:T(2,128)}, u32[]{:S(2)}) copy-start(s32[4,2]{0,1:T(2,128)} %param.8) | copy-start | bytes 100
  5.0 25.2 %copy-start.1 = (s32[4,2]{0,1:T(2,128)S(1)}, s32[4,2]{0,1:T(2,128)}, u32[]{:S(2)}) copy-start(s32[4,2]{0,1:T(2,128)} %param.9) | copy-start | bytes 100
  5.0 5.0 %collective-permute-start.4 = (bf16[8,2048]{1,0:T(8,128)(2,1)S(1)}, bf16[8,2048]{1,0:T(8,128)(2,1)S(1)}, u32[]{:S(2)}, u32[]{:S(2)}) collective-permute-start(bf16[8,2048]{1,0:T(8,128)(2,1)S(1)} %stack.1.refs_0_), channel_id=1, source_target_pairs={{2,0},{3,1},{0,2},{1,3},{6,4},{7,5},{4,6},{5,7},{10,8},{11,9},{8,1... | collective-permute-start | bytes 98312 | tf_op jit(solution)/shard_map/ppermute | solution.py:30
  8.1 3.7 %collective-permute-start.1 = (bf16[8,2048]{1,0:T(8,128)(2,1)S(1)}, bf16[8,2048]{1,0:T(8,128)(2,1)S(1)}, u32[]{:S(2)}, u32[]{:S(2)}) collective-permute-start(bf16[8,2048]{1,0:T(8,128)(2,1)S(1)} %stack.1.refs_0_), channel_id=1, source_target_pairs={{4,0},{0,4},{12,8},{8,12},{5,1},{1,5},{13,9},{9,13},{6,2},{2,6},{1... | collective-permute-start | bytes 98312 | tf_op jit(solution)/shard_map/ppermute | solution.py:30
  8.1 3.9 %collective-permute-start.2 = (bf16[8,2048]{1,0:T(8,128)(2,1)S(1)}, bf16[8,2048]{1,0:T(8,128)(2,1)S(1)}, u32[]{:S(2)}, u32[]{:S(2)}) collective-permute-start(bf16[8,2048]{1,0:T(8,128)(2,1)S(1)} %stack.1.refs_0_), channel_id=1, source_target_pairs={{8,0},{12,4},{0,8},{4,12},{9,1},{13,5},{1,9},{5,13},{10,2},{14,6},... | collective-permute-start | bytes 98312 | tf_op jit(solution)/shard_map/ppermute | solution.py:30
  9.6 3.3 %collective-permute-start.3 = (bf16[8,2048]{1,0:T(8,128)(2,1)S(1)}, bf16[8,2048]{1,0:T(8,128)(2,1)S(1)}, u32[]{:S(2)}, u32[]{:S(2)}) collective-permute-start(bf16[8,2048]{1,0:T(8,128)(2,1)S(1)} %stack.1.refs_0_), channel_id=1, source_target_pairs={{12,0},{8,4},{4,8},{0,12},{13,1},{9,5},{5,9},{1,13},{14,2},{10,6},... | collective-permute-start | bytes 98312 | tf_op jit(solution)/shard_map/ppermute | solution.py:30
  10.0 2.9 %collective-permute-start.5 = (bf16[8,2048]{1,0:T(8,128)(2,1)S(1)}, bf16[8,2048]{1,0:T(8,128)(2,1)S(1)}, u32[]{:S(2)}, u32[]{:S(2)}) collective-permute-start(bf16[8,2048]{1,0:T(8,128)(2,1)S(1)} %collective-permute-done.4.refs_4_), channel_id=1, source_target_pairs={{4,0},{0,4},{12,8},{8,12},{5,1},{1,5},{13,9},{9,13},{6,2},{2,6},{1... | collective-permute-start | bytes 98312 | tf_op jit(solution)/shard_map/ppermute | solution.py:30
  10.3 3.9 %collective-permute-start.6 = (bf16[8,2048]{1,0:T(8,128)(2,1)S(1)}, bf16[8,2048]{1,0:T(8,128)(2,1)S(1)}, u32[]{:S(2)}, u32[]{:S(2)}) collective-permute-start(bf16[8,2048]{1,0:T(8,128)(2,1)S(1)} %collective-permute-done.4.refs_4_), channel_id=1, source_target_pairs={{8,0},{12,4},{0,8},{4,12},{9,1},{13,5},{1,9},{5,13},{10,2},{14,6},... | collective-permute-start | bytes 98312 | tf_op jit(solution)/shard_map/ppermute | solution.py:30
  11.8 3.3 %collective-permute-start.7 = (bf16[8,2048]{1,0:T(8,128)(2,1)S(1)}, bf16[8,2048]{1,0:T(8,128)(2,1)S(1)}, u32[]{:S(2)}, u32[]{:S(2)}) collective-permute-start(bf16[8,2048]{1,0:T(8,128)(2,1)S(1)} %collective-permute-done.4.refs_4_), channel_id=1, source_target_pairs={{12,0},{8,4},{4,8},{0,12},{13,1},{9,5},{5,9},{1,13},{14,2},{10,6},... | collective-permute-start | bytes 98312 | tf_op jit(solution)/shard_map/ppermute | solution.py:30
  18.7 6.8 %collective-permute-start.10 = (bf16[16,2048]{1,0:T(8,128)(2,1)S(1)}, bf16[16,2048]{1,0:T(8,128)(2,1)S(1)}, u32[]{:S(2)}, u32[]{:S(2)}) collective-permute-start(bf16[16,2048]{1,0:T(8,128)(2,1)S(1)} %get-tuple-element.16), channel_id=1, source_target_pairs={{0,2},{1,3},{2,0},{3,1},{4,6},{5,7},{6,4},{7,5},{8,10},{9,11},{10,... | collective-permute-start | bytes 196616 | tf_op jit(solution)/shard_map/ppermute | solution.py:35
  21.4 6.5 %collective-permute-start.8 = (bf16[16,2048]{1,0:T(8,128)(2,1)S(1)}, bf16[16,2048]{1,0:T(8,128)(2,1)S(1)}, u32[]{:S(2)}, u32[]{:S(2)}) collective-permute-start(bf16[16,2048]{1,0:T(8,128)(2,1)S(1)} %get-tuple-element.14), channel_id=1, source_target_pairs={{0,3},{1,2},{2,1},{3,0},{4,7},{5,6},{6,5},{7,4},{8,11},{9,10},{10,... | collective-permute-start | bytes 196616 | tf_op jit(solution)/shard_map/ppermute | solution.py:35
  22.7 5.5 %collective-permute-start.9 = (bf16[16,2048]{1,0:T(8,128)(2,1)S(1)}, bf16[16,2048]{1,0:T(8,128)(2,1)S(1)}, u32[]{:S(2)}, u32[]{:S(2)}) collective-permute-start(bf16[16,2048]{1,0:T(8,128)(2,1)S(1)} %get-tuple-element.15), channel_id=1, source_target_pairs={{0,1},{1,0},{2,3},{3,2},{4,5},{5,4},{6,7},{7,6},{8,9},{9,8},{10,11... | collective-permute-start | bytes 196616 | tf_op jit(solution)/shard_map/ppermute | solution.py:35
  28.2 3.2 %collective-permute-start.11 = (bf16[4,2048]{1,0:T(4,128)(2,1)S(1)}, bf16[4,2048]{1,0:T(4,128)(2,1)S(1)}, u32[]{:S(2)}, u32[]{:S(2)}) collective-permute-start(bf16[4,2048]{1,0:T(4,128)(2,1)S(1)} %get-tuple-element.18), channel_id=1, source_target_pairs={{0,12},{4,8},{8,4},{12,0},{1,13},{5,9},{9,5},{13,1},{2,14},{6,10},... | collective-permute-start | bytes 49160 | tf_op jit(solution)/shard_map/ppermute | solution.py:35
  28.3 3.9 %collective-permute-start.12 = (bf16[4,2048]{1,0:T(4,128)(2,1)S(1)}, bf16[4,2048]{1,0:T(4,128)(2,1)S(1)}, u32[]{:S(2)}, u32[]{:S(2)}) collective-permute-start(bf16[4,2048]{1,0:T(4,128)(2,1)S(1)} %get-tuple-element.19), channel_id=1, source_target_pairs={{0,8},{4,12},{8,0},{12,4},{1,9},{5,13},{9,1},{13,5},{2,10},{6,14},... | collective-permute-start | bytes 49160 | tf_op jit(solution)/shard_map/ppermute | solution.py:35
  29.2 3.0 %collective-permute-start.13 = (bf16[4,2048]{1,0:T(4,128)(2,1)S(1)}, bf16[4,2048]{1,0:T(4,128)(2,1)S(1)}, u32[]{:S(2)}, u32[]{:S(2)}) collective-permute-start(bf16[4,2048]{1,0:T(4,128)(2,1)S(1)} %get-tuple-element.20), channel_id=1, source_target_pairs={{0,4},{4,0},{8,12},{12,8},{1,5},{5,1},{9,13},{13,9},{2,6},{6,2},{1... | collective-permute-start | bytes 49160 | tf_op jit(solution)/shard_map/ppermute | solution.py:35

commit v7 on v5

--- a/solution.py
+++ b/solution.py
@@ -146,30 +146,46 @@
     )(*[parts[i] for i in order])
 
 
-def mix_kernel(order, ids_ref, fixed_ref, *refs):
-    blocks, out, n_e = restored(refs[:-1], order), refs[-1], len(order)
+def shares_kernel(n_e, ids_ref, fixed_ref, out):
     me = lax.axis_index("expert")
     ids = ids_ref[...]
     fixed = fixed_ref[...].astype(jnp.float32)
     shares = fixed / jnp.sum(fixed, axis=1, keepdims=True)
+    for m in range(n_e):
+        share = jnp.sum(jnp.where(ids == source(me, m, n_e), shares, 0.0), axis=1, keepdims=True)
+        out[m] = jnp.broadcast_to(share, out.shape[1:])
+
+
+def shares_of(route_ids, gate_fixed, n_e):
+    return pl.pallas_call(
+        functools.partial(shares_kernel, n_e),
+        name="shares",
+        compiler_params=limit(1),
+        out_shape=jax.ShapeDtypeStruct((n_e, route_ids.shape[0], 128), jnp.float32),
+        in_specs=[VMEM] * 2,
+        out_specs=VMEM,
+    )(route_ids, gate_fixed)
+
+
+def mix_kernel(order, shares, *refs):
+    blocks, out = restored(refs[:-1], order), refs[-1]
     mixed = None
     for m, block in enumerate(blocks):
-        share = jnp.sum(jnp.where(ids == source(me, m, n_e), shares, 0.0), axis=1, keepdims=True)
-        part = share * block[...].astype(jnp.float32)
+        part = shares[m, :, :1] * block[...].astype(jnp.float32)
         mixed = part if m == 0 else mixed + part
     out[...] = mixed.astype(out.dtype)
 
 
-def mix(route_ids, gate_fixed, blocks):
+def mix(shares, blocks):
     order = half_first(len(blocks))
     return pl.pallas_call(
         functools.partial(mix_kernel, order),
         name="mix",
         compiler_params=limit(4),
         out_shape=jax.ShapeDtypeStruct(blocks[0].shape, jnp.bfloat16),
-        in_specs=[VMEM] * (2 + len(blocks)),
-        out_specs=VMEM,
-    )(route_ids, gate_fixed, *[blocks[i] for i in order])
+        in_specs=[VMEM] * (1 + len(blocks)),
+        out_specs=VMEM,
+    )(shares, *[blocks[i] for i in order])
 
 
 def on_device(tokens, route_ids, route_slots, gate_fixed, w_gate, w_up, w_down):
@@ -186,7 +202,7 @@
     parts = [parts[0]] + [deliver(parts[d], "blk", d) for d in range(1, n_b)]
     blocks = merge(parts, n_e)
     blocks = [blocks[0]] + [deliver(blocks[m], "expert", m) for m in range(1, n_e)]
-    return mix(route_ids, gate_fixed, blocks)
+    return mix(shares_of(route_ids, gate_fixed, n_e), blocks)
 
 
 def solution(mesh):

time: 33.3 us -> 33.2 us (level)
  no operation moved by 1% of the time
where the time goes in v7:
time: 33.2 us; the launch traced here: 33 us
  starting transfers between devices  16.6 us (50%)
  waiting for transfers between devices  10.7 us (32%)
  Pallas kernels  5.24 us (16%)
    ppermute x8, starting transfers between devices, fetch(): return lax.ppermute(x, axis, [(peer(i, d, n), i) for i in range(n)])  9.95 us
    ppermute x6, starting transfers between devices, deliver(): return lax.ppermute(x, axis, [(i, peer(i, d, n)) for i in range(n)])  6.67 us
    ppermute x6, waiting for transfers between devices, deliver(): return lax.ppermute(x, axis, [(i, peer(i, d, n)) for i in range(n)])  6.48 us
    ppermute x8, waiting for transfers between devices, fetch(): return lax.ppermute(x, axis, [(peer(i, d, n), i) for i in range(n)])  4.25 us
    pallas_call x1, Pallas kernels, ffn(): pl.pallas_call(functools.partial(ffn_kernel, order, n_e, n_b, count), nam...  3.47 us
    pallas_call x1, Pallas kernels, on_chip(): pl.pallas_call(rows_kernel, name='rows', compiler_params=limit(1), cost_e...  0.87 us
    pallas_call x1, Pallas kernels, mix(): pl.pallas_call(functools.partial(mix_kernel, order), name='mix', compiler...  0.69 us
  transfers between devices with their start and end apart: 14, of which 10 were waited for; matrix products, arithmetic and copies ran while one was open for 1% of the time, Pallas kernels for 3%

profile of v7, /device:TPU:0, one launch (start us, length us, event | category | flops | bytes accessed | tf_op | source)
XLA Modules:
  0.0 33.0 jit_solution(14472901740556902772)
XLA Ops:
  0.0 3.1 %collective-permute-start = (bf16[4,2048]{1,0:T(4,128)(2,1)}, bf16[4,2048]{1,0:T(4,128)(2,1)S(1)}, u32[]{:S(2)}, u32[]{:S(2)}) collective-permute-start(bf16[4,2048]{1,0:T(4,128)(2,1)} %src.1), channel_id=1, source_target_pairs={{1,0},{0,1},{3,2},{2,3},{5,4},{4,5},{7,6},{6,7},{9,8},{8,9},{11,10... | collective-permute-start | bytes 49160 | tf_op jit(solution)/shard_map/ppermute | solution.py:30
  3.1 0.9 %rows.1.upper = bf16[4,2048]{1,0:T(4,128)(2,1)S(1)} custom-call(bf16[4,2048]{1,0:T(4,128)(2,1)} %src.1), custom_call_target="tpu_custom_call" | custom-call | bytes 32768 | tf_op jit(solution)/shard_map/rows/pallas_call | solution.py:60
  4.0 1.0 %collective-permute-done.lower = bf16[4,2048]{1,0:T(4,128)(2,1)S(1)} collective-permute-done((bf16[4,2048]{1,0:T(4,128)(2,1)}, bf16[4,2048]{1,0:T(4,128)(2,1)S(1)}, u32[]{:S(2)}, u32[]{:S(2)}) %collective-permute-start) | collective-permute-done | bytes 16416 | tf_op jit(solution)/shard_map/ppermute | solution.py:30
  5.0 3.1 %collective-permute-start.4 = (bf16[8,2048]{1,0:T(8,128)(2,1)S(1)}, bf16[8,2048]{1,0:T(8,128)(2,1)S(1)}, u32[]{:S(2)}, u32[]{:S(2)}) collective-permute-start(bf16[8,2048]{1,0:T(8,128)(2,1)S(1)} %stack.1.refs_0_), channel_id=1, source_target_pairs={{2,0},{3,1},{0,2},{1,3},{6,4},{7,5},{4,6},{5,7},{10,8},{11,9},{8,1... | collective-permute-start | bytes 98312 | tf_op jit(solution)/shard_map/ppermute | solution.py:30
  8.1 1.5 %collective-permute-start.2 = (bf16[8,2048]{1,0:T(8,128)(2,1)S(1)}, bf16[8,2048]{1,0:T(8,128)(2,1)S(1)}, u32[]{:S(2)}, u32[]{:S(2)}) collective-permute-start(bf16[8,2048]{1,0:T(8,128)(2,1)S(1)} %stack.1.refs_0_), channel_id=1, source_target_pairs={{8,0},{12,4},{0,8},{4,12},{9,1},{13,5},{1,9},{5,13},{10,2},{14,6},... | collective-permute-start | bytes 98312 | tf_op jit(solution)/shard_map/ppermute | solution.py:30
  9.6 0.4 %collective-permute-start.3 = (bf16[8,2048]{1,0:T(8,128)(2,1)S(1)}, bf16[8,2048]{1,0:T(8,128)(2,1)S(1)}, u32[]{:S(2)}, u32[]{:S(2)}) collective-permute-start(bf16[8,2048]{1,0:T(8,128)(2,1)S(1)} %stack.1.refs_0_), channel_id=1, source_target_pairs={{12,0},{8,4},{4,8},{0,12},{13,1},{9,5},{5,9},{1,13},{14,2},{10,6},... | collective-permute-start | bytes 98312 | tf_op jit(solution)/shard_map/ppermute | solution.py:30
  10.0 0.3 collective-permute-start.5
  10.3 1.6 %collective-permute-start.6 = (bf16[8,2048]{1,0:T(8,128)(2,1)S(1)}, bf16[8,2048]{1,0:T(8,128)(2,1)S(1)}, u32[]{:S(2)}, u32[]{:S(2)}) collective-permute-start(bf16[8,2048]{1,0:T(8,128)(2,1)S(1)} %collective-permute-done.4.refs_4_), channel_id=1, source_target_pairs={{8,0},{12,4},{0,8},{4,12},{9,1},{13,5},{1,9},{5,13},{10,2},{14,6},... | collective-permute-start | bytes 98312 | tf_op jit(solution)/shard_map/ppermute | solution.py:30
  12.0 0.9 %collective-permute-done.3.refs_3_ = bf16[8,2048]{1,0:T(8,128)(2,1)S(1)} collective-permute-done((bf16[8,2048]{1,0:T(8,128)(2,1)S(1)}, bf16[8,2048]{1,0:T(8,128)(2,1)S(1)}, u32[]{:S(2)}, u32[]{:S(2)}) %collective-permute-start.3) | collective-permute-done | bytes 32800 | tf_op jit(solution)/shard_map/ppermute | solution.py:30
  13.0 1.2 %collective-permute-done.6.refs_6_ = bf16[8,2048]{1,0:T(8,128)(2,1)S(1)} collective-permute-done((bf16[8,2048]{1,0:T(8,128)(2,1)S(1)}, bf16[8,2048]{1,0:T(8,128)(2,1)S(1)}, u32[]{:S(2)}, u32[]{:S(2)}) %collective-permute-start.6) | collective-permute-done | bytes 32800 | tf_op jit(solution)/shard_map/ppermute | solution.py:30
  14.2 1.0 %collective-permute-done.7.refs_7_ = bf16[8,2048]{1,0:T(8,128)(2,1)S(1)} collective-permute-done((bf16[8,2048]{1,0:T(8,128)(2,1)S(1)}, bf16[8,2048]{1,0:T(8,128)(2,1)S(1)}, u32[]{:S(2)}, u32[]{:S(2)}) %collective-permute-start.7) | collective-permute-done | bytes 32800 | tf_op jit(solution)/shard_map/ppermute | solution.py:30
  15.2 3.5 %ffn.1 = (f32[16,2048]{1,0:T(8,128)S(1)}, bf16[16,2048]{1,0:T(8,128)(2,1)S(1)}, bf16[16,2048]{1,0:T(8,128)(2,1)S(1)}, bf16[16,2048]{1,0:T(8,128)(2,1)S(1)}) custom-call(bf16[8,2048]{1,0:T(8,128)(2,1)S(1)} %stack.1.refs_0_, bf16[8,2048]{1,0:T(8,128)(2,1)S(1)} %collective-permute-done.1.refs_1_, bf16[8,2048]{1,0:T(8,128)(2,1)S(1)} %collective-permute-done.2.refs_2_, ...), custom_call_target="tpu_custom_call" | custom-call | flops 1610612736 | bytes 25165824 | tf_op jit(solution)/shard_map/ffn/pallas_call | solution.py:113
  18.7 2.7 %collective-permute-start.10 = (bf16[16,2048]{1,0:T(8,128)(2,1)S(1)}, bf16[16,2048]{1,0:T(8,128)(2,1)S(1)}, u32[]{:S(2)}, u32[]{:S(2)}) collective-permute-start(bf16[16,2048]{1,0:T(8,128)(2,1)S(1)} %get-tuple-element.16), channel_id=1, source_target_pairs={{0,2},{1,3},{2,0},{3,1},{4,6},{5,7},{6,4},{7,5},{8,10},{9,11},{10,... | collective-permute-start | bytes 196616 | tf_op jit(solution)/shard_map/ppermute | solution.py:35
  21.4 1.3 %collective-permute-start.8 = (bf16[16,2048]{1,0:T(8,128)(2,1)S(1)}, bf16[16,2048]{1,0:T(8,128)(2,1)S(1)}, u32[]{:S(2)}, u32[]{:S(2)}) collective-permute-start(bf16[16,2048]{1,0:T(8,128)(2,1)S(1)} %get-tuple-element.14), channel_id=1, source_target_pairs={{0,3},{1,2},{2,1},{3,0},{4,7},{5,6},{6,5},{7,4},{8,11},{9,10},{10,... | collective-permute-start | bytes 196616 | tf_op jit(solution)/shard_map/ppermute | solution.py:35
  22.7 0.5 %collective-permute-start.9 = (bf16[16,2048]{1,0:T(8,128)(2,1)S(1)}, bf16[16,2048]{1,0:T(8,128)(2,1)S(1)}, u32[]{:S(2)}, u32[]{:S(2)}) collective-permute-start(bf16[16,2048]{1,0:T(8,128)(2,1)S(1)} %get-tuple-element.15), channel_id=1, source_target_pairs={{0,1},{1,0},{2,3},{3,2},{4,5},{5,4},{6,7},{7,6},{8,9},{9,8},{10,11... | collective-permute-start | bytes 196616 | tf_op jit(solution)/shard_map/ppermute | solution.py:35
  23.2 2.3 %collective-permute-done.10.refs_3_ = bf16[16,2048]{1,0:T(8,128)(2,1)S(1)} collective-permute-done((bf16[16,2048]{1,0:T(8,128)(2,1)S(1)}, bf16[16,2048]{1,0:T(8,128)(2,1)S(1)}, u32[]{:S(2)}, u32[]{:S(2)}) %collective-permute-start.10) | collective-permute-done | bytes 65568 | tf_op jit(solution)/shard_map/ppermute | solution.py:35
  25.5 2.3 %collective-permute-done.8.refs_1_ = bf16[16,2048]{1,0:T(8,128)(2,1)S(1)} collective-permute-done((bf16[16,2048]{1,0:T(8,128)(2,1)S(1)}, bf16[16,2048]{1,0:T(8,128)(2,1)S(1)}, u32[]{:S(2)}, u32[]{:S(2)}) %collective-permute-start.8) | collective-permute-done | bytes 65568 | tf_op jit(solution)/shard_map/ppermute | solution.py:35
  27.9 0.3 %collective-permute-done.9.refs_2_ = bf16[16,2048]{1,0:T(8,128)(2,1)S(1)} collective-permute-done((bf16[16,2048]{1,0:T(8,128)(2,1)S(1)}, bf16[16,2048]{1,0:T(8,128)(2,1)S(1)}, u32[]{:S(2)}, u32[]{:S(2)}) %collective-permute-start.9) | collective-permute-done | bytes 65568 | tf_op jit(solution)/shard_map/ppermute | solution.py:35
  28.2 0.9 %collective-permute-start.11 = (bf16[4,2048]{1,0:T(4,128)(2,1)S(1)}, bf16[4,2048]{1,0:T(4,128)(2,1)S(1)}, u32[]{:S(2)}, u32[]{:S(2)}) collective-permute-start(bf16[4,2048]{1,0:T(4,128)(2,1)S(1)} %get-tuple-element.18), channel_id=1, source_target_pairs={{0,8},{4,12},{8,0},{12,4},{1,9},{5,13},{9,1},{13,5},{2,10},{6,14},... | collective-permute-start | bytes 49160 | tf_op jit(solution)/shard_map/ppermute | solution.py:35
  29.1 1.3 %collective-permute-start.13 = (bf16[4,2048]{1,0:T(4,128)(2,1)S(1)}, bf16[4,2048]{1,0:T(4,128)(2,1)S(1)}, u32[]{:S(2)}, u32[]{:S(2)}) collective-permute-start(bf16[4,2048]{1,0:T(4,128)(2,1)S(1)} %get-tuple-element.20), channel_id=1, source_target_pairs={{0,12},{4,8},{8,4},{12,0},{1,13},{5,9},{9,5},{13,1},{2,14},{6,10},... | collective-permute-start | bytes 49160 | tf_op jit(solution)/shard_map/ppermute | solution.py:35
  30.6 0.2 shares.1
  30.8 1.2 %collective-permute-done.11.refs_1_ = bf16[4,2048]{1,0:T(4,128)(2,1)S(1)} collective-permute-done((bf16[4,2048]{1,0:T(4,128)(2,1)S(1)}, bf16[4,2048]{1,0:T(4,128)(2,1)S(1)}, u32[]{:S(2)}, u32[]{:S(2)}) %collective-permute-start.11) | collective-permute-done | bytes 16416 | tf_op jit(solution)/shard_map/ppermute | solution.py:35
  32.0 0.2 collective-permute-done.13.refs_3_
  32.3 0.7 %mix.1 = bf16[4,2048]{1,0:T(4,128)(2,1)} custom-call(f32[4,4,128]{2,1,0:T(4,128)S(1)} %shares.1, bf16[4,2048]{1,0:T(4,128)(2,1)S(1)} %get-tuple-element.17.refs_0_, bf16[4,2048]{1,0:T(4,128)(2,1)S(1)} %collective-permute-done.11.refs_1_, bf16[4,2048]{1,0:T(4,128)(2,1)S(1)} %collective-permute-done.12.refs_2_, bf16[4,2048]{1,0:T(4,128)(2,1)S(1)} %collective-permute-done.13.refs_3_), custom_call_target="tpu_custom_call" | custom-call | tf_op jit(solution)/shard_map/mix/pallas_call | solution.py:181
  (31 shorter events, 0.5 us)
Async XLA Ops:
  0.0 5.0 %collective-permute-start = (bf16[4,2048]{1,0:T(4,128)(2,1)}, bf16[4,2048]{1,0:T(4,128)(2,1)S(1)}, u32[]{:S(2)}, u32[]{:S(2)}) collective-permute-start(bf16[4,2048]{1,0:T(4,128)(2,1)} %src.1), channel_id=1, source_target_pairs={{1,0},{0,1},{3,2},{2,3},{5,4},{4,5},{7,6},{6,7},{9,8},{8,9},{11,10... | collective-permute-start | bytes 49160 | tf_op jit(solution)/shard_map/ppermute | solution.py:30
  3.1 12.1 %slice-start = ((s8[8388608]{0:T(1024)(128)(4,1)}), s8[4194304]{0:T(1024)(128)(4,1)S(1)}, s32[]{:S(2)}) async-start(s8[8388608]{0:T(1024)(128)(4,1)} %bitcast), calls=%async_computation | async-start | bytes 8388608
  3.1 12.1 %slice-start.2 = ((s8[8388608]{0:T(1024)(128)(4,1)}), s8[4194304]{0:T(1024)(128)(4,1)S(1)}, s32[]{:S(2)}) async-start(s8[8388608]{0:T(1024)(128)(4,1)} %bitcast.2), calls=%async_computation.2 | async-start | bytes 8388608
  3.1 12.1 %slice-start.4 = ((s8[8388608]{0:T(1024)(128)(4,1)}), s8[4194304]{0:T(1024)(128)(4,1)S(1)}, s32[]{:S(2)}) async-start(s8[8388608]{0:T(1024)(128)(4,1)} %bitcast.4), calls=%async_computation.4 | async-start | bytes 8388608
  3.9 11.3 %slice-start.1 = ((s8[8388608]{0:T(1024)(128)(4,1)}), s8[4194304]{0:T(1024)(128)(4,1)S(1)}, s32[]{:S(2)}) async-start(s8[8388608]{0:T(1024)(128)(4,1)} %bitcast), calls=%async_computation.1 | async-start | bytes 8388608
  4.0 11.3 %slice-start.3 = ((s8[8388608]{0:T(1024)(128)(4,1)}), s8[4194304]{0:T(1024)(128)(4,1)S(1)}, s32[]{:S(2)}) async-start(s8[8388608]{0:T(1024)(128)(4,1)} %bitcast.2), calls=%async_computation.3 | async-start | bytes 8388608
  4.0 11.2 %slice-start.5 = ((s8[8388608]{0:T(1024)(128)(4,1)}), s8[4194304]{0:T(1024)(128)(4,1)S(1)}, s32[]{:S(2)}) async-start(s8[8388608]{0:T(1024)(128)(4,1)} %bitcast.4), calls=%async_computation.5 | async-start | bytes 8388608
  5.0 25.4 %copy-start = (s32[4,2]{0,1:T(2,128)S(1)}, s32[4,2]{0,1:T(2,128)}, u32[]{:S(2)}) copy-start(s32[4,2]{0,1:T(2,128)} %param.8) | copy-start | bytes 100
  5.0 25.5 %copy-start.1 = (s32[4,2]{0,1:T(2,128)S(1)}, s32[4,2]{0,1:T(2,128)}, u32[]{:S(2)}) copy-start(s32[4,2]{0,1:T(2,128)} %param.9) | copy-start | bytes 100
  5.0 5.0 %collective-permute-start.4 = (bf16[8,2048]{1,0:T(8,128)(2,1)S(1)}, bf16[8,2048]{1,0:T(8,128)(2,1)S(1)}, u32[]{:S(2)}, u32[]{:S(2)}) collective-permute-start(bf16[8,2048]{1,0:T(8,128)(2,1)S(1)} %stack.1.refs_0_), channel_id=1, source_target_pairs={{2,0},{3,1},{0,2},{1,3},{6,4},{7,5},{4,6},{5,7},{10,8},{11,9},{8,1... | collective-permute-start | bytes 98312 | tf_op jit(solution)/shard_map/ppermute | solution.py:30
  8.1 3.7 %collective-permute-start.1 = (bf16[8,2048]{1,0:T(8,128)(2,1)S(1)}, bf16[8,2048]{1,0:T(8,128)(2,1)S(1)}, u32[]{:S(2)}, u32[]{:S(2)}) collective-permute-start(bf16[8,2048]{1,0:T(8,128)(2,1)S(1)} %stack.1.refs_0_), channel_id=1, source_target_pairs={{4,0},{0,4},{12,8},{8,12},{5,1},{1,5},{13,9},{9,13},{6,2},{2,6},{1... | collective-permute-start | bytes 98312 | tf_op jit(solution)/shard_map/ppermute | solution.py:30
  8.1 3.9 %collective-permute-start.2 = (bf16[8,2048]{1,0:T(8,128)(2,1)S(1)}, bf16[8,2048]{1,0:T(8,128)(2,1)S(1)}, u32[]{:S(2)}, u32[]{:S(2)}) collective-permute-start(bf16[8,2048]{1,0:T(8,128)(2,1)S(1)} %stack.1.refs_0_), channel_id=1, source_target_pairs={{8,0},{12,4},{0,8},{4,12},{9,1},{13,5},{1,9},{5,13},{10,2},{14,6},... | collective-permute-start | bytes 98312 | tf_op jit(solution)/shard_map/ppermute | solution.py:30
  9.6 3.3 %collective-permute-start.3 = (bf16[8,2048]{1,0:T(8,128)(2,1)S(1)}, bf16[8,2048]{1,0:T(8,128)(2,1)S(1)}, u32[]{:S(2)}, u32[]{:S(2)}) collective-permute-start(bf16[8,2048]{1,0:T(8,128)(2,1)S(1)} %stack.1.refs_0_), channel_id=1, source_target_pairs={{12,0},{8,4},{4,8},{0,12},{13,1},{9,5},{5,9},{1,13},{14,2},{10,6},... | collective-permute-start | bytes 98312 | tf_op jit(solution)/shard_map/ppermute | solution.py:30
  10.0 2.9 %collective-permute-start.5 = (bf16[8,2048]{1,0:T(8,128)(2,1)S(1)}, bf16[8,2048]{1,0:T(8,128)(2,1)S(1)}, u32[]{:S(2)}, u32[]{:S(2)}) collective-permute-start(bf16[8,2048]{1,0:T(8,128)(2,1)S(1)} %collective-permute-done.4.refs_4_), channel_id=1, source_target_pairs={{4,0},{0,4},{12,8},{8,12},{5,1},{1,5},{13,9},{9,13},{6,2},{2,6},{1... | collective-permute-start | bytes 98312 | tf_op jit(solution)/shard_map/ppermute | solution.py:30
  10.3 3.9 %collective-permute-start.6 = (bf16[8,2048]{1,0:T(8,128)(2,1)S(1)}, bf16[8,2048]{1,0:T(8,128)(2,1)S(1)}, u32[]{:S(2)}, u32[]{:S(2)}) collective-permute-start(bf16[8,2048]{1,0:T(8,128)(2,1)S(1)} %collective-permute-done.4.refs_4_), channel_id=1, source_target_pairs={{8,0},{12,4},{0,8},{4,12},{9,1},{13,5},{1,9},{5,13},{10,2},{14,6},... | collective-permute-start | bytes 98312 | tf_op jit(solution)/shard_map/ppermute | solution.py:30
  11.8 3.3 %collective-permute-start.7 = (bf16[8,2048]{1,0:T(8,128)(2,1)S(1)}, bf16[8,2048]{1,0:T(8,128)(2,1)S(1)}, u32[]{:S(2)}, u32[]{:S(2)}) collective-permute-start(bf16[8,2048]{1,0:T(8,128)(2,1)S(1)} %collective-permute-done.4.refs_4_), channel_id=1, source_target_pairs={{12,0},{8,4},{4,8},{0,12},{13,1},{9,5},{5,9},{1,13},{14,2},{10,6},... | collective-permute-start | bytes 98312 | tf_op jit(solution)/shard_map/ppermute | solution.py:30
  18.7 6.8 %collective-permute-start.10 = (bf16[16,2048]{1,0:T(8,128)(2,1)S(1)}, bf16[16,2048]{1,0:T(8,128)(2,1)S(1)}, u32[]{:S(2)}, u32[]{:S(2)}) collective-permute-start(bf16[16,2048]{1,0:T(8,128)(2,1)S(1)} %get-tuple-element.16), channel_id=1, source_target_pairs={{0,2},{1,3},{2,0},{3,1},{4,6},{5,7},{6,4},{7,5},{8,10},{9,11},{10,... | collective-permute-start | bytes 196616 | tf_op jit(solution)/shard_map/ppermute | solution.py:35
  21.4 6.5 %collective-permute-start.8 = (bf16[16,2048]{1,0:T(8,128)(2,1)S(1)}, bf16[16,2048]{1,0:T(8,128)(2,1)S(1)}, u32[]{:S(2)}, u32[]{:S(2)}) collective-permute-start(bf16[16,2048]{1,0:T(8,128)(2,1)S(1)} %get-tuple-element.14), channel_id=1, source_target_pairs={{0,3},{1,2},{2,1},{3,0},{4,7},{5,6},{6,5},{7,4},{8,11},{9,10},{10,... | collective-permute-start | bytes 196616 | tf_op jit(solution)/shard_map/ppermute | solution.py:35
  22.7 5.5 %collective-permute-start.9 = (bf16[16,2048]{1,0:T(8,128)(2,1)S(1)}, bf16[16,2048]{1,0:T(8,128)(2,1)S(1)}, u32[]{:S(2)}, u32[]{:S(2)}) collective-permute-start(bf16[16,2048]{1,0:T(8,128)(2,1)S(1)} %get-tuple-element.15), channel_id=1, source_target_pairs={{0,1},{1,0},{2,3},{3,2},{4,5},{5,4},{6,7},{7,6},{8,9},{9,8},{10,11... | collective-permute-start | bytes 196616 | tf_op jit(solution)/shard_map/ppermute | solution.py:35
  28.2 3.8 %collective-permute-start.11 = (bf16[4,2048]{1,0:T(4,128)(2,1)S(1)}, bf16[4,2048]{1,0:T(4,128)(2,1)S(1)}, u32[]{:S(2)}, u32[]{:S(2)}) collective-permute-start(bf16[4,2048]{1,0:T(4,128)(2,1)S(1)} %get-tuple-element.18), channel_id=1, source_target_pairs={{0,8},{4,12},{8,0},{12,4},{1,9},{5,13},{9,1},{13,5},{2,10},{6,14},... | collective-permute-start | bytes 49160 | tf_op jit(solution)/shard_map/ppermute | solution.py:35
  29.1 2.9 %collective-permute-start.12 = (bf16[4,2048]{1,0:T(4,128)(2,1)S(1)}, bf16[4,2048]{1,0:T(4,128)(2,1)S(1)}, u32[]{:S(2)}, u32[]{:S(2)}) collective-permute-start(bf16[4,2048]{1,0:T(4,128)(2,1)S(1)} %get-tuple-element.19), channel_id=1, source_target_pairs={{0,4},{4,0},{8,12},{12,8},{1,5},{5,1},{9,13},{13,9},{2,6},{6,2},{1... | collective-permute-start | bytes 49160 | tf_op jit(solution)/shard_map/ppermute | solution.py:35
  29.1 3.2 %collective-permute-start.13 = (bf16[4,2048]{1,0:T(4,128)(2,1)S(1)}, bf16[4,2048]{1,0:T(4,128)(2,1)S(1)}, u32[]{:S(2)}, u32[]{:S(2)}) collective-permute-start(bf16[4,2048]{1,0:T(4,128)(2,1)S(1)} %get-tuple-element.20), channel_id=1, source_target_pairs={{0,12},{4,8},{8,4},{12,0},{1,13},{5,9},{9,5},{13,1},{2,14},{6,10},... | collective-permute-start | bytes 49160 | tf_op jit(solution)/shard_map/ppermute | solution.py:35
